TPU v7x, 32 devices: a whole 2x2x4 slice. The times are simulated.
32 devices in a mesh: groups: 2 (over y), node: 4 (over z), rep: 4 (over x, core).
Axes of the slice: x: 2, y: 2, z: 4, core: 2. Of those that a mesh axis runs over, the one named last changes fastest.
Arguments:
- node_states: bfloat16 [8, 512, 512], P(('groups', 'rep'), 'node'), parts along dimension 0, may hold values from -6 to 6
- cotangent: bfloat16 [8, 512, 512], P(('groups', 'rep'), 'node'), parts along dimension 0, may hold values from -1.1953125 to 1.1953125
- reach_blocks: int32 [8, 8, 8], P(('groups', 'rep'), 'node'), parts along dimension 0, may hold values from 0 to 7, as said below
- reach_count: int32 [8, 8], P(('groups', 'rep'), 'node'), parts along dimension 0, may hold values from 1 to 8, as said below
- level_start: int32 [8, 17], P(('groups', 'rep')), parts along dimension 0, may hold values from 0 to 512, as said below
- query_weight: bfloat16 [512, 256], replicated, may hold values from -0.25 to 0.25
- key_weight: bfloat16 [512, 256], replicated, may hold values from -0.25 to 0.25
- value_weight: bfloat16 [512, 256], replicated, may hold values from -0.25 to 0.25
- out_weight: bfloat16 [256, 512], replicated, may hold values from -0.375 to 0.375
- bias_table: float32 [4, 32], replicated, may hold values from -4 to 412
Outputs:
- updated: bfloat16 [8, 512, 512], P(('groups', 'rep'), 'node'), parts along dimension 0
- node_state_gradient: bfloat16 [8, 512, 512], P(('groups', 'rep'), 'node'), parts along dimension 0
- grad_query: float32 [1024, 256], P('groups'), parts along dimension 0
- grad_key: float32 [1024, 256], P('groups'), parts along dimension 0
- grad_value: float32 [1024, 256], P('groups'), parts along dimension 0
- grad_out: float32 [512, 512], P('groups'), parts along dimension 0
There are 2 independent parts, one for each index of `groups`. A program takes and returns all parts, laid end to end along the dimension named above; an argument that names none is the same for every part. Nothing has to cross between parts.
Inputs may be any that keep to these rules, and one draw needn't show every extreme that they name: `reach_blocks`: in row b of a graph, entry 0 is b, entries 1 to min(b, 7) are distinct blocks below b, and any later entries are b. `reach_count`: row b holds at most b + 1; row 7 of every graph holds 8. `level_start`: strictly increasing; entry 0 is 0 and entry 16 is 512.
All inputs are finite; a program needn't handle non-finite values.
Results may differ from a plain program's by a relative error of at most 0.011.
Values may be sent and summed in bfloat16 or wider, within the bound.
No kernel may reach another device: no remote copies, remote signals or barrier semaphores. Data moves between devices by JAX's collectives and lax.ppermute only.
A program may use at most 64 MiB of HBM per device.

v0:
```python
import jax
import jax.numpy as jnp
from jax import lax
from jax.sharding import PartitionSpec as P

HEADS = 4
HEAD = 64
BLOCK = 64
DIST = 32


EPS = 1e-05
NEG = -1e30
HIGH = lax.Precision.HIGHEST
CONTRACT_ROWS = (((0,), (0,)), ((), ()))
CONTRACT_COLS = (((1,), (1,)), ((), ()))


def rows_product(left, right):
    return lax.dot_general(left, right, CONTRACT_ROWS, preferred_element_type=jnp.float32)


def cols_product(left, right):
    return lax.dot_general(left, right, CONTRACT_COLS, preferred_element_type=jnp.float32)


def expand(listed):
    return jnp.repeat(jnp.repeat(listed, BLOCK, axis=0), BLOCK, axis=1)


def level_tables(starts, total, bias_table):
    level_count = starts.shape[0] - 1
    places = jnp.arange(total, dtype=jnp.int32)
    inner = starts[1:level_count]
    levels = jnp.sum((places[:, None] >= inner[None, :]).astype(jnp.int32), axis=1)
    marks = jnp.arange(level_count, dtype=jnp.int32)
    onehot = (levels[:, None] == marks[None, :]).astype(jnp.float32)
    spread = jnp.clip(marks[:, None] - marks[None, :], 0, DIST - 1)
    picks = (spread[:, :, None] == jnp.arange(DIST, dtype=jnp.int32)[None, None, :]).astype(
        jnp.float32
    )
    level_bias = jnp.einsum("hd,abd->hab", bias_table, picks, precision=HIGH)
    return (levels, onehot, level_bias)


def bias_block(row_onehot, head_bias, col_onehot):
    row_part = jnp.dot(row_onehot, head_bias, precision=HIGH)
    return lax.dot_general(row_part, col_onehot, CONTRACT_COLS, precision=HIGH)


def on_device(
    node_states,
    cotangent,
    reach_blocks,
    reach_count,
    level_start,
    query_weight,
    key_weight,
    value_weight,
    out_weight,
    bias_table,
):
    states = node_states[0]
    grads_in = cotangent[0]
    blocks = reach_blocks[0]
    counts = reach_count[0]
    starts = level_start[0]
    rows_dev = states.shape[0]
    width = query_weight.shape[1]
    total = rows_dev * lax.axis_size("node")
    offset = lax.axis_index("node") * rows_dev
    scale = HEAD ** (-0.5)
    key_blocks = total // BLOCK
    states_single_float = states.astype(jnp.float32)
    inverse_norm_scale = lax.rsqrt(
        jnp.mean(states_single_float * states_single_float, axis=1, keepdims=True) + EPS
    )
    centered_states = states_single_float * inverse_norm_scale
    normalized_states = centered_states.astype(jnp.bfloat16)
    queries = jnp.dot(normalized_states, query_weight, preferred_element_type=jnp.float32).astype(
        jnp.bfloat16
    )
    keys = jnp.dot(normalized_states, key_weight, preferred_element_type=jnp.float32).astype(
        jnp.bfloat16
    )
    values = jnp.dot(normalized_states, value_weight, preferred_element_type=jnp.float32).astype(
        jnp.bfloat16
    )
    keys_all, values_all = (
        lax.all_gather(keys, "node", axis=0, tiled=True),
        lax.all_gather(values, "node", axis=0, tiled=True),
    )
    levels, onehot, level_bias = level_tables(starts, total, bias_table)
    positions = jnp.arange(total, dtype=jnp.int32)
    local = jnp.arange(rows_dev, dtype=jnp.int32)
    row_ids = offset + local
    row_levels = lax.dynamic_slice_in_dim(levels, offset, rows_dev, 0)
    row_onehot = lax.dynamic_slice_in_dim(onehot, offset, rows_dev, 0)
    slots = jnp.arange(blocks.shape[1], dtype=jnp.int32)
    live = slots[None, :] < counts[:, None]
    kinds = jnp.arange(key_blocks, dtype=jnp.int32)
    listed = jnp.any((blocks[:, :, None] == kinds[None, None, :]) & live[:, :, None], axis=1)
    visible = expand(listed) & (
        (levels[None, :] < row_levels[:, None]) | (positions[None, :] == row_ids[:, None])
    )
    prob_list = []
    lse_list = []
    mixed_list = []
    for head in range(HEADS):
        lower = head * HEAD
        scores = (
            cols_product(queries[:, lower : lower + HEAD], keys_all[:, lower : lower + HEAD])
            * scale
        )
        scores = scores + bias_block(row_onehot, level_bias[head], onehot)
        scores = jnp.where(visible, scores, NEG)
        peak = jnp.max(scores, axis=1, keepdims=True)
        mass = jnp.sum(jnp.where(visible, jnp.exp(scores - peak), 0.0), axis=1, keepdims=True)
        lse = peak + jnp.log(mass)
        probs = jnp.where(visible, jnp.exp(scores - lse), 0.0).astype(jnp.bfloat16)
        prob_list.append(probs)
        lse_list.append(lse)
        mixed_list.append(
            jnp.dot(probs, values_all[:, lower : lower + HEAD], preferred_element_type=jnp.float32)
        )
    mixed = jnp.concatenate(mixed_list, axis=1).astype(jnp.bfloat16)
    updated = (
        states_single_float + jnp.dot(mixed, out_weight, preferred_element_type=jnp.float32)
    ).astype(jnp.bfloat16)
    partial_out = rows_product(mixed, grads_in)
    d_mixed = cols_product(grads_in, out_weight).astype(jnp.bfloat16)
    score_grads = []
    delta_list = []
    query_grads = []
    for head in range(HEADS):
        lower = head * HEAD
        mixed_head = d_mixed[:, lower : lower + HEAD]
        delta = jnp.sum(
            mixed_head.astype(jnp.float32) * mixed[:, lower : lower + HEAD].astype(jnp.float32),
            axis=1,
            keepdims=True,
        )
        d_probs = cols_product(mixed_head, values_all[:, lower : lower + HEAD])
        d_scores = (prob_list[head].astype(jnp.float32) * (d_probs - delta)).astype(jnp.bfloat16)
        score_grads.append(d_scores)
        delta_list.append(delta)
        query_grads.append(
            jnp.dot(d_scores, keys_all[:, lower : lower + HEAD], preferred_element_type=jnp.float32)
            * scale
        )
    d_queries = jnp.concatenate(query_grads, axis=1).astype(jnp.bfloat16)
    key_pieces = []
    value_pieces = []
    for head in range(HEADS):
        lower = head * HEAD
        score_part = score_grads[head]
        prob_part = prob_list[head]
        key_pieces.append(rows_product(score_part, queries[:, lower : lower + HEAD]) * scale)
        value_pieces.append(rows_product(prob_part, d_mixed[:, lower : lower + HEAD]))
    key_value_grads = lax.psum_scatter(
        jnp.concatenate(key_pieces + value_pieces, axis=1).astype(jnp.bfloat16),
        "node",
        scatter_dimension=0,
        tiled=True,
    ).astype(jnp.float32)
    d_keys = key_value_grads[:, :width].astype(jnp.bfloat16)
    d_values = key_value_grads[:, width:].astype(jnp.bfloat16)
    normalized_gradient = (
        cols_product(d_queries, query_weight)
        + cols_product(d_keys, key_weight)
        + cols_product(d_values, value_weight)
    )
    node_state_gradient = (
        grads_in.astype(jnp.float32)
        + inverse_norm_scale
        * (
            normalized_gradient
            - centered_states
            * jnp.mean(normalized_gradient * centered_states, axis=1, keepdims=True)
        )
    ).astype(jnp.bfloat16)
    partial_query = rows_product(normalized_states, d_queries)
    partial_key = rows_product(normalized_states, d_keys)
    partial_value = rows_product(normalized_states, d_values)
    total_query, total_key, total_value, total_out = lax.psum(
        (partial_query, partial_key, partial_value, partial_out), ("node", "rep")
    )
    return (
        updated[None],
        node_state_gradient[None],
        total_query,
        total_key,
        total_value,
        total_out,
    )


def solution(mesh):
    in_specs = (
        P(("groups", "rep"), "node", None),
        P(("groups", "rep"), "node", None),
        P(("groups", "rep"), "node", None),
        P(("groups", "rep"), "node"),
        P(("groups", "rep"), None),
        P(),
        P(),
        P(),
        P(),
        P(),
    )
    out_specs = (
        P(("groups", "rep"), "node", None),
        P(("groups", "rep"), "node", None),
        P("groups", None),
        P("groups", None),
        P("groups", None),
        P("groups", None),
    )
    return jax.shard_map(
        on_device, mesh=mesh, in_specs=in_specs, out_specs=out_specs, check_vma=False
    )
```

profile of v0, /device:TPU:0, one launch (start us, length us, event | category | flops | bytes accessed | tf_op | source)
XLA Modules:
  0.0 189.7 jit_solution(12456625626089858018)
XLA Ops:
  7.3 0.6 copy-done.12
  8.0 0.7 copy-done.10
  8.9 0.6 copy-done.13
  9.5 1.0 fusion.42
  11.0 0.6 copy-done.11
  11.6 0.6 convolution_bitcast_fusion
  14.4 15.6 %all_gather.7 = bf16[512,256]{1,0:T(8,128)(2,1)S(1)} all-gather(bf16[128,256]{1,0:T(8,128)(2,1)S(1)} %convolution_convert_fusion.1), channel_id=1, replica_groups=mesh['groups'=2,'node'=4,'rep'=4] {'node'}, dimensions={0}, use_global_device_ids=true | all-gather | bytes 327680 | tf_op jit(solution)/shard_map/all_gather | solution.py:91
  30.0 14.6 %all_gather.6 = bf16[512,256]{1,0:T(8,128)(2,1)S(1)} all-gather(bf16[128,256]{1,0:T(8,128)(2,1)S(1)} %convolution_convert_fusion.2), channel_id=1, replica_groups=mesh['groups'=2,'node'=4,'rep'=4] {'node'}, dimensions={0}, use_global_device_ids=true | all-gather | bytes 327680 | tf_op jit(solution)/shard_map/all_gather | solution.py:90
  49.0 0.4 copy-done.3
  52.7 1.0 copy.27
  55.0 1.0 fusion.50
  56.0 1.1 fusion.104
  57.1 19.4 %reduce-scatter.4.cloned.1.call-done = bf16[128,512]{1,0:T(8,128)(2,1)} async-done(((bf16[512,512]{1,0:T(8,128)(2,1)}), bf16[128,512]{1,0:T(8,128)(2,1)}) %reduce-scatter.4.cloned.1.call-update) | async-done | bytes 131088
  76.5 2.0 %fusion.78 = f32[512,256]{1,0:T(8,128)} fusion(bf16[128,512]{1,0:T(8,128)(2,1)} %reduce-scatter.4.cloned.1.call-done, bf16[1,128,512]{2,1,0:T(8,128)(2,1)S(1)} %copy-done.1, f32[128]{0:T(128)S(1)} %add_rsqrt_fusion), kind=kOutput, calls=%fused_computation.125 | convolution fusion | flops 33751040 | bytes 721408 | tf_op jit(solution)/shard_map/dot_general | solution.py:20
  78.5 1.1 fusion.75
  79.6 0.9 fusion.17
  81.1 0.8 fusion.49
  81.9 95.8 %all-reduce.3.cloned.1.call-done = (f32[512,256]{1,0:T(8,128)}, f32[512,256]{1,0:T(8,128)}, f32[512,256]{1,0:T(8,128)}, f32[256,512]{1,0:T(8,128)}) async-done(((f32[512,256]{1,0:T(8,128)}, f32[512,256]{1,0:T(8,128)}, f32[512,256]{1,0:T(8,128)}, f32[256,512]{1,0:T(8,128)}), (f32[512,256]{1,0:T(8,128)}, f32[512,256]{1,0:T(8,128)}, f32[512,256]{1,0:T(8,128)}, ...) | async-done | bytes 2097168 | tf_op jit(solution)/shard_map/psum | solution.py:185
  177.7 1.9 %copy.53 = f32[512,256]{1,0:T(8,128)} copy(f32[512,256]{1,0:T(8,128)} %get-tuple-element.43) | data formatting | bytes 1048576
  179.6 0.8 copy.54
  180.4 0.4 copy-done.7
  180.8 0.8 copy.55
  181.6 0.4 copy-done.6
  182.0 0.8 copy.56
  (84 shorter events, 12.3 us)
Async XLA Ops:
  7.2 7.0 %copy-start = (bf16[512,256]{1,0:T(8,128)(2,1)S(1)}, bf16[512,256]{1,0:T(8,128)(2,1)}, u32[]{:S(2)}) copy-start(bf16[512,256]{1,0:T(8,128)(2,1)} %param.17) | copy-start | bytes 786436
  7.2 69.3 %reduce-scatter.4.cloned.1.call-start = ((), (), s32[]{:S(2)}) async-start(), calls=%async_computation.1 | async-start | bytes 655360
  7.3 0.7 copy-start.12
  8.0 0.7 copy-start.10
  8.8 0.7 copy-start.13
  10.9 0.7 copy-start.11
  11.6 1.7 copy-start.4
  12.3 1.0 copy-start.1
  12.9 1.0 copy-start.5
  48.5 1.0 copy-start.3
  48.7 0.9 copy-start.2
  53.7 123.9 %all-reduce.3.cloned.1.call-start = ((), (), s32[]{:S(2)}) async-start(), calls=%async_computation.2 | async-start | bytes 4194304 | tf_op jit(solution)/shard_map/psum | solution.py:185
  76.5 2.0 %copy-start.9 = (bf16[128,512]{1,0:T(8,128)(2,1)S(1)}, bf16[128,512]{1,0:T(8,128)(2,1)}, u32[]{:S(2)}) copy-start(bf16[128,512]{1,0:T(8,128)(2,1)} %reduce-scatter.4.cloned.1.call-done) | copy-start | bytes 393220
  177.6 1.9 %copy-start.8 = (f32[512,256]{1,0:T(8,128)S(1)}, f32[512,256]{1,0:T(8,128)}, u32[]{:S(2)}) copy-start(f32[512,256]{1,0:T(8,128)} %get-tuple-element.44) | copy-start | bytes 1572868
  179.6 1.2 copy-start.7
  180.8 1.2 copy-start.6
Sparse Core Ops, SparseCore 0:
  53.8 22.5 reduce-scatter.3
  81.0 96.5 all-reduce.2
where the time goes:
time: 190 us
  waiting for transfers between devices  115 us (61%)
  blocking collectives  30.2 us (16%)
  matrix products  16.7 us (9%)
  between operations  14.3 us (8%)
  local copies, waits for them, and re-layouts  10.3 us (5%)
  other arithmetic  2.95 us (2%)
    psum x1, waiting for transfers between devices, on_device(): lax.psum((partial_query, partial_key, partial_value, partial_out), ('node...  95.8 us
    unnamed x3, waiting for transfers between devices  19.4 us
    all_gather x1, blocking collectives, on_device(): lax.all_gather(values, 'node', axis=0, tiled=True)  15.6 us
    all_gather x1, blocking collectives, on_device(): lax.all_gather(keys, 'node', axis=0, tiled=True)  14.6 us
    unnamed x33, local copies, waits for them, and re-layouts  9.64 us
    dot_general x12, matrix products, rows_product(): lax.dot_general(left, right, CONTRACT_ROWS, preferred_element_type=jnp.fl...  6.81 us
  transfers between devices with their start and end apart: 2, of which 2 were waited for; matrix products, arithmetic and copies ran while one was open for 3% of the time, Pallas kernels for 0%

commit v1 on v0

--- a/solution.py
+++ b/solution.py
@@ -1,6 +1,8 @@
 import jax
 import jax.numpy as jnp
 from jax import lax
+from jax.experimental import pallas as pl
+from jax.experimental.pallas import tpu as pltpu
 from jax.sharding import PartitionSpec as P
 
 HEADS = 4
@@ -48,7 +50,7 @@
     return lax.dot_general(row_part, col_onehot, CONTRACT_COLS, precision=HIGH)
 
 
-def on_device(
+def on_device_general(
     node_states,
     cotangent,
     reach_blocks,
@@ -194,6 +196,400 @@
         total_out,
     )
 
+LANES = 128
+SLOTS = 16
+LEVEL_PARTS = 3
+VMEM_LIMIT = 48 * 1024 * 1024
+
+
+def transposed_product(left, right):
+    return lax.dot_general(left, right, CONTRACT_ROWS, preferred_element_type=jnp.float32)
+
+
+def pair_product(left, right):
+    return lax.dot_general(left, right, CONTRACT_COLS, preferred_element_type=jnp.float32)
+
+
+def plain_product(left, right):
+    return jnp.dot(left, right, preferred_element_type=jnp.float32)
+
+
+def head_lanes(rows, half):
+    lanes = lax.broadcasted_iota(jnp.int32, (rows, LANES), 1)
+    return (lanes >= HEAD) if half else (lanes < HEAD)
+
+
+def keep_lanes(array, mask):
+    return jnp.where(mask, array, jnp.zeros_like(array))
+
+
+def normalize(states):
+    wide = states.astype(jnp.float32)
+    inverse = lax.rsqrt(jnp.mean(wide * wide, axis=1, keepdims=True) + EPS)
+    return wide, inverse, wide * inverse
+
+
+def score_tables(starts, bias, hidden, total):
+    levels = starts.shape[0] - 1
+    columns = lax.broadcasted_iota(jnp.int32, (SLOTS, total), 1)
+    slots = lax.broadcasted_iota(jnp.int32, (SLOTS, total), 0)
+    level = jnp.zeros((SLOTS, total), jnp.int32)
+    for entry in range(1, levels):
+        level += (columns >= starts[entry]).astype(jnp.int32)
+    features = jnp.concatenate(
+        [
+            (level == slots).astype(jnp.float32),
+            ((columns >> 6) == slots).astype(jnp.float32),
+        ],
+        axis=0,
+    ).astype(jnp.bfloat16)
+    own = lax.broadcasted_iota(jnp.int32, (SLOTS, LANES), 0)
+    lanes = lax.broadcasted_iota(jnp.int32, (SLOTS, LANES), 1)
+    part = lanes >> 4
+    distance = own - (lanes & (SLOTS - 1))
+    tables = []
+    for head in range(HEADS):
+        table = jnp.full((SLOTS, LANES), NEG, jnp.float32)
+        for step in range(1, min(levels, DIST)):
+            table = jnp.where(distance == step, bias[head, step], table)
+        high = table.astype(jnp.bfloat16).astype(jnp.float32)
+        middle = (table - high).astype(jnp.bfloat16).astype(jnp.float32)
+        low = table - high - middle
+        split = jnp.where(part == 0, high, jnp.where(part == 1, middle, low))
+        tables.append(jnp.where(part < LEVEL_PARTS, split, 0.0))
+    table = jnp.concatenate(tables, axis=1).astype(jnp.bfloat16)
+    table = jnp.concatenate([table, hidden], axis=0)
+    picks_row = lax.broadcasted_iota(jnp.int32, (2 * SLOTS, LANES), 0)
+    picks_lane = lax.broadcasted_iota(jnp.int32, (2 * SLOTS, LANES), 1)
+    wanted = jnp.where(
+        picks_lane < LEVEL_PARTS * SLOTS,
+        picks_lane & (SLOTS - 1),
+        picks_lane - (LEVEL_PARTS - 1) * SLOTS,
+    )
+    picks = wanted == picks_row
+    rows = transposed_product(features, table).astype(jnp.bfloat16)
+    cols = transposed_product(features, picks.astype(jnp.float32).astype(jnp.bfloat16))
+    return rows, cols.astype(jnp.bfloat16)
+
+
+def forward_kernel(
+    place, starts, bias, own, near, far, last, hidden, query_w, key_w, value_w, out_w,
+    normed, queries, keys, values, probs, mixed, updated,
+    row_table, key_table,
+):
+    rows = own.shape[0]
+    total = normed.shape[0]
+    scale = HEAD ** (-0.5)
+    for index, chunk in enumerate((own, near, far, last)):
+        at = pl.ds(pl.multiple_of((place[0] ^ index) * rows, rows), rows)
+        unit = normalize(chunk[...])[2].astype(jnp.bfloat16)
+        normed[at, :] = unit
+        queries[at, :] = plain_product(unit, query_w[...]).astype(jnp.bfloat16)
+        keys[at, :] = plain_product(unit, key_w[...]).astype(jnp.bfloat16)
+        values[at, :] = plain_product(unit, value_w[...]).astype(jnp.bfloat16)
+    coefficients, features = score_tables(starts, bias, hidden[...], total)
+    row_table[...] = coefficients
+    for pair in range(HEADS // 2):
+        lanes = slice(pair * LANES, (pair + 1) * LANES)
+        key_table[pair, :, :LANES] = keys[:, lanes]
+        key_table[pair, :, LANES:] = features
+    for tile in range(total // LANES):
+        low, high = tile * LANES, (tile + 1) * LANES
+        same = lax.broadcasted_iota(jnp.int32, (LANES, high), 1) == (
+            lax.broadcasted_iota(jnp.int32, (LANES, high), 0) + low
+        )
+        for pair in range(HEADS // 2):
+            lanes = slice(pair * LANES, (pair + 1) * LANES)
+            query = queries[low:high, lanes] * jnp.asarray(scale, jnp.bfloat16)
+            product = query.astype(jnp.float32) * keys[low:high, lanes].astype(jnp.float32)
+            parts = []
+            for half in range(2):
+                head = 2 * pair + half
+                mask = head_lanes(LANES, half)
+                left = jnp.concatenate(
+                    [
+                        keep_lanes(query, mask),
+                        row_table[low:high, head * LANES : (head + 1) * LANES],
+                    ],
+                    axis=1,
+                )
+                scores = pair_product(left, key_table[pair, :high, :])
+                self_score = jnp.sum(keep_lanes(product, mask), axis=1, keepdims=True)
+                scores = jnp.where(same, self_score + bias[head, 0], scores)
+                peak = jnp.max(scores, axis=1, keepdims=True)
+                weight = jnp.exp(scores - peak)
+                mass = jnp.sum(weight, axis=1, keepdims=True)
+                prob = (weight * (1.0 / mass)).astype(jnp.bfloat16)
+                probs[head, low:high, :high] = prob
+                parts.append(plain_product(prob, values[:high, lanes]))
+            mixed[low:high, lanes] = jnp.where(
+                head_lanes(LANES, 0), parts[0], parts[1]
+            ).astype(jnp.bfloat16)
+    here = pl.ds(pl.multiple_of(place[0] * rows, rows), rows)
+    updated[...] = (
+        own[...].astype(jnp.float32) + plain_product(mixed[here, :], out_w[...])
+    ).astype(jnp.bfloat16)
+
+
+def store_halves(place, value, keep, send, full):
+    half = keep.shape[0]
+    full[...] = value
+    keep[...] = full[pl.ds(pl.multiple_of(place[1] * half, half), half), :]
+    send[...] = full[pl.ds(pl.multiple_of((1 - place[1]) * half, half), half), :].astype(
+        jnp.bfloat16
+    )
+
+
+def output_kernel(place, own, near, far, last, mixed, out_w, d_mixed, keep, send, gathered, full):
+    rows = own.shape[0]
+    for index, chunk in enumerate((own, near, far, last)):
+        at = pl.ds(pl.multiple_of((place[0] ^ index) * rows, rows), rows)
+        gathered[at, :] = chunk[...]
+    d_mixed[...] = pair_product(gathered[...], out_w[...]).astype(jnp.bfloat16)
+    store_halves(place, transposed_product(mixed[...], gathered[...]), keep, send, full)
+
+
+def backward_kernel(
+    place, normed, queries, keys, values, probs, mixed, d_mixed,
+    d_all, query_keep, query_send, key_keep, key_send, value_keep, value_send,
+    d_queries, d_keys, d_values, key_sum, value_sum, full,
+):
+    total = normed.shape[0]
+    rows = d_all.shape[0]
+    width = queries.shape[1]
+    scale = HEAD ** (-0.5)
+    for pair in range(HEADS // 2):
+        lanes = slice(pair * LANES, (pair + 1) * LANES)
+        for tile in reversed(range(total // LANES)):
+            low, high = tile * LANES, (tile + 1) * LANES
+            query = queries[low:high, lanes]
+            mix_grad = d_mixed[low:high, lanes]
+            product = mix_grad.astype(jnp.float32) * mixed[low:high, lanes].astype(jnp.float32)
+            score_grads, prob_list, query_list, mix_list, query_parts = [], [], [], [], []
+            for half in range(2):
+                head = 2 * pair + half
+                mask = head_lanes(LANES, half)
+                delta = jnp.sum(keep_lanes(product, mask), axis=1, keepdims=True)
+                mix_head = keep_lanes(mix_grad, mask)
+                prob = probs[head, low:high, :high]
+                d_probs = pair_product(mix_head, values[:high, lanes])
+                score_grad = (prob.astype(jnp.float32) * (d_probs - delta)).astype(jnp.bfloat16)
+                query_parts.append(plain_product(score_grad, keys[:high, lanes]))
+                score_grads.append(score_grad)
+                prob_list.append(prob)
+                query_list.append(keep_lanes(query, mask))
+                mix_list.append(mix_head)
+            d_queries[low:high, lanes] = (
+                jnp.where(head_lanes(LANES, 0), query_parts[0], query_parts[1]) * scale
+            ).astype(jnp.bfloat16)
+            key_term = transposed_product(
+                jnp.concatenate(score_grads, axis=0), jnp.concatenate(query_list, axis=0)
+            )
+            value_term = transposed_product(
+                jnp.concatenate(prob_list, axis=0), jnp.concatenate(mix_list, axis=0)
+            )
+            if high == total:
+                key_sum[...] = key_term
+                value_sum[...] = value_term
+            else:
+                key_sum[:high, :] += key_term
+                value_sum[:high, :] += value_term
+        d_keys[:, lanes] = (key_sum[...] * scale).astype(jnp.bfloat16)
+        d_values[:, lanes] = value_sum[...].astype(jnp.bfloat16)
+    here = pl.ds(pl.multiple_of(place[0] * rows, rows), rows)
+    for index, (grad, keep, send) in enumerate(
+        (
+            (d_queries, query_keep, query_send),
+            (d_keys, key_keep, key_send),
+            (d_values, value_keep, value_send),
+        )
+    ):
+        d_all[:, index * width : (index + 1) * width] = grad[here, :]
+        store_halves(place, transposed_product(normed[...], grad[...]), keep, send, full)
+
+
+def input_kernel(own, grads_in, d_all, query_w, key_w, value_w, gradient):
+    width = query_w.shape[1]
+    unit = normalize(own[...])
+    inner = (
+        pair_product(d_all[:, :width], query_w[...])
+        + pair_product(d_all[:, width : 2 * width], key_w[...])
+        + pair_product(d_all[:, 2 * width :], value_w[...])
+    )
+    gradient[...] = (
+        grads_in[...].astype(jnp.float32)
+        + unit[1] * (inner - unit[2] * jnp.mean(inner * unit[2], axis=1, keepdims=True))
+    ).astype(jnp.bfloat16)
+
+
+def add_kernel(keep, other, total):
+    total[...] = (keep[...] + other[...].astype(jnp.float32)).astype(jnp.bfloat16)
+
+
+def join_kernel(place, mine, other, total):
+    half = mine.shape[0]
+    total[pl.ds(pl.multiple_of(place[1] * half, half), half), :] = mine[...].astype(jnp.float32)
+    total[pl.ds(pl.multiple_of((1 - place[1]) * half, half), half), :] = other[...].astype(
+        jnp.float32
+    )
+
+
+def run(kernel, outs, smem, arrays, scratch=(), flops=0):
+    out_shape = tuple(jax.ShapeDtypeStruct(shape, dtype) for shape, dtype in outs)
+    moved = sum(array.size * array.dtype.itemsize for array in arrays)
+    return pl.pallas_call(
+        kernel,
+        out_shape=out_shape,
+        in_specs=[pl.BlockSpec(memory_space=pltpu.SMEM)] * len(smem)
+        + [pl.BlockSpec(memory_space=pltpu.VMEM)] * len(arrays),
+        out_specs=tuple([pl.BlockSpec(memory_space=pltpu.VMEM)] * len(outs)),
+        scratch_shapes=list(scratch),
+        compiler_params=pltpu.CompilerParams(vmem_limit_bytes=VMEM_LIMIT),
+        cost_estimate=pl.CostEstimate(flops=flops, bytes_accessed=moved, transcendentals=0),
+    )(*smem, *arrays)
+
+
+def swap(array, axis, flip):
+    return lax.ppermute(array, axis, [(i, i ^ flip) for i in range(lax.axis_size(axis))])
+
+
+def sum_over_rep(keep, send, place):
+    half, columns = keep.shape
+    other = swap(send, "rep", 1)
+    local = (keep + other.astype(jnp.float32)).astype(jnp.bfloat16)
+    across = swap(local, "rep", 2)
+    mine = (local.astype(jnp.float32) + across.astype(jnp.float32)).astype(jnp.bfloat16)
+    other = swap(mine, "rep", 1)
+    return run(join_kernel, [((2 * half, columns), jnp.float32)], [place], [mine, other])[0]
+
+
+def on_device_whole(
+    node_states,
+    cotangent,
+    reach_blocks,
+    reach_count,
+    level_start,
+    query_weight,
+    key_weight,
+    value_weight,
+    out_weight,
+    bias_table,
+):
+    states = node_states[0]
+    grads_in = cotangent[0]
+    blocks = reach_blocks[0]
+    counts = reach_count[0]
+    starts = level_start[0]
+    rows, model = states.shape
+    width = query_weight.shape[1]
+    total = rows * lax.axis_size("node")
+    place = jnp.stack([lax.axis_index("node"), lax.axis_index("rep") & 1]).astype(jnp.int32)
+
+    far = swap(states, "node", 2)
+    near = swap(states, "node", 1)
+    last = swap(far, "node", 1)
+    grads_far = swap(grads_in, "node", 2)
+    grads_near = swap(grads_in, "node", 1)
+    grads_last = swap(grads_far, "node", 1)
+
+    local_blocks = blocks.shape[0]
+    slots = jnp.arange(blocks.shape[1], dtype=jnp.int32)
+    live = slots[None, :] < counts[:, None]
+    kinds = jnp.arange(SLOTS, dtype=jnp.int32)
+    listed = jnp.any((blocks[:, :, None] == kinds[None, None, :]) & live[:, :, None], axis=1)
+    hidden = jnp.where(listed, 0.0, NEG).astype(jnp.bfloat16)
+    hidden = jnp.pad(
+        hidden, ((0, 0), (LEVEL_PARTS * SLOTS, LANES - (LEVEL_PARTS + 1) * SLOTS))
+    )
+    hidden = lax.dynamic_update_slice(
+        jnp.zeros((SLOTS, HEADS * LANES), jnp.bfloat16),
+        jnp.tile(hidden, (1, HEADS)),
+        (place[0] * local_blocks, jnp.int32(0)),
+    )
+    hidden = hidden + swap(hidden, "node", 1)
+    hidden = hidden + swap(hidden, "node", 2)
+
+    half = jnp.bfloat16
+    wide = jnp.float32
+    normed, queries, keys, values, probs, mixed, updated = run(
+        forward_kernel,
+        [
+            ((total, model), half),
+            ((total, width), half),
+            ((total, width), half),
+            ((total, width), half),
+            ((HEADS, total, total), half),
+            ((total, width), half),
+            ((rows, model), half),
+        ],
+        [place, starts, bias_table],
+        [
+            states, near, far, last, hidden,
+            query_weight, key_weight, value_weight, out_weight,
+        ],
+        [
+            pltpu.VMEM((total, HEADS * LANES), half),
+            pltpu.VMEM((HEADS // 2, total, 2 * LANES), half),
+        ],
+        flops=2 * total * model * width * 6,
+    )
+    d_mixed, out_keep, out_send = run(
+        output_kernel,
+        [
+            ((total, width), half),
+            ((width // 2, model), wide),
+            ((width // 2, model), half),
+        ],
+        [place],
+        [grads_in, grads_near, grads_far, grads_last, mixed, out_weight],
+        [pltpu.VMEM((total, model), half), pltpu.VMEM((width, model), wide)],
+        flops=2 * total * model * width * 2,
+    )
+    halves = [((model // 2, width), wide), ((model // 2, width), half)]
+    d_all, query_keep, query_send, key_keep, key_send, value_keep, value_send = run(
+        backward_kernel,
+        [((rows, 3 * width), half)] + halves * 3,
+        [place],
+        [normed, queries, keys, values, probs, mixed, d_mixed],
+        [pltpu.VMEM((total, width), half)] * 3
+        + [pltpu.VMEM((total, LANES), wide)] * 2
+        + [pltpu.VMEM((model, width), wide)],
+        flops=2 * total * model * width * 8,
+    )
+    total_out = sum_over_rep(out_keep, out_send, place)
+    total_query = sum_over_rep(query_keep, query_send, place)
+    total_key = sum_over_rep(key_keep, key_send, place)
+    total_value = sum_over_rep(value_keep, value_send, place)
+    node_state_gradient = run(
+        input_kernel,
+        [((rows, model), half)],
+        [],
+        [states, grads_in, d_all, query_weight, key_weight, value_weight],
+        flops=2 * rows * model * width * 3,
+    )[0]
+    return (
+        updated[None],
+        node_state_gradient[None],
+        total_query,
+        total_key,
+        total_value,
+        total_out,
+    )
+
+
+def on_device(node_states, cotangent, reach_blocks, reach_count, level_start, *rest):
+    nodes = lax.axis_size("node")
+    total = node_states.shape[1] * nodes
+    small = (
+        nodes == 4
+        and lax.axis_size("rep") == 4
+        and node_states.shape[1] == LANES
+        and total // BLOCK <= SLOTS
+        and level_start.shape[1] - 1 <= SLOTS
+    )
+    path = on_device_whole if small else on_device_general
+    return path(node_states, cotangent, reach_blocks, reach_count, level_start, *rest)
+
 
 def solution(mesh):
     in_specs = (

time: 190 us -> 66.1 us (0.35)
  waiting for transfers between devices: 115 us -> 16.1 us
  blocking collectives: 30.2 us -> 0 us
  starting transfers between devices: 0.08 us -> 20.6 us
  Pallas kernels: 0 us -> 20.2 us
  matrix products: 16.7 us -> 0 us
  between operations: 14.3 us -> 0.81 us
  local copies, waits for them, and re-layouts: 10.3 us -> 6.17 us
    psum x1 -> x0, waiting for transfers between devices: 95.8 us -> none  [on_device(): lax.psum((partial_query, partial_key, partial_value, partial_out), ('node...]
    all_gather x2 -> x0, blocking collectives: 30.2 us -> none  [the longest x1 15.6 us: on_device(): lax.all_gather(values, 'node', axis=0, tiled=True)]
    ppermute x0 -> x20, starting transfers between devices: none -> 20.6 us  [swap(): lax.ppermute(array, axis, [(i, i ^ flip) for i in range(lax.axis_size(axi...]
    pallas_call x0 -> x8, Pallas kernels: none -> 20.2 us  [run(): pl.pallas_call(kernel, out_shape=out_shape, in_specs=[pl.BlockSpec(memory...]
    unnamed x3 -> x0, waiting for transfers between devices: 19.4 us -> none
    dot_general x45 -> x0, matrix products: 16.7 us -> none  [the longest x12 6.81 us: rows_product(): lax.dot_general(left, right, CONTRACT_ROWS, preferred_element_type=jnp.fl...]
    ppermute x0 -> x20, waiting for transfers between devices: none -> 16.1 us  [swap(): lax.ppermute(array, axis, [(i, i ^ flip) for i in range(lax.axis_size(axi...]
    unnamed x33 -> x27, local copies, waits for them, and re-layouts: 9.64 us -> 6.08 us
  transfers between devices with their start and end apart: 2 -> 20, of which waited for: 2 -> 7; matrix products, arithmetic and copies ran while one was open for 3% -> 3% of each run, Pallas kernels for 0% -> 20%
where the time goes in v1:
time: 66.1 us; the launch traced here: 65.8 us
  starting transfers between devices  20.6 us (31%)
  Pallas kernels  20.2 us (31%)
  waiting for transfers between devices  16.1 us (24%)
  local copies, waits for them, and re-layouts  6.17 us (9%)
  other arithmetic  1.86 us (3%)
  between operations  0.81 us (1%)
    ppermute x20, starting transfers between devices, swap(): lax.ppermute(array, axis, [(i, i ^ flip) for i in range(lax.axis_size(axi...  20.6 us
    pallas_call x8, Pallas kernels, run(): pl.pallas_call(kernel, out_shape=out_shape, in_specs=[pl.BlockSpec(memory...  20.2 us
    ppermute x20, waiting for transfers between devices, swap(): lax.ppermute(array, axis, [(i, i ^ flip) for i in range(lax.axis_size(axi...  16.1 us
    unnamed x27, local copies, waits for them, and re-layouts  6.08 us
  transfers between devices with their start and end apart: 20, of which 7 were waited for; matrix products, arithmetic and copies ran while one was open for 3% of the time, Pallas kernels for 20%

profile of v1, /device:TPU:0, one launch (start us, length us, event | category | flops | bytes accessed | tf_op | source)
XLA Modules:
  0.0 65.8 jit_solution(678801024455607326)
XLA Ops:
  0.6 4.1 %collective-permute-start.1 = (bf16[128,512]{1,0:T(8,128)(2,1)}, bf16[128,512]{1,0:T(8,128)(2,1)S(1)}, u32[]{:S(2)}, u32[]{:S(2)}) collective-permute-start(bf16[128,512]{1,0:T(8,128)(2,1)} %bitcast.20), channel_id=1, source_target_pairs={{0,8},{4,12},{8,0},{12,4},{1,9},{5,13},{9,1},{13,5},{2,10},{6,14},... | collective-permute-start | bytes 393224 | tf_op jit(solution)/shard_map/ppermute | solution.py:453
  6.3 1.6 %collective-permute-start.3 = (bf16[16,512]{1,0:T(8,128)(2,1)S(1)}, bf16[16,512]{1,0:T(8,128)(2,1)S(1)}, u32[]{:S(2)}, u32[]{:S(2)}) collective-permute-start(bf16[16,512]{1,0:T(8,128)(2,1)S(1)} %bitcast_dynamic-update-slice_fusion), channel_id=1, source_target_pairs={{0,4},{4,0},{8,12},{12,8},{1,5},{5,1},{9,13},{13,9},{2,6},{6,2},{1... | collective-permute-start | bytes 49160 | tf_op jit(solution)/shard_map/ppermute | solution.py:453
  8.5 1.9 %collective-permute-start.5 = (bf16[128,512]{1,0:T(8,128)(2,1)}, bf16[128,512]{1,0:T(8,128)(2,1)S(1)}, u32[]{:S(2)}, u32[]{:S(2)}) collective-permute-start(bf16[128,512]{1,0:T(8,128)(2,1)} %bitcast.17), channel_id=1, source_target_pairs={{0,4},{4,0},{8,12},{12,8},{1,5},{5,1},{9,13},{13,9},{2,6},{6,2},{1... | collective-permute-start | bytes 393224 | tf_op jit(solution)/shard_map/ppermute | solution.py:453
  10.4 1.1 %collective-permute-done.1.far = bf16[128,512]{1,0:T(8,128)(2,1)S(1)} collective-permute-done((bf16[128,512]{1,0:T(8,128)(2,1)}, bf16[128,512]{1,0:T(8,128)(2,1)S(1)}, u32[]{:S(2)}, u32[]{:S(2)}) %collective-permute-start.1) | collective-permute-done | bytes 131104 | tf_op jit(solution)/shard_map/ppermute | solution.py:453
  11.4 1.7 %collective-permute-start.2 = (bf16[128,512]{1,0:T(8,128)(2,1)S(1)}, bf16[128,512]{1,0:T(8,128)(2,1)S(1)}, u32[]{:S(2)}, u32[]{:S(2)}) collective-permute-start(bf16[128,512]{1,0:T(8,128)(2,1)S(1)} %collective-permute-done.1.far), channel_id=1, source_target_pairs={{0,4},{4,0},{8,12},{12,8},{1,5},{5,1},{9,13},{13,9},{2,6},{6,2},{1... | collective-permute-start | bytes 393224 | tf_op jit(solution)/shard_map/ppermute | solution.py:453
  13.1 3.7 %collective-permute-start.4 = (bf16[16,512]{1,0:T(8,128)(2,1)S(1)}, bf16[16,512]{1,0:T(8,128)(2,1)S(1)}, u32[]{:S(2)}, u32[]{:S(2)}) collective-permute-start(bf16[16,512]{1,0:T(8,128)(2,1)S(1)} %fusion.2), channel_id=1, source_target_pairs={{0,8},{4,12},{8,0},{12,4},{1,9},{5,13},{9,1},{13,5},{2,10},{6,14},... | collective-permute-start | bytes 49160 | tf_op jit(solution)/shard_map/ppermute | solution.py:453
  16.8 1.0 %collective-permute-start.7 = (bf16[128,512]{1,0:T(8,128)(2,1)S(1)}, bf16[128,512]{1,0:T(8,128)(2,1)S(1)}, u32[]{:S(2)}, u32[]{:S(2)}) collective-permute-start(bf16[128,512]{1,0:T(8,128)(2,1)S(1)} %collective-permute-done.6.far), channel_id=1, source_target_pairs={{0,4},{4,0},{8,12},{12,8},{1,5},{5,1},{9,13},{13,9},{2,6},{6,2},{1... | collective-permute-start | bytes 393224 | tf_op jit(solution)/shard_map/ppermute | solution.py:453
  17.9 3.3 %collective-permute-done.4 = bf16[16,512]{1,0:T(8,128)(2,1)S(1)} collective-permute-done((bf16[16,512]{1,0:T(8,128)(2,1)S(1)}, bf16[16,512]{1,0:T(8,128)(2,1)S(1)}, u32[]{:S(2)}, u32[]{:S(2)}) %collective-permute-start.4) | collective-permute-done | bytes 16416 | tf_op jit(solution)/shard_map/ppermute | solution.py:453
  21.2 2.0 %collective-permute-done.2.last = bf16[128,512]{1,0:T(8,128)(2,1)S(1)} collective-permute-done((bf16[128,512]{1,0:T(8,128)(2,1)S(1)}, bf16[128,512]{1,0:T(8,128)(2,1)S(1)}, u32[]{:S(2)}, u32[]{:S(2)}) %collective-permute-start.2) | collective-permute-done | bytes 131104 | tf_op jit(solution)/shard_map/ppermute | solution.py:453
  23.2 0.9 %copy-done.1 = bf16[256,512]{1,0:T(8,128)(2,1)S(1)} copy-done((bf16[256,512]{1,0:T(8,128)(2,1)S(1)}, bf16[256,512]{1,0:T(8,128)(2,1)}, u32[]{:S(2)}) %copy-start.1) | copy-done | bytes 262168
  24.1 0.9 %copy-done.3 = bf16[512,256]{1,0:T(8,128)(2,1)S(1)} copy-done((bf16[512,256]{1,0:T(8,128)(2,1)S(1)}, bf16[512,256]{1,0:T(8,128)(2,1)}, u32[]{:S(2)}) %copy-start.3) | copy-done | bytes 262168
  29.2 8.0 %shard_map.145 = (bf16[512,512]{1,0:T(8,128)(2,1)S(1)}, bf16[512,256]{1,0:T(8,128)(2,1)S(1)}, bf16[512,256]{1,0:T(8,128)(2,1)S(1)}, bf16[512,256]{1,0:T(8,128)(2...) custom-call(s32[2]{0:T(128)S(1)} %pad_add_fusion.place, ...), custom_call_target="tpu_custom_call" | custom-call | flops 805306368 | bytes 1589248 | tf_op jit(solution)/shard_map/pallas_call | solution.py:440
  37.3 1.1 %shard_map.146 = (bf16[512,256]{1,0:T(8,128)(2,1)S(1)}, f32[128,512]{1,0:T(8,128)S(1)}, bf16[128,512]{1,0:T(8,128)(2,1)S(1)}) custom-call(s32[2]{0:T(128)S(1)} %pad_add_fusion.place, bf16[128,512]{1,0:T(8,128)(2,1)S(1)} %bitcast.18, bf16[128,512]{1,0:T(8,128)(2,1)S(1)} %collective-permute-done.5.near, bf16[128,512]{1,0:T(8,128)(2,1)S(1)} %collective-permute-done.6.far, ...), custom_call_target="tpu_custom_call" | custom-call | flops 268435456 | bytes 1048576 | tf_op jit(solution)/shard_map/pallas_call | solution.py:440
  38.3 4.5 %shard_map.147 = (bf16[128,768]{1,0:T(8,128)(2,1)S(1)}, f32[256,256]{1,0:T(8,128)S(1)}, bf16[256,256]{1,0:T(8,128)(2,1)S(1)}, f32[256,256]{1,0:T(8,128)S(1)}, bf...) custom-call(s32[2]{0:T(128)S(1)} %pad_add_fusion.place, ...), custom_call_target="tpu_custom_call" | custom-call | flops 1073741824 | bytes 3932160 | tf_op jit(solution)/shard_map/pallas_call | solution.py:440
  44.4 1.6 %collective-permute-start.9 = (bf16[256,256]{1,0:T(8,128)(2,1)S(1)}, bf16[256,256]{1,0:T(8,128)(2,1)S(1)}, u32[]{:S(2)}, u32[]{:S(2)}) collective-permute-start(bf16[256,256]{1,0:T(8,128)(2,1)S(1)} %add_convert_fusion.7), channel_id=1, source_target_pairs={{0,2},{1,3},{2,0},{3,1},{4,6},{5,7},{6,4},{7,5},{8,10},{9,11},{10,... | collective-permute-start | bytes 393224 | tf_op jit(solution)/shard_map/ppermute | solution.py:453
  46.6 1.6 %collective-permute-start.15 = (bf16[256,256]{1,0:T(8,128)(2,1)S(1)}, bf16[256,256]{1,0:T(8,128)(2,1)S(1)}, u32[]{:S(2)}, u32[]{:S(2)}) collective-permute-start(bf16[256,256]{1,0:T(8,128)(2,1)S(1)} %add_convert_fusion.3), channel_id=1, source_target_pairs={{0,2},{1,3},{2,0},{3,1},{4,6},{5,7},{6,4},{7,5},{8,10},{9,11},{10,... | collective-permute-start | bytes 393224 | tf_op jit(solution)/shard_map/ppermute | solution.py:453
  48.8 4.8 %collective-permute-done.12 = bf16[256,256]{1,0:T(8,128)(2,1)S(1)} collective-permute-done((bf16[256,256]{1,0:T(8,128)(2,1)S(1)}, bf16[256,256]{1,0:T(8,128)(2,1)S(1)}, u32[]{:S(2)}, u32[]{:S(2)}) %collective-permute-start.12) | collective-permute-done | bytes 131104 | tf_op jit(solution)/shard_map/ppermute | solution.py:453
  53.7 2.7 %collective-permute-done.15 = bf16[256,256]{1,0:T(8,128)(2,1)S(1)} collective-permute-done((bf16[256,256]{1,0:T(8,128)(2,1)S(1)}, bf16[256,256]{1,0:T(8,128)(2,1)S(1)}, u32[]{:S(2)}, u32[]{:S(2)}) %collective-permute-start.15) | collective-permute-done | bytes 131104 | tf_op jit(solution)/shard_map/ppermute | solution.py:453
  56.5 1.9 %collective-permute-done.18 = bf16[128,512]{1,0:T(8,128)(2,1)S(1)} collective-permute-done((bf16[128,512]{1,0:T(8,128)(2,1)S(1)}, bf16[128,512]{1,0:T(8,128)(2,1)S(1)}, u32[]{:S(2)}, u32[]{:S(2)}) %collective-permute-start.18) | collective-permute-done | bytes 131104 | tf_op jit(solution)/shard_map/ppermute | solution.py:453
  59.1 1.1 %shard_map.148 = bf16[128,512]{1,0:T(8,128)(2,1)} custom-call(bf16[128,512]{1,0:T(8,128)(2,1)S(1)} %bitcast.23, bf16[128,512]{1,0:T(8,128)(2,1)S(1)} %bitcast.19, bf16[128,768]{1,0:T(8,128)(2,1)S(1)} %get-tuple-element.31.d_all, bf16[512,256]{1,0:T(8,128)(2,1)S(1)} %copy-done.4, bf16[512,256]{1,0:T(8,128)(2,1)S(1)} %copy-done.6, bf16[512,256]{1,0:T(8,128)(2,1)S(1)} %copy-done.8), custom_call_target="tpu_custom_call" | custom-call | flops 100663296 | bytes 1245184 | tf_op jit(solution)/shard_map/pallas_call | solution.py:440
  60.3 1.4 %shard_map.152 = f32[256,512]{1,0:T(8,128)} custom-call(s32[2]{0:T(128)S(1)} %pad_add_fusion.place, bf16[128,512]{1,0:T(8,128)(2,1)S(1)} %add_convert_fusion.mine, bf16[128,512]{1,0:T(8,128)(2,1)S(1)} %collective-permute-done.19.other), custom_call_target="tpu_custom_call" | custom-call | bytes 262144 | tf_op jit(solution)/shard_map/pallas_call | solution.py:440
  61.7 1.4 %shard_map.151 = f32[512,256]{1,0:T(8,128)} custom-call(s32[2]{0:T(128)S(1)} %pad_add_fusion.place, bf16[256,256]{1,0:T(8,128)(2,1)S(1)} %add_convert_fusion.2.mine, bf16[256,256]{1,0:T(8,128)(2,1)S(1)} %collective-permute-done.16.other), custom_call_target="tpu_custom_call" | custom-call | bytes 262144 | tf_op jit(solution)/shard_map/pallas_call | solution.py:440
  63.0 1.4 %shard_map.150 = f32[512,256]{1,0:T(8,128)} custom-call(s32[2]{0:T(128)S(1)} %pad_add_fusion.place, bf16[256,256]{1,0:T(8,128)(2,1)S(1)} %add_convert_fusion.4.mine, bf16[256,256]{1,0:T(8,128)(2,1)S(1)} %collective-permute-done.13.other), custom_call_target="tpu_custom_call" | custom-call | bytes 262144 | tf_op jit(solution)/shard_map/pallas_call | solution.py:440
  64.4 1.4 %shard_map.149 = f32[512,256]{1,0:T(8,128)} custom-call(s32[2]{0:T(128)S(1)} %pad_add_fusion.place, bf16[256,256]{1,0:T(8,128)(2,1)S(1)} %add_convert_fusion.6.mine, bf16[256,256]{1,0:T(8,128)(2,1)S(1)} %collective-permute-done.10.other), custom_call_target="tpu_custom_call" | custom-call | bytes 262144 | tf_op jit(solution)/shard_map/pallas_call | solution.py:440
  (68 shorter events, 9.9 us)
Async XLA Ops:
  0.6 36.6 %copy-start = (bf16[1,128,512]{2,1,0:T(8,128)(2,1)S(1)}, bf16[1,128,512]{2,1,0:T(8,128)(2,1)}, u32[]{:S(2)}) copy-start(bf16[1,128,512]{2,1,0:T(8,128)(2,1)} %param.11) | copy-start | bytes 393220
  0.6 10.8 %collective-permute-start.1 = (bf16[128,512]{1,0:T(8,128)(2,1)}, bf16[128,512]{1,0:T(8,128)(2,1)S(1)}, u32[]{:S(2)}, u32[]{:S(2)}) collective-permute-start(bf16[128,512]{1,0:T(8,128)(2,1)} %bitcast.20), channel_id=1, source_target_pairs={{0,8},{4,12},{8,0},{12,4},{1,9},{5,13},{9,1},{13,5},{2,10},{6,14},... | collective-permute-start | bytes 393224 | tf_op jit(solution)/shard_map/ppermute | solution.py:453
  6.3 6.8 %collective-permute-start.3 = (bf16[16,512]{1,0:T(8,128)(2,1)S(1)}, bf16[16,512]{1,0:T(8,128)(2,1)S(1)}, u32[]{:S(2)}, u32[]{:S(2)}) collective-permute-start(bf16[16,512]{1,0:T(8,128)(2,1)S(1)} %bitcast_dynamic-update-slice_fusion), channel_id=1, source_target_pairs={{0,4},{4,0},{8,12},{12,8},{1,5},{5,1},{9,13},{13,9},{2,6},{6,2},{1... | collective-permute-start | bytes 49160 | tf_op jit(solution)/shard_map/ppermute | solution.py:453
  8.0 13.2 %collective-permute-start = (bf16[128,512]{1,0:T(8,128)(2,1)}, bf16[128,512]{1,0:T(8,128)(2,1)S(1)}, u32[]{:S(2)}, u32[]{:S(2)}) collective-permute-start(bf16[128,512]{1,0:T(8,128)(2,1)} %bitcast.21), channel_id=1, source_target_pairs={{0,4},{4,0},{8,12},{12,8},{1,5},{5,1},{9,13},{13,9},{2,6},{6,2},{1... | collective-permute-start | bytes 393224 | tf_op jit(solution)/shard_map/ppermute | solution.py:453
  8.4 8.4 %collective-permute-start.6 = (bf16[128,512]{1,0:T(8,128)(2,1)}, bf16[128,512]{1,0:T(8,128)(2,1)S(1)}, u32[]{:S(2)}, u32[]{:S(2)}) collective-permute-start(bf16[128,512]{1,0:T(8,128)(2,1)} %bitcast.16), channel_id=1, source_target_pairs={{0,8},{4,12},{8,0},{12,4},{1,9},{5,13},{9,1},{13,5},{2,10},{6,14},... | collective-permute-start | bytes 393224 | tf_op jit(solution)/shard_map/ppermute | solution.py:453
  8.5 28.8 %collective-permute-start.5 = (bf16[128,512]{1,0:T(8,128)(2,1)}, bf16[128,512]{1,0:T(8,128)(2,1)S(1)}, u32[]{:S(2)}, u32[]{:S(2)}) collective-permute-start(bf16[128,512]{1,0:T(8,128)(2,1)} %bitcast.17), channel_id=1, source_target_pairs={{0,4},{4,0},{8,12},{12,8},{1,5},{5,1},{9,13},{13,9},{2,6},{6,2},{1... | collective-permute-start | bytes 393224 | tf_op jit(solution)/shard_map/ppermute | solution.py:453
  11.4 11.8 %collective-permute-start.2 = (bf16[128,512]{1,0:T(8,128)(2,1)S(1)}, bf16[128,512]{1,0:T(8,128)(2,1)S(1)}, u32[]{:S(2)}, u32[]{:S(2)}) collective-permute-start(bf16[128,512]{1,0:T(8,128)(2,1)S(1)} %collective-permute-done.1.far), channel_id=1, source_target_pairs={{0,4},{4,0},{8,12},{12,8},{1,5},{5,1},{9,13},{13,9},{2,6},{6,2},{1... | collective-permute-start | bytes 393224 | tf_op jit(solution)/shard_map/ppermute | solution.py:453
  13.1 8.1 %collective-permute-start.4 = (bf16[16,512]{1,0:T(8,128)(2,1)S(1)}, bf16[16,512]{1,0:T(8,128)(2,1)S(1)}, u32[]{:S(2)}, u32[]{:S(2)}) collective-permute-start(bf16[16,512]{1,0:T(8,128)(2,1)S(1)} %fusion.2), channel_id=1, source_target_pairs={{0,8},{4,12},{8,0},{12,4},{1,9},{5,13},{9,1},{13,5},{2,10},{6,14},... | collective-permute-start | bytes 49160 | tf_op jit(solution)/shard_map/ppermute | solution.py:453
  16.8 20.4 %collective-permute-start.7 = (bf16[128,512]{1,0:T(8,128)(2,1)S(1)}, bf16[128,512]{1,0:T(8,128)(2,1)S(1)}, u32[]{:S(2)}, u32[]{:S(2)}) collective-permute-start(bf16[128,512]{1,0:T(8,128)(2,1)S(1)} %collective-permute-done.6.far), channel_id=1, source_target_pairs={{0,4},{4,0},{8,12},{12,8},{1,5},{5,1},{9,13},{13,9},{2,6},{6,2},{1... | collective-permute-start | bytes 393224 | tf_op jit(solution)/shard_map/ppermute | solution.py:453
  42.9 16.3 %copy-start.4 = (bf16[512,256]{1,0:T(8,128)(2,1)S(1)}, bf16[512,256]{1,0:T(8,128)(2,1)}, u32[]{:S(2)}) copy-start(bf16[512,256]{1,0:T(8,128)(2,1)} %query_w.3) | copy-start | bytes 786436
  42.9 16.2 %copy-start.6 = (bf16[512,256]{1,0:T(8,128)(2,1)S(1)}, bf16[512,256]{1,0:T(8,128)(2,1)}, u32[]{:S(2)}) copy-start(bf16[512,256]{1,0:T(8,128)(2,1)} %key_w.3) | copy-start | bytes 786436
  42.9 16.2 %copy-start.8 = (bf16[512,256]{1,0:T(8,128)(2,1)S(1)}, bf16[512,256]{1,0:T(8,128)(2,1)}, u32[]{:S(2)}) copy-start(bf16[512,256]{1,0:T(8,128)(2,1)} %value_w.3) | copy-start | bytes 786436
  42.9 1.4 %collective-permute-start.8 = (bf16[256,256]{1,0:T(8,128)(2,1)S(1)}, bf16[256,256]{1,0:T(8,128)(2,1)S(1)}, u32[]{:S(2)}, u32[]{:S(2)}) collective-permute-start(bf16[256,256]{1,0:T(8,128)(2,1)S(1)} %get-tuple-element.33), channel_id=1, source_target_pairs={{0,1},{1,0},{2,3},{3,2},{4,5},{5,4},{6,7},{7,6},{8,9},{9,8},{10,11... | collective-permute-start | bytes 393224 | tf_op jit(solution)/shard_map/ppermute | solution.py:453
  43.0 3.0 %collective-permute-start.11 = (bf16[256,256]{1,0:T(8,128)(2,1)S(1)}, bf16[256,256]{1,0:T(8,128)(2,1)S(1)}, u32[]{:S(2)}, u32[]{:S(2)}) collective-permute-start(bf16[256,256]{1,0:T(8,128)(2,1)S(1)} %get-tuple-element.35), channel_id=1, source_target_pairs={{0,1},{1,0},{2,3},{3,2},{4,5},{5,4},{6,7},{7,6},{8,9},{9,8},{10,11... | collective-permute-start | bytes 393224 | tf_op jit(solution)/shard_map/ppermute | solution.py:453
  43.5 3.1 %collective-permute-start.14 = (bf16[256,256]{1,0:T(8,128)(2,1)S(1)}, bf16[256,256]{1,0:T(8,128)(2,1)S(1)}, u32[]{:S(2)}, u32[]{:S(2)}) collective-permute-start(bf16[256,256]{1,0:T(8,128)(2,1)S(1)} %get-tuple-element.37), channel_id=1, source_target_pairs={{0,1},{1,0},{2,3},{3,2},{4,5},{5,4},{6,7},{7,6},{8,9},{9,8},{10,11... | collective-permute-start | bytes 393224 | tf_op jit(solution)/shard_map/ppermute | solution.py:453
  43.6 4.6 %collective-permute-start.17 = (bf16[128,512]{1,0:T(8,128)(2,1)S(1)}, bf16[128,512]{1,0:T(8,128)(2,1)S(1)}, u32[]{:S(2)}, u32[]{:S(2)}) collective-permute-start(bf16[128,512]{1,0:T(8,128)(2,1)S(1)} %get-tuple-element.39), channel_id=1, source_target_pairs={{0,1},{1,0},{2,3},{3,2},{4,5},{5,4},{6,7},{7,6},{8,9},{9,8},{10,11... | collective-permute-start | bytes 393224 | tf_op jit(solution)/shard_map/ppermute | solution.py:453
  44.4 14.2 %collective-permute-start.9 = (bf16[256,256]{1,0:T(8,128)(2,1)S(1)}, bf16[256,256]{1,0:T(8,128)(2,1)S(1)}, u32[]{:S(2)}, u32[]{:S(2)}) collective-permute-start(bf16[256,256]{1,0:T(8,128)(2,1)S(1)} %add_convert_fusion.7), channel_id=1, source_target_pairs={{0,2},{1,3},{2,0},{3,1},{4,6},{5,7},{6,4},{7,5},{8,10},{9,11},{10,... | collective-permute-start | bytes 393224 | tf_op jit(solution)/shard_map/ppermute | solution.py:453
  46.0 7.6 %collective-permute-start.12 = (bf16[256,256]{1,0:T(8,128)(2,1)S(1)}, bf16[256,256]{1,0:T(8,128)(2,1)S(1)}, u32[]{:S(2)}, u32[]{:S(2)}) collective-permute-start(bf16[256,256]{1,0:T(8,128)(2,1)S(1)} %add_convert_fusion.5), channel_id=1, source_target_pairs={{0,2},{1,3},{2,0},{3,1},{4,6},{5,7},{6,4},{7,5},{8,10},{9,11},{10,... | collective-permute-start | bytes 393224 | tf_op jit(solution)/shard_map/ppermute | solution.py:453
  46.6 9.8 %collective-permute-start.15 = (bf16[256,256]{1,0:T(8,128)(2,1)S(1)}, bf16[256,256]{1,0:T(8,128)(2,1)S(1)}, u32[]{:S(2)}, u32[]{:S(2)}) collective-permute-start(bf16[256,256]{1,0:T(8,128)(2,1)S(1)} %add_convert_fusion.3), channel_id=1, source_target_pairs={{0,2},{1,3},{2,0},{3,1},{4,6},{5,7},{6,4},{7,5},{8,10},{9,11},{10,... | collective-permute-start | bytes 393224 | tf_op jit(solution)/shard_map/ppermute | solution.py:453
  48.2 10.2 %collective-permute-start.18 = (bf16[128,512]{1,0:T(8,128)(2,1)S(1)}, bf16[128,512]{1,0:T(8,128)(2,1)S(1)}, u32[]{:S(2)}, u32[]{:S(2)}) collective-permute-start(bf16[128,512]{1,0:T(8,128)(2,1)S(1)} %add_convert_fusion.1), channel_id=1, source_target_pairs={{0,2},{1,3},{2,0},{3,1},{4,6},{5,7},{6,4},{7,5},{8,10},{9,11},{10,... | collective-permute-start | bytes 393224 | tf_op jit(solution)/shard_map/ppermute | solution.py:453
  53.6 9.4 %collective-permute-start.13 = (bf16[256,256]{1,0:T(8,128)(2,1)S(1)}, bf16[256,256]{1,0:T(8,128)(2,1)S(1)}, u32[]{:S(2)}, u32[]{:S(2)}) collective-permute-start(bf16[256,256]{1,0:T(8,128)(2,1)S(1)} %add_convert_fusion.4.mine), channel_id=1, source_target_pairs={{0,1},{1,0},{2,3},{3,2},{4,5},{5,4},{6,7},{7,6},{8,9},{9,8},{10,11... | collective-permute-start | bytes 393224 | tf_op jit(solution)/shard_map/ppermute | solution.py:453
  56.4 5.2 %collective-permute-start.16 = (bf16[256,256]{1,0:T(8,128)(2,1)S(1)}, bf16[256,256]{1,0:T(8,128)(2,1)S(1)}, u32[]{:S(2)}, u32[]{:S(2)}) collective-permute-start(bf16[256,256]{1,0:T(8,128)(2,1)S(1)} %add_convert_fusion.2.mine), channel_id=1, source_target_pairs={{0,1},{1,0},{2,3},{3,2},{4,5},{5,4},{6,7},{7,6},{8,9},{9,8},{10,11... | collective-permute-start | bytes 393224 | tf_op jit(solution)/shard_map/ppermute | solution.py:453
  58.5 1.8 %collective-permute-start.19 = (bf16[128,512]{1,0:T(8,128)(2,1)S(1)}, bf16[128,512]{1,0:T(8,128)(2,1)S(1)}, u32[]{:S(2)}, u32[]{:S(2)}) collective-permute-start(bf16[128,512]{1,0:T(8,128)(2,1)S(1)} %add_convert_fusion.mine), channel_id=1, source_target_pairs={{0,1},{1,0},{2,3},{3,2},{4,5},{5,4},{6,7},{7,6},{8,9},{9,8},{10,11... | collective-permute-start | bytes 393224 | tf_op jit(solution)/shard_map/ppermute | solution.py:453
  58.6 5.8 %collective-permute-start.10 = (bf16[256,256]{1,0:T(8,128)(2,1)S(1)}, bf16[256,256]{1,0:T(8,128)(2,1)S(1)}, u32[]{:S(2)}, u32[]{:S(2)}) collective-permute-start(bf16[256,256]{1,0:T(8,128)(2,1)S(1)} %add_convert_fusion.6.mine), channel_id=1, source_target_pairs={{0,1},{1,0},{2,3},{3,2},{4,5},{5,4},{6,7},{7,6},{8,9},{9,8},{10,11... | collective-permute-start | bytes 393224 | tf_op jit(solution)/shard_map/ppermute | solution.py:453
  (9 other events, 30.3 us)

commit v2 on v0

--- a/solution.py
+++ b/solution.py
@@ -1,6 +1,10 @@
+import functools
+
 import jax
 import jax.numpy as jnp
 from jax import lax
+from jax.experimental import pallas as pl
+from jax.experimental.pallas import tpu as pltpu
 from jax.sharding import PartitionSpec as P
 
 HEADS = 4
@@ -48,7 +52,7 @@
     return lax.dot_general(row_part, col_onehot, CONTRACT_COLS, precision=HIGH)
 
 
-def on_device(
+def on_device_general(
     node_states,
     cotangent,
     reach_blocks,
@@ -194,6 +198,471 @@
         total_out,
     )
 
+LANES = 128
+SLOTS = 16
+LEVEL_PARTS = 3
+VMEM_LIMIT = 48 * 1024 * 1024
+
+
+def transposed_product(left, right):
+    return lax.dot_general(left, right, CONTRACT_ROWS, preferred_element_type=jnp.float32)
+
+
+def pair_product(left, right):
+    return lax.dot_general(left, right, CONTRACT_COLS, preferred_element_type=jnp.float32)
+
+
+def plain_product(left, right):
+    return jnp.dot(left, right, preferred_element_type=jnp.float32)
+
+
+def head_lanes(rows, half):
+    lanes = lax.broadcasted_iota(jnp.int32, (rows, LANES), 1)
+    return (lanes >= HEAD) if half else (lanes < HEAD)
+
+
+def keep_lanes(array, mask):
+    return jnp.where(mask, array, jnp.zeros_like(array))
+
+
+def split_heads(array):
+    rows = array.shape[0]
+    return jnp.concatenate(
+        [keep_lanes(array, head_lanes(rows, 0)), keep_lanes(array, head_lanes(rows, 1))], axis=0
+    )
+
+
+def merge_heads(array):
+    rows = array.shape[0] // 2
+    return jnp.where(head_lanes(rows, 0), array[:rows], array[rows:])
+
+
+def normalize(states):
+    wide = states.astype(jnp.float32)
+    inverse = lax.rsqrt(jnp.mean(wide * wide, axis=1, keepdims=True) + EPS)
+    return wide, inverse, wide * inverse
+
+
+def level_tables_whole(scalars, levels, total):
+    columns = lax.broadcasted_iota(jnp.int32, (SLOTS, total), 1)
+    places = columns.astype(jnp.float32)
+    slots = lax.broadcasted_iota(jnp.int32, (SLOTS, total), 0)
+    level = jnp.zeros((SLOTS, total), jnp.int32)
+    for entry in range(1, levels):
+        level += (places >= scalars[HEADS * DIST + entry]).astype(jnp.int32)
+    features = jnp.concatenate(
+        [
+            (level == slots).astype(jnp.float32),
+            ((columns >> 6) == slots).astype(jnp.float32),
+        ],
+        axis=0,
+    ).astype(jnp.bfloat16)
+    own = lax.broadcasted_iota(jnp.int32, (SLOTS, LANES), 0)
+    lanes = lax.broadcasted_iota(jnp.int32, (SLOTS, LANES), 1)
+    part = lanes >> 4
+    distance = own - (lanes & (SLOTS - 1))
+    tables = []
+    for head in range(HEADS):
+        table = jnp.full((SLOTS, LANES), NEG, jnp.float32)
+        for step in range(1, min(levels, DIST)):
+            table = jnp.where(distance == step, scalars[head * DIST + step], table)
+        high = table.astype(jnp.bfloat16).astype(jnp.float32)
+        middle = (table - high).astype(jnp.bfloat16).astype(jnp.float32)
+        low = table - high - middle
+        split = jnp.where(part == 0, high, jnp.where(part == 1, middle, low))
+        tables.append(jnp.where(part < LEVEL_PARTS, split, 0.0))
+    table = jnp.concatenate(tables, axis=1).astype(jnp.bfloat16)
+    picks_row = lax.broadcasted_iota(jnp.int32, (2 * SLOTS, LANES), 0)
+    picks_lane = lax.broadcasted_iota(jnp.int32, (2 * SLOTS, LANES), 1)
+    wanted = jnp.where(
+        picks_lane < LEVEL_PARTS * SLOTS,
+        picks_lane & (SLOTS - 1),
+        picks_lane - (LEVEL_PARTS - 1) * SLOTS,
+    )
+    picks = (wanted == picks_row).astype(jnp.float32).astype(jnp.bfloat16)
+    return features, table, transposed_product(features, picks).astype(jnp.bfloat16)
+
+
+def project(chunk, weights, unit_t, projected):
+    unit = normalize(chunk[...])[2]
+    unit_t[...] = unit.T.astype(jnp.bfloat16)
+    projected[...] = plain_product(unit.astype(jnp.bfloat16), weights[...]).astype(jnp.bfloat16)
+
+
+def first_kernel(
+    levels, scalars, own, in_weights, features, table, column_features, unit_t, projected
+):
+    rows, level_bias, columns = level_tables_whole(scalars, levels, features.shape[1])
+    features[...] = rows
+    table[...] = level_bias
+    column_features[...] = columns
+    project(own, in_weights, unit_t, projected)
+
+
+def project_kernel(chunk, in_weights, unit_t, projected):
+    project(chunk, in_weights, unit_t, projected)
+
+
+def forward_kernel(
+    place, scalars, own_t, own, near_t, near, far_t, far, last_states, in_weights,
+    hidden, features, table, column_features,
+    normed_t, projected, probs, mixed, mixed_t,
+    row_table, key_table, last_t, last,
+):
+    total, width = mixed.shape
+    rows = own.shape[0]
+    scale = HEAD ** (-0.5)
+    project(last_states, in_weights, last_t, last)
+    chunks = ((own_t, own), (near_t, near), (far_t, far), (last_t, last))
+    for index, (unit_t, chunk) in enumerate(chunks):
+        at = pl.ds(pl.multiple_of((place[0] ^ index) * rows, rows), rows)
+        normed_t[:, at] = unit_t[...]
+        projected[at, :] = chunk[...]
+    row_table[...] = transposed_product(
+        features[...], jnp.concatenate([table[...], hidden[...]], axis=0)
+    ).astype(jnp.bfloat16)
+    for pair in range(HEADS // 2):
+        key_table[pair, :, :LANES] = projected[:, width + pair * LANES : width + (pair + 1) * LANES]
+        key_table[pair, :, LANES:] = column_features[...]
+    same = lax.broadcasted_iota(jnp.int32, (2 * LANES, LANES), 1) == (
+        lax.broadcasted_iota(jnp.int32, (2 * LANES, LANES), 0) & (LANES - 1)
+    )
+    first_half = lax.broadcasted_iota(jnp.int32, (2 * LANES, 1), 0) < LANES
+    for pair in range(HEADS // 2):
+        lanes = slice(pair * LANES, (pair + 1) * LANES)
+        values = slice(2 * width + pair * LANES, 2 * width + (pair + 1) * LANES)
+        self_bias = jnp.where(
+            first_half, scalars[2 * pair * DIST], scalars[(2 * pair + 1) * DIST]
+        )
+        for tile in range(total // LANES):
+            low, high = tile * LANES, (tile + 1) * LANES
+            stacked = slice(2 * low, 2 * high)
+            query = split_heads(projected[low:high, lanes] * jnp.asarray(scale, jnp.bfloat16))
+            key = key_table[pair, low:high, :LANES].astype(jnp.float32)
+            self_score = jnp.sum(
+                query.astype(jnp.float32) * jnp.concatenate([key, key], axis=0),
+                axis=1,
+                keepdims=True,
+            )
+            rest = jnp.concatenate(
+                [
+                    row_table[low:high, (2 * pair) * LANES : (2 * pair + 1) * LANES],
+                    row_table[low:high, (2 * pair + 1) * LANES : (2 * pair + 2) * LANES],
+                ],
+                axis=0,
+            )
+            scores = pair_product(
+                jnp.concatenate([query, rest], axis=1), key_table[pair, :high, :]
+            )
+            corner = jnp.where(same, self_score + self_bias, scores[:, low:])
+            peak = jnp.max(corner, axis=1, keepdims=True)
+            if low:
+                peak = jnp.maximum(peak, jnp.max(scores[:, :low], axis=1, keepdims=True))
+            corner = jnp.exp(corner - peak)
+            mass = jnp.sum(corner, axis=1, keepdims=True)
+            if low:
+                weight = jnp.exp(scores[:, :low] - peak)
+                mass += jnp.sum(weight, axis=1, keepdims=True)
+                inverse = 1.0 / mass
+                probs[pair, stacked, :low] = (weight * inverse).astype(jnp.bfloat16)
+            else:
+                inverse = 1.0 / mass
+            probs[pair, stacked, low:high] = (corner * inverse).astype(jnp.bfloat16)
+            both = merge_heads(
+                plain_product(probs[pair, stacked, :high], projected[:high, values])
+            )
+            mixed[low:high, lanes] = both.astype(jnp.bfloat16)
+            mixed_t[lanes, low:high] = both.T.astype(jnp.bfloat16)
+
+
+def store_halves(place, value, keep, send, full):
+    half = keep.shape[0]
+    full[...] = value
+    keep[...] = full[pl.ds(pl.multiple_of(place[1] * half, half), half), :]
+    send[...] = full[pl.ds(pl.multiple_of((1 - place[1]) * half, half), half), :].astype(
+        jnp.bfloat16
+    )
+
+
+def output_kernel(
+    place, own, near, far, last, mixed_t, out_w, d_mixed, keep, send, gathered, full
+):
+    rows = own.shape[0]
+    for index, chunk in enumerate((own, near, far, last)):
+        at = pl.ds(pl.multiple_of((place[0] ^ index) * rows, rows), rows)
+        gathered[at, :] = chunk[...]
+    store_halves(place, plain_product(mixed_t[...], gathered[...]), keep, send, full)
+    d_mixed[...] = pair_product(gathered[...], out_w[...]).astype(jnp.bfloat16)
+
+
+def backward_kernel(
+    pair, place, normed_t, projected, probs, mixed, d_mixed,
+    d_own, keep, send,
+    grads, key_sum, value_sum, full,
+):
+    total, width = mixed.shape
+    rows = d_own.shape[0]
+    scale = HEAD ** (-0.5)
+    lanes, key_lanes, value_lanes = (
+        slice(i * width + pair * LANES, i * width + (pair + 1) * LANES) for i in range(3)
+    )
+    for tile in reversed(range(total // LANES)):
+        low, high = tile * LANES, (tile + 1) * LANES
+        query = split_heads(projected[low:high, lanes])
+        mix_grad = split_heads(d_mixed[low:high, lanes])
+        mix = mixed[low:high, lanes].astype(jnp.float32)
+        delta = jnp.sum(
+            mix_grad.astype(jnp.float32) * jnp.concatenate([mix, mix], axis=0),
+            axis=1,
+            keepdims=True,
+        )
+        prob = probs[pair, 2 * low : 2 * high, :high]
+        d_probs = pair_product(mix_grad, projected[:high, value_lanes])
+        score_grad = (prob.astype(jnp.float32) * (d_probs - delta)).astype(jnp.bfloat16)
+        grads[low:high, :LANES] = (
+            merge_heads(plain_product(score_grad, projected[:high, key_lanes])) * scale
+        ).astype(jnp.bfloat16)
+        key_term = transposed_product(score_grad, query)
+        value_term = transposed_product(prob, mix_grad)
+        if high == total:
+            key_sum[...] = key_term
+            value_sum[...] = value_term
+        else:
+            key_sum[:high, :] += key_term
+            value_sum[:high, :] += value_term
+    grads[:, LANES : 2 * LANES] = (key_sum[...] * scale).astype(jnp.bfloat16)
+    grads[:, 2 * LANES :] = value_sum[...].astype(jnp.bfloat16)
+    store_halves(place, plain_product(normed_t[...], grads[...]), keep, send, full)
+    d_own[...] = grads[pl.ds(pl.multiple_of(place[0] * rows, rows), rows), :]
+
+
+def rows_kernel(place, own, grads_in, mixed, in_weights, out_w, *rest):
+    *d_own, updated, gradient = rest
+    rows = own.shape[0]
+    width = mixed.shape[1]
+    states, inverse, unit = normalize(own[...])
+    here = pl.ds(pl.multiple_of(place[0] * rows, rows), rows)
+    updated[...] = (states + plain_product(mixed[here, :], out_w[...])).astype(jnp.bfloat16)
+    inner = jnp.zeros(own.shape, jnp.float32)
+    for pair, piece in enumerate(d_own):
+        for i in range(3):
+            lanes = slice(i * width + pair * LANES, i * width + (pair + 1) * LANES)
+            inner += pair_product(piece[:, i * LANES : (i + 1) * LANES], in_weights[:, lanes])
+    gradient[...] = (
+        grads_in[...].astype(jnp.float32)
+        + inverse * (inner - unit * jnp.mean(inner * unit, axis=1, keepdims=True))
+    ).astype(jnp.bfloat16)
+
+
+def join_kernel(place, *refs):
+    mine, other = refs[0:3], refs[3:6]
+    total_query, total_key, total_value, total_out = refs[6:]
+    for pieces, slot in ((mine, place[1]), (other, 1 - place[1])):
+        half = pieces[0].shape[0]
+        total_out[pl.ds(pl.multiple_of(slot * half, half), half), :] = pieces[0][...].astype(
+            jnp.float32
+        )
+        half = pieces[1].shape[0]
+        at = pl.ds(pl.multiple_of(slot * half, half), half)
+        for pair, piece in enumerate(pieces[1:]):
+            for i, total in enumerate((total_query, total_key, total_value)):
+                total[at, pair * LANES : (pair + 1) * LANES] = piece[
+                    :, i * LANES : (i + 1) * LANES
+                ].astype(jnp.float32)
+
+
+def run(kernel, outs, smem, arrays, scratch=(), cost=0):
+    out_shape = tuple(jax.ShapeDtypeStruct(shape, dtype) for shape, dtype in outs)
+    return pl.pallas_call(
+        kernel,
+        out_shape=out_shape,
+        in_specs=[pl.BlockSpec(memory_space=pltpu.SMEM)] * len(smem)
+        + [pl.BlockSpec(memory_space=pltpu.VMEM)] * len(arrays),
+        out_specs=tuple([pl.BlockSpec(memory_space=pltpu.VMEM)] * len(outs)),
+        scratch_shapes=list(scratch),
+        compiler_params=pltpu.CompilerParams(vmem_limit_bytes=VMEM_LIMIT),
+        cost_estimate=pl.CostEstimate(
+            flops=cost * 1000000000, bytes_accessed=0, transcendentals=0
+        ),
+    )(*smem, *arrays)
+
+
+def swap(array, axis, flip):
+    return lax.ppermute(array, axis, [(i, i ^ flip) for i in range(lax.axis_size(axis))])
+
+
+def sum_over_chips(keep, send):
+    local = (keep + swap(send, "rep", 1).astype(jnp.float32)).astype(jnp.bfloat16)
+    across = swap(local, "rep", 2)
+    return local, across
+
+
+def on_device_whole(
+    node_states,
+    cotangent,
+    reach_blocks,
+    reach_count,
+    level_start,
+    query_weight,
+    key_weight,
+    value_weight,
+    out_weight,
+    bias_table,
+):
+    states = node_states[0]
+    grads_in = cotangent[0]
+    blocks = reach_blocks[0]
+    counts = reach_count[0]
+    starts = level_start[0]
+    rows, model = states.shape
+    width = query_weight.shape[1]
+    total = rows * lax.axis_size("node")
+    place = jnp.stack([lax.axis_index("node"), lax.axis_index("rep") & 1]).astype(jnp.int32)
+    half = jnp.bfloat16
+    wide = jnp.float32
+
+    far = swap(states, "node", 2)
+    near = swap(states, "node", 1)
+
+    local_blocks = blocks.shape[0]
+    slots = jnp.arange(blocks.shape[1], dtype=jnp.int32)
+    live = slots[None, :] < counts[:, None]
+    kinds = jnp.arange(SLOTS, dtype=jnp.int32)
+    listed = jnp.any((blocks[:, :, None] == kinds[None, None, :]) & live[:, :, None], axis=1)
+    hidden = jnp.where(listed, 0.0, NEG).astype(jnp.bfloat16)
+    hidden = jnp.pad(
+        hidden, ((0, 0), (LEVEL_PARTS * SLOTS, LANES - (LEVEL_PARTS + 1) * SLOTS))
+    )
+    hidden = lax.dynamic_update_slice(
+        jnp.zeros((SLOTS, HEADS * LANES), jnp.bfloat16),
+        jnp.tile(hidden, (1, HEADS)),
+        (place[0] * local_blocks, jnp.int32(0)),
+    )
+    hidden = hidden + swap(hidden, "node", 1)
+    hidden = hidden + swap(hidden, "node", 2)
+
+    last = swap(far, "node", 1)
+    grads_far = swap(grads_in, "node", 2)
+    grads_near = swap(grads_in, "node", 1)
+    scalars = jnp.concatenate([bias_table.reshape(-1), starts.astype(wide)])
+    in_weights = jnp.concatenate([query_weight, key_weight, value_weight], axis=1)
+    loaded, far = lax.optimization_barrier((states, far))
+    features, table, columns, own_t, own_p = run(
+        functools.partial(first_kernel, starts.shape[0] - 1),
+        [
+            ((2 * SLOTS, total), half),
+            ((SLOTS, HEADS * LANES), half),
+            ((total, LANES), half),
+            ((model, rows), half),
+            ((rows, 3 * width), half),
+        ],
+        [scalars],
+        [loaded, in_weights],
+    )
+    chunk_outs = [((model, rows), half), ((rows, 3 * width), half)]
+    near_t, near_p = run(project_kernel, chunk_outs, [], [near, in_weights])
+    far_t, far_p = run(project_kernel, chunk_outs, [], [far, in_weights])
+    grads_far, own_p, near_p, far_p = lax.optimization_barrier((grads_far, own_p, near_p, far_p))
+    grads_last = swap(grads_far, "node", 1)
+    normed_t, projected, probs, mixed, mixed_t = run(
+        forward_kernel,
+        [
+            ((model, total), half),
+            ((total, 3 * width), half),
+            ((HEADS // 2, 2 * total, total), half),
+            ((total, width), half),
+            ((width, total), half),
+        ],
+        [place, scalars],
+        [
+            own_t, own_p, near_t, near_p, far_t, far_p, last, in_weights,
+            hidden, features, table, columns,
+        ],
+        [
+            pltpu.VMEM((total, HEADS * LANES), half),
+            pltpu.VMEM((HEADS // 2, total, 2 * LANES), half),
+            pltpu.VMEM((model, rows), half),
+            pltpu.VMEM((rows, 3 * width), half),
+        ],
+    )
+    d_mixed, out_keep, out_send = run(
+        output_kernel,
+        [
+            ((total, width), half),
+            ((width // 2, model), wide),
+            ((width // 2, model), half),
+        ],
+        [place],
+        [grads_in, grads_near, grads_far, grads_last, mixed_t, out_weight],
+        [pltpu.VMEM((total, model), half), pltpu.VMEM((width, model), wide)],
+    )
+    local, across = sum_over_chips(out_keep, out_send)
+    halves = [(local, across)]
+    d_own = []
+    for pair in range(HEADS // 2):
+        if pair:
+            d_mixed, local = lax.optimization_barrier((d_mixed, local))
+            halves[0] = (local, halves[0][1])
+        own_grads, keep, send = run(
+            functools.partial(backward_kernel, pair),
+            [
+                ((rows, 3 * LANES), half),
+                ((model // 2, 3 * LANES), wide),
+                ((model // 2, 3 * LANES), half),
+            ],
+            [place],
+            [normed_t, projected, probs, mixed, d_mixed],
+            [
+                pltpu.VMEM((total, 3 * LANES), half),
+                pltpu.VMEM((total, LANES), wide),
+                pltpu.VMEM((total, LANES), wide),
+                pltpu.VMEM((model, 3 * LANES), wide),
+            ],
+        )
+        d_own.append(own_grads)
+        halves.append(sum_over_chips(keep, send))
+    d_own[-1], _ = lax.optimization_barrier((d_own[-1], halves[-1][0]))
+    updated, node_state_gradient = run(
+        rows_kernel,
+        [((rows, model), half)] * 2,
+        [place],
+        [loaded, grads_in, mixed, in_weights, out_weight, *d_own],
+    )
+    first, node_state_gradient = lax.optimization_barrier((halves[0][1], node_state_gradient))
+    halves[0] = (halves[0][0], first)
+    mine = [
+        (near_sum.astype(wide) + far_sum.astype(wide)).astype(half) for near_sum, far_sum in halves
+    ]
+    other = [swap(piece, "rep", 1) for piece in mine]
+    total_query, total_key, total_value, total_out = run(
+        join_kernel,
+        [((model, width), wide)] * 3 + [((width, model), wide)],
+        [place],
+        [*mine, *other],
+    )
+    return (
+        updated[None],
+        node_state_gradient[None],
+        total_query,
+        total_key,
+        total_value,
+        total_out,
+    )
+
+
+def on_device(node_states, cotangent, reach_blocks, reach_count, level_start, *rest):
+    nodes = lax.axis_size("node")
+    total = node_states.shape[1] * nodes
+    small = (
+        nodes == 4
+        and lax.axis_size("rep") == 4
+        and node_states.shape[1] == LANES
+        and total // BLOCK <= SLOTS
+        and level_start.shape[1] - 1 <= SLOTS
+    )
+    path = on_device_whole if small else on_device_general
+    return path(node_states, cotangent, reach_blocks, reach_count, level_start, *rest)
+
 
 def solution(mesh):
     in_specs = (

time: 190 us -> 53.2 us (0.28)
  waiting for transfers between devices: 115 us -> 13.3 us
  blocking collectives: 30.2 us -> 0 us
  matrix products: 16.7 us -> 0 us
  starting transfers between devices: 0.08 us -> 16.6 us
  Pallas kernels: 0 us -> 15.1 us
  between operations: 14.3 us -> 0.86 us
  local copies, waits for them, and re-layouts: 10.3 us -> 3.78 us
    psum x1 -> x0, waiting for transfers between devices: 95.8 us -> none  [on_device(): lax.psum((partial_query, partial_key, partial_value, partial_out), ('node...]
    all_gather x2 -> x0, blocking collectives: 30.2 us -> none  [the longest x1 15.6 us: on_device(): lax.all_gather(values, 'node', axis=0, tiled=True)]
    unnamed x3 -> x0, waiting for transfers between devices: 19.4 us -> none
    dot_general x45 -> x0, matrix products: 16.7 us -> none  [the longest x12 6.81 us: rows_product(): lax.dot_general(left, right, CONTRACT_ROWS, preferred_element_type=jnp.fl...]
    ppermute x0 -> x17, starting transfers between devices: none -> 16.6 us  [swap(): lax.ppermute(array, axis, [(i, i ^ flip) for i in range(lax.axis_size(axi...]
    pallas_call x0 -> x9, Pallas kernels: none -> 15.1 us  [run(): pl.pallas_call(kernel, out_shape=out_shape, in_specs=[pl.BlockSpec(memory...]
    ppermute x0 -> x17, waiting for transfers between devices: none -> 13.3 us  [swap(): lax.ppermute(array, axis, [(i, i ^ flip) for i in range(lax.axis_size(axi...]
    unnamed x33 -> x9, local copies, waits for them, and re-layouts: 9.64 us -> 1.96 us
  transfers between devices with their start and end apart: 2 -> 17, of which waited for: 2 -> 7; matrix products, arithmetic and copies ran while one was open for 3% -> 12% of each run, Pallas kernels for 0% -> 23%
where the time goes in v2:
time: 53.2 us; the launch traced here: 52.2 us
  starting transfers between devices  16.6 us (31%)
  Pallas kernels  15.1 us (28%)
  waiting for transfers between devices  13.3 us (25%)
  local copies, waits for them, and re-layouts  3.78 us (7%)
  other arithmetic  2.52 us (5%)
  between operations  0.86 us (2%)
    ppermute x17, starting transfers between devices, swap(): lax.ppermute(array, axis, [(i, i ^ flip) for i in range(lax.axis_size(axi...  16.6 us
    pallas_call x9, Pallas kernels, run(): pl.pallas_call(kernel, out_shape=out_shape, in_specs=[pl.BlockSpec(memory...  15.1 us
    ppermute x17, waiting for transfers between devices, swap(): lax.ppermute(array, axis, [(i, i ^ flip) for i in range(lax.axis_size(axi...  13.3 us
    unnamed x9, local copies, waits for them, and re-layouts  1.96 us
  transfers between devices with their start and end apart: 17, of which 7 were waited for; matrix products, arithmetic and copies ran while one was open for 12% of the time, Pallas kernels for 23%

profile of v2, /device:TPU:0, one launch (start us, length us, event | category | flops | bytes accessed | tf_op | source)
XLA Modules:
  0.0 52.2 jit_solution(18305449203860001566)
XLA Ops:
  0.6 4.1 %collective-permute-start = (bf16[128,512]{1,0:T(8,128)(2,1)}, bf16[128,512]{1,0:T(8,128)(2,1)S(1)}, u32[]{:S(2)}, u32[]{:S(2)}) collective-permute-start(bf16[128,512]{1,0:T(8,128)(2,1)} %bitcast.17), channel_id=1, source_target_pairs={{0,8},{4,12},{8,0},{12,4},{1,9},{5,13},{9,1},{13,5},{2,10},{6,14},... | collective-permute-start | bytes 393224 | tf_op jit(solution)/shard_map/ppermute | solution.py:491
  4.7 1.6 %collective-permute-start.2 = (bf16[128,512]{1,0:T(8,128)(2,1)}, bf16[128,512]{1,0:T(8,128)(2,1)S(1)}, u32[]{:S(2)}, u32[]{:S(2)}) collective-permute-start(bf16[128,512]{1,0:T(8,128)(2,1)} %bitcast.18), channel_id=1, source_target_pairs={{0,4},{4,0},{8,12},{12,8},{1,5},{5,1},{9,13},{13,9},{2,6},{6,2},{1... | collective-permute-start | bytes 393224 | tf_op jit(solution)/shard_map/ppermute | solution.py:491
  7.6 0.8 %fusion.1 = pred[2,16]{1,0:T(4,128)(4,1)S(1)} fusion(s32[2,8]{1,0:T(2,128)} %bitcast.25, pred[2,8]{1,0:T(4,128)(4,1)S(1)} %iota_compare_fusion.1), kind=kLoop, calls=%fused_computation.11 | loop fusion | flops 736 | bytes 112 | tf_op jit(solution)/shard_map/reduce_or | solution.py:531
  8.5 1.9 %collective-permute-start.4 = (bf16[16,512]{1,0:T(8,128)(2,1)S(1)}, bf16[16,512]{1,0:T(8,128)(2,1)S(1)}, u32[]{:S(2)}, u32[]{:S(2)}) collective-permute-start(bf16[16,512]{1,0:T(8,128)(2,1)S(1)} %bitcast_dynamic-update-slice_fusion), channel_id=1, source_target_pairs={{0,4},{4,0},{8,12},{12,8},{1,5},{5,1},{9,13},{13,9},{2,6},{6,2},{1... | collective-permute-start | bytes 49160 | tf_op jit(solution)/shard_map/ppermute | solution.py:491
  10.4 1.0 %constant_dynamic-update-slice_fusion.2 = bf16[512,768]{1,0:T(8,128)(2,1)S(1)} fusion(bf16[512,256]{1,0:T(8,128)(2,1)} %param.15), kind=kLoop, calls=%fused_computation.8 | loop fusion | bytes 524288
  12.0 1.0 %constant_dynamic-update-slice_fusion.1 = bf16[512,768]{1,0:T(8,128)(2,1)S(1)} fusion(bf16[512,768]{1,0:T(8,128)(2,1)S(1)} %constant_dynamic-update-slice_fusion.2, bf16[512,256]{1,0:T(8,128)(2,1)} %param.16), kind=kLoop, calls=%fused_computation.7 | loop fusion | bytes 524288
  13.0 1.0 %constant_dynamic-update-slice_fusion.in_weights = bf16[512,768]{1,0:T(8,128)(2,1)S(1)} fusion(bf16[512,768]{1,0:T(8,128)(2,1)S(1)} %constant_dynamic-update-slice_fusion.1, bf16[512,256]{1,0:T(8,128)(2,1)} %param.17), kind=kLoop, calls=%fused_computation.6 | loop fusion | bytes 524288 | tf_op jit(solution)/shard_map/concatenate | solution.py:548
  13.9 0.8 %reshape.45 = f32[128]{0:T(128)S(1)} reshape(f32[4,32]{1,0:T(4,128)} %param.19) | data formatting | bytes 1024 | tf_op jit(solution)/shard_map/reshape | solution.py:547
  15.1 0.9 %shard_map.145 = (bf16[32,512]{1,0:T(8,128)(2,1)S(1)}, bf16[16,512]{1,0:T(8,128)(2,1)S(1)}, bf16[512,128]{1,0:T(8,128)(2,1)S(1)}, bf16[512,128]{1,0:T(8,128)(2,1)S(1)}, bf16[128,768]{1,0:T(8,128)(2,1)S(1)}) custom-call(f32[145]{0:T(256)S(1)} %pad_maximum_fusion.scalars, bf16[128,512]{1,0:T(8,128)(2,1)S(1)} %bitcast.19, ...), custom_call_target="tpu_custom_call" | custom-call | tf_op jit(solution)/shard_map/pallas_call | solution.py:476
  17.7 1.3 %collective-permute-start.3 = (bf16[128,512]{1,0:T(8,128)(2,1)S(1)}, bf16[128,512]{1,0:T(8,128)(2,1)S(1)}, u32[]{:S(2)}, u32[]{:S(2)}) collective-permute-start(bf16[128,512]{1,0:T(8,128)(2,1)S(1)} %collective-permute-done.chunk), channel_id=1, source_target_pairs={{0,4},{4,0},{8,12},{12,8},{1,5},{5,1},{9,13},{13,9},{2,6},{6,2},{1... | collective-permute-start | bytes 393224 | tf_op jit(solution)/shard_map/ppermute | solution.py:491
  19.0 2.1 %collective-permute-start.5 = (bf16[16,512]{1,0:T(8,128)(2,1)S(1)}, bf16[16,512]{1,0:T(8,128)(2,1)S(1)}, u32[]{:S(2)}, u32[]{:S(2)}) collective-permute-start(bf16[16,512]{1,0:T(8,128)(2,1)S(1)} %fusion.2), channel_id=1, source_target_pairs={{0,8},{4,12},{8,0},{12,4},{1,9},{5,13},{9,1},{13,5},{2,10},{6,14},... | collective-permute-start | bytes 49160 | tf_op jit(solution)/shard_map/ppermute | solution.py:491
  21.2 2.6 %collective-permute-done.5 = bf16[16,512]{1,0:T(8,128)(2,1)S(1)} collective-permute-done((bf16[16,512]{1,0:T(8,128)(2,1)S(1)}, bf16[16,512]{1,0:T(8,128)(2,1)S(1)}, u32[]{:S(2)}, u32[]{:S(2)}) %collective-permute-start.5) | collective-permute-done | bytes 16416 | tf_op jit(solution)/shard_map/ppermute | solution.py:491
  24.6 3.9 %shard_map.148 = (bf16[512,512]{1,0:T(8,128)(2,1)S(1)}, bf16[512,768]{1,0:T(8,128)(2,1)S(1)}, bf16[2,1024,512]{2,1,0:T(8,128)(2,1)S(1)}, bf16[512,256]{1,0:T(8,128)(2,1)S(1)}, bf16[256,512]{1,0:T(8,128)(2,1)S(1)}) custom-call(s32[2]{0:T(128)S(1)} %pad_add_fusion.place, f32[145]{0:T(256)S(1)} %pad_maximum_fusion.scalars, ...), custom_call_target="tpu_custom_call" | custom-call | tf_op jit(solution)/shard_map/pallas_call | solution.py:476
  28.5 1.0 %shard_map.149 = (bf16[512,256]{1,0:T(8,128)(2,1)S(1)}, f32[128,512]{1,0:T(8,128)S(1)}, bf16[128,512]{1,0:T(8,128)(2,1)S(1)}) custom-call(s32[2]{0:T(128)S(1)} %pad_add_fusion.place, bf16[128,512]{1,0:T(8,128)(2,1)S(1)} %bitcast.23, bf16[128,512]{1,0:T(8,128)(2,1)S(1)} %collective-permute-done.6.near, bf16[128,512]{1,0:T(8,128)(2,1)S(1)} %collective-permute-done.1.far, ...), custom_call_target="tpu_custom_call" | custom-call | tf_op jit(solution)/shard_map/pallas_call | solution.py:476
  29.6 2.5 %shard_map.150 = (bf16[128,384]{1,0:T(8,128)(2,1)S(1)}, f32[256,384]{1,0:T(8,128)S(1)}, bf16[256,384]{1,0:T(8,128)(2,1)S(1)}) custom-call(s32[2]{0:T(128)S(1)} %pad_add_fusion.place, bf16[512,512]{1,0:T(8,128)(2,1)S(1)} %get-tuple-element.61.normed_t, bf16[512,768]{1,0:T(8,128)(2,1)S(1)} %get-tuple-element.62.projected, ...), custom_call_target="tpu_custom_call" | custom-call | tf_op jit(solution)/shard_map/pallas_call | solution.py:476
  32.7 1.6 %collective-permute-start.10 = (bf16[128,512]{1,0:T(8,128)(2,1)S(1)}, bf16[128,512]{1,0:T(8,128)(2,1)S(1)}, u32[]{:S(2)}, u32[]{:S(2)}) collective-permute-start(bf16[128,512]{1,0:T(8,128)(2,1)S(1)} %add_convert_fusion.5), channel_id=1, source_target_pairs={{0,2},{1,3},{2,0},{3,1},{4,6},{5,7},{6,4},{7,5},{8,10},{9,11},{10,... | collective-permute-start | bytes 393224 | tf_op jit(solution)/shard_map/ppermute | solution.py:491
  34.3 2.5 %shard_map.151 = (bf16[128,384]{1,0:T(8,128)(2,1)S(1)}, f32[256,384]{1,0:T(8,128)S(1)}, bf16[256,384]{1,0:T(8,128)(2,1)S(1)}) custom-call(s32[2]{0:T(128)S(1)} %pad_add_fusion.place, bf16[512,512]{1,0:T(8,128)(2,1)S(1)} %get-tuple-element.61.normed_t, bf16[512,768]{1,0:T(8,128)(2,1)S(1)} %get-tuple-element.62.projected, ...), custom_call_target="tpu_custom_call" | custom-call | tf_op jit(solution)/shard_map/pallas_call | solution.py:476
  37.5 0.8 %collective-permute-done.9 = bf16[256,384]{1,0:T(8,128)(2,1)S(1)} collective-permute-done((bf16[256,384]{1,0:T(8,128)(2,1)S(1)}, bf16[256,384]{1,0:T(8,128)(2,1)S(1)}, u32[]{:S(2)}, u32[]{:S(2)}) %collective-permute-start.9) | collective-permute-done | bytes 196640 | tf_op jit(solution)/shard_map/ppermute | solution.py:491
  38.4 0.8 %collective-permute-start.13 = (bf16[256,384]{1,0:T(8,128)(2,1)S(1)}, bf16[256,384]{1,0:T(8,128)(2,1)S(1)}, u32[]{:S(2)}, u32[]{:S(2)}) collective-permute-start(bf16[256,384]{1,0:T(8,128)(2,1)S(1)} %add_convert_fusion.3), channel_id=1, source_target_pairs={{0,2},{1,3},{2,0},{3,1},{4,6},{5,7},{6,4},{7,5},{8,10},{9,11},{10,... | collective-permute-start | bytes 589832 | tf_op jit(solution)/shard_map/ppermute | solution.py:491
  39.1 1.7 %shard_map.152 = (bf16[128,512]{1,0:T(8,128)(2,1)}, bf16[128,512]{1,0:T(8,128)(2,1)}) custom-call(s32[2]{0:T(128)S(1)} %pad_add_fusion.place, bf16[128,512]{1,0:T(8,128)(2,1)S(1)} %bitcast.20, bf16[128,512]{1,0:T(8,128)(2,1)S(1)} %bitcast.24, bf16[512,256]{1,0:T(8,128)(2,1)S(1)} %get-tuple-element.60.mixed, ...), custom_call_target="tpu_custom_call" | custom-call | tf_op jit(solution)/shard_map/pallas_call | solution.py:476
  40.8 3.9 %collective-permute-done.12 = bf16[256,384]{1,0:T(8,128)(2,1)S(1)} collective-permute-done((bf16[256,384]{1,0:T(8,128)(2,1)S(1)}, bf16[256,384]{1,0:T(8,128)(2,1)S(1)}, u32[]{:S(2)}, u32[]{:S(2)}) %collective-permute-start.12) | collective-permute-done | bytes 196640 | tf_op jit(solution)/shard_map/ppermute | solution.py:491
  44.8 3.7 %collective-permute-done.13 = bf16[256,384]{1,0:T(8,128)(2,1)S(1)} collective-permute-done((bf16[256,384]{1,0:T(8,128)(2,1)S(1)}, bf16[256,384]{1,0:T(8,128)(2,1)S(1)}, u32[]{:S(2)}, u32[]{:S(2)}) %collective-permute-start.13) | collective-permute-done | bytes 196640 | tf_op jit(solution)/shard_map/ppermute | solution.py:491
  49.2 1.0 %collective-permute-done.14.refs_3_ = bf16[128,512]{1,0:T(8,128)(2,1)S(1)} collective-permute-done((bf16[128,512]{1,0:T(8,128)(2,1)S(1)}, bf16[128,512]{1,0:T(8,128)(2,1)S(1)}, u32[]{:S(2)}, u32[]{:S(2)}) %collective-permute-start.14) | collective-permute-done | bytes 131104 | tf_op jit(solution)/shard_map/ppermute | solution.py:491
  50.3 1.9 %shard_map.153 = (f32[512,256]{1,0:T(8,128)}, f32[512,256]{1,0:T(8,128)}, f32[512,256]{1,0:T(8,128)}, f32[256,512]{1,0:T(8,128)}) custom-call(s32[2]{0:T(128)S(1)} %pad_add_fusion.place, bf16[128,512]{1,0:T(8,128)(2,1)S(1)} %add_convert_fusion.4.refs_0_, bf16[256,384]{1,0:T(8,128)(2,1)S(1)} %add_convert_fusion.1.refs_1_, ...), custom_call_target="tpu_custom_call" | custom-call | tf_op jit(solution)/shard_map/pallas_call | solution.py:476
  (47 shorter events, 7.1 us)
Async XLA Ops:
  0.6 14.4 %copy-start.1 = (bf16[1,128,512]{2,1,0:T(8,128)(2,1)S(1)}, bf16[1,128,512]{2,1,0:T(8,128)(2,1)}, u32[]{:S(2)}) copy-start(bf16[1,128,512]{2,1,0:T(8,128)(2,1)} %param.10) | copy-start | bytes 393220
  0.6 14.1 %collective-permute-start = (bf16[128,512]{1,0:T(8,128)(2,1)}, bf16[128,512]{1,0:T(8,128)(2,1)S(1)}, u32[]{:S(2)}, u32[]{:S(2)}) collective-permute-start(bf16[128,512]{1,0:T(8,128)(2,1)} %bitcast.17), channel_id=1, source_target_pairs={{0,8},{4,12},{8,0},{12,4},{1,9},{5,13},{9,1},{13,5},{2,10},{6,14},... | collective-permute-start | bytes 393224 | tf_op jit(solution)/shard_map/ppermute | solution.py:491
  4.7 11.3 %collective-permute-start.2 = (bf16[128,512]{1,0:T(8,128)(2,1)}, bf16[128,512]{1,0:T(8,128)(2,1)S(1)}, u32[]{:S(2)}, u32[]{:S(2)}) collective-permute-start(bf16[128,512]{1,0:T(8,128)(2,1)} %bitcast.18), channel_id=1, source_target_pairs={{0,4},{4,0},{8,12},{12,8},{1,5},{5,1},{9,13},{13,9},{2,6},{6,2},{1... | collective-permute-start | bytes 393224 | tf_op jit(solution)/shard_map/ppermute | solution.py:491
  6.3 10.7 %collective-permute-start.1 = (bf16[128,512]{1,0:T(8,128)(2,1)}, bf16[128,512]{1,0:T(8,128)(2,1)S(1)}, u32[]{:S(2)}, u32[]{:S(2)}) collective-permute-start(bf16[128,512]{1,0:T(8,128)(2,1)} %bitcast.21), channel_id=1, source_target_pairs={{0,8},{4,12},{8,0},{12,4},{1,9},{5,13},{9,1},{13,5},{2,10},{6,14},... | collective-permute-start | bytes 393224 | tf_op jit(solution)/shard_map/ppermute | solution.py:491
  6.7 21.9 %collective-permute-start.6 = (bf16[128,512]{1,0:T(8,128)(2,1)}, bf16[128,512]{1,0:T(8,128)(2,1)S(1)}, u32[]{:S(2)}, u32[]{:S(2)}) collective-permute-start(bf16[128,512]{1,0:T(8,128)(2,1)} %bitcast.22), channel_id=1, source_target_pairs={{0,4},{4,0},{8,12},{12,8},{1,5},{5,1},{9,13},{13,9},{2,6},{6,2},{1... | collective-permute-start | bytes 393224 | tf_op jit(solution)/shard_map/ppermute | solution.py:491
  8.5 10.6 %collective-permute-start.4 = (bf16[16,512]{1,0:T(8,128)(2,1)S(1)}, bf16[16,512]{1,0:T(8,128)(2,1)S(1)}, u32[]{:S(2)}, u32[]{:S(2)}) collective-permute-start(bf16[16,512]{1,0:T(8,128)(2,1)S(1)} %bitcast_dynamic-update-slice_fusion), channel_id=1, source_target_pairs={{0,4},{4,0},{8,12},{12,8},{1,5},{5,1},{9,13},{13,9},{2,6},{6,2},{1... | collective-permute-start | bytes 49160 | tf_op jit(solution)/shard_map/ppermute | solution.py:491
  15.1 13.5 %copy-start = (bf16[256,512]{1,0:T(8,128)(2,1)S(1)}, bf16[256,512]{1,0:T(8,128)(2,1)}, u32[]{:S(2)}) copy-start(bf16[256,512]{1,0:T(8,128)(2,1)} %out_w.3) | copy-start | bytes 786436
  15.1 13.5 %copy-start.2 = (bf16[1,128,512]{2,1,0:T(8,128)(2,1)S(1)}, bf16[1,128,512]{2,1,0:T(8,128)(2,1)}, u32[]{:S(2)}) copy-start(bf16[1,128,512]{2,1,0:T(8,128)(2,1)} %param.11) | copy-start | bytes 393220
  17.0 11.5 %collective-permute-start.7 = (bf16[128,512]{1,0:T(8,128)(2,1)S(1)}, bf16[128,512]{1,0:T(8,128)(2,1)S(1)}, u32[]{:S(2)}, u32[]{:S(2)}) collective-permute-start(bf16[128,512]{1,0:T(8,128)(2,1)S(1)} %collective-permute-done.1.far), channel_id=1, source_target_pairs={{0,4},{4,0},{8,12},{12,8},{1,5},{5,1},{9,13},{13,9},{2,6},{6,2},{1... | collective-permute-start | bytes 393224 | tf_op jit(solution)/shard_map/ppermute | solution.py:491
  17.7 6.9 %collective-permute-start.3 = (bf16[128,512]{1,0:T(8,128)(2,1)S(1)}, bf16[128,512]{1,0:T(8,128)(2,1)S(1)}, u32[]{:S(2)}, u32[]{:S(2)}) collective-permute-start(bf16[128,512]{1,0:T(8,128)(2,1)S(1)} %collective-permute-done.chunk), channel_id=1, source_target_pairs={{0,4},{4,0},{8,12},{12,8},{1,5},{5,1},{9,13},{13,9},{2,6},{6,2},{1... | collective-permute-start | bytes 393224 | tf_op jit(solution)/shard_map/ppermute | solution.py:491
  19.0 4.8 %collective-permute-start.5 = (bf16[16,512]{1,0:T(8,128)(2,1)S(1)}, bf16[16,512]{1,0:T(8,128)(2,1)S(1)}, u32[]{:S(2)}, u32[]{:S(2)}) collective-permute-start(bf16[16,512]{1,0:T(8,128)(2,1)S(1)} %fusion.2), channel_id=1, source_target_pairs={{0,8},{4,12},{8,0},{12,4},{1,9},{5,13},{9,1},{13,5},{2,10},{6,14},... | collective-permute-start | bytes 49160 | tf_op jit(solution)/shard_map/ppermute | solution.py:491
  29.6 3.1 %collective-permute-start.8 = (bf16[128,512]{1,0:T(8,128)(2,1)S(1)}, bf16[128,512]{1,0:T(8,128)(2,1)S(1)}, u32[]{:S(2)}, u32[]{:S(2)}) collective-permute-start(bf16[128,512]{1,0:T(8,128)(2,1)S(1)} %get-tuple-element.69), channel_id=1, source_target_pairs={{0,1},{1,0},{2,3},{3,2},{4,5},{5,4},{6,7},{7,6},{8,9},{9,8},{10,11... | collective-permute-start | bytes 393224 | tf_op jit(solution)/shard_map/ppermute | solution.py:491
  32.1 4.8 %collective-permute-start.11 = (bf16[256,384]{1,0:T(8,128)(2,1)S(1)}, bf16[256,384]{1,0:T(8,128)(2,1)S(1)}, u32[]{:S(2)}, u32[]{:S(2)}) collective-permute-start(bf16[256,384]{1,0:T(8,128)(2,1)S(1)} %get-tuple-element.81), channel_id=1, source_target_pairs={{0,1},{1,0},{2,3},{3,2},{4,5},{5,4},{6,7},{7,6},{8,9},{9,8},{10,11... | collective-permute-start | bytes 589832 | tf_op jit(solution)/shard_map/ppermute | solution.py:491
  32.7 8.1 %collective-permute-start.10 = (bf16[128,512]{1,0:T(8,128)(2,1)S(1)}, bf16[128,512]{1,0:T(8,128)(2,1)S(1)}, u32[]{:S(2)}, u32[]{:S(2)}) collective-permute-start(bf16[128,512]{1,0:T(8,128)(2,1)S(1)} %add_convert_fusion.5), channel_id=1, source_target_pairs={{0,2},{1,3},{2,0},{3,1},{4,6},{5,7},{6,4},{7,5},{8,10},{9,11},{10,... | collective-permute-start | bytes 393224 | tf_op jit(solution)/shard_map/ppermute | solution.py:491
  36.8 1.5 %collective-permute-start.9 = (bf16[256,384]{1,0:T(8,128)(2,1)S(1)}, bf16[256,384]{1,0:T(8,128)(2,1)S(1)}, u32[]{:S(2)}, u32[]{:S(2)}) collective-permute-start(bf16[256,384]{1,0:T(8,128)(2,1)S(1)} %get-tuple-element.73), channel_id=1, source_target_pairs={{0,1},{1,0},{2,3},{3,2},{4,5},{5,4},{6,7},{7,6},{8,9},{9,8},{10,11... | collective-permute-start | bytes 589832 | tf_op jit(solution)/shard_map/ppermute | solution.py:491
  36.9 7.8 %collective-permute-start.12 = (bf16[256,384]{1,0:T(8,128)(2,1)S(1)}, bf16[256,384]{1,0:T(8,128)(2,1)S(1)}, u32[]{:S(2)}, u32[]{:S(2)}) collective-permute-start(bf16[256,384]{1,0:T(8,128)(2,1)S(1)} %add_convert_fusion.2), channel_id=1, source_target_pairs={{0,2},{1,3},{2,0},{3,1},{4,6},{5,7},{6,4},{7,5},{8,10},{9,11},{10,... | collective-permute-start | bytes 589832 | tf_op jit(solution)/shard_map/ppermute | solution.py:491
  38.4 10.2 %collective-permute-start.13 = (bf16[256,384]{1,0:T(8,128)(2,1)S(1)}, bf16[256,384]{1,0:T(8,128)(2,1)S(1)}, u32[]{:S(2)}, u32[]{:S(2)}) collective-permute-start(bf16[256,384]{1,0:T(8,128)(2,1)S(1)} %add_convert_fusion.3), channel_id=1, source_target_pairs={{0,2},{1,3},{2,0},{3,1},{4,6},{5,7},{6,4},{7,5},{8,10},{9,11},{10,... | collective-permute-start | bytes 589832 | tf_op jit(solution)/shard_map/ppermute | solution.py:491
  44.8 5.5 %collective-permute-start.15 = (bf16[256,384]{1,0:T(8,128)(2,1)S(1)}, bf16[256,384]{1,0:T(8,128)(2,1)S(1)}, u32[]{:S(2)}, u32[]{:S(2)}) collective-permute-start(bf16[256,384]{1,0:T(8,128)(2,1)S(1)} %add_convert_fusion.1.refs_1_), channel_id=1, source_target_pairs={{0,1},{1,0},{2,3},{3,2},{4,5},{5,4},{6,7},{7,6},{8,9},{9,8},{10,11... | collective-permute-start | bytes 589832 | tf_op jit(solution)/shard_map/ppermute | solution.py:491
  48.6 1.7 %collective-permute-start.16 = (bf16[256,384]{1,0:T(8,128)(2,1)S(1)}, bf16[256,384]{1,0:T(8,128)(2,1)S(1)}, u32[]{:S(2)}, u32[]{:S(2)}) collective-permute-start(bf16[256,384]{1,0:T(8,128)(2,1)S(1)} %add_convert_fusion.refs_2_), channel_id=1, source_target_pairs={{0,1},{1,0},{2,3},{3,2},{4,5},{5,4},{6,7},{7,6},{8,9},{9,8},{10,11... | collective-permute-start | bytes 589832 | tf_op jit(solution)/shard_map/ppermute | solution.py:491
  48.7 1.6 %collective-permute-start.14 = (bf16[128,512]{1,0:T(8,128)(2,1)S(1)}, bf16[128,512]{1,0:T(8,128)(2,1)S(1)}, u32[]{:S(2)}, u32[]{:S(2)}) collective-permute-start(bf16[128,512]{1,0:T(8,128)(2,1)S(1)} %add_convert_fusion.4.refs_0_), channel_id=1, source_target_pairs={{0,1},{1,0},{2,3},{3,2},{4,5},{5,4},{6,7},{7,6},{8,9},{9,8},{10,11... | collective-permute-start | bytes 393224 | tf_op jit(solution)/shard_map/ppermute | solution.py:491

commit v3 on v2

--- a/solution.py
+++ b/solution.py
@@ -201,7 +201,7 @@
 LANES = 128
 SLOTS = 16
 LEVEL_PARTS = 3
-VMEM_LIMIT = 48 * 1024 * 1024
+VMEM_LIMIT = 24 * 1024 * 1024
 
 
 def transposed_product(left, right):
@@ -249,7 +249,7 @@
     slots = lax.broadcasted_iota(jnp.int32, (SLOTS, total), 0)
     level = jnp.zeros((SLOTS, total), jnp.int32)
     for entry in range(1, levels):
-        level += (places >= scalars[HEADS * DIST + entry]).astype(jnp.int32)
+        level += (places >= scalars[HEADS, entry]).astype(jnp.int32)
     features = jnp.concatenate(
         [
             (level == slots).astype(jnp.float32),
@@ -265,7 +265,7 @@
     for head in range(HEADS):
         table = jnp.full((SLOTS, LANES), NEG, jnp.float32)
         for step in range(1, min(levels, DIST)):
-            table = jnp.where(distance == step, scalars[head * DIST + step], table)
+            table = jnp.where(distance == step, scalars[head, step], table)
         high = table.astype(jnp.bfloat16).astype(jnp.float32)
         middle = (table - high).astype(jnp.bfloat16).astype(jnp.float32)
         low = table - high - middle
@@ -284,42 +284,51 @@
 
 
 def project(chunk, weights, unit_t, projected):
-    unit = normalize(chunk[...])[2]
+    unit = normalize(chunk[: projected.shape[0], :])[2]
     unit_t[...] = unit.T.astype(jnp.bfloat16)
-    projected[...] = plain_product(unit.astype(jnp.bfloat16), weights[...]).astype(jnp.bfloat16)
-
-
-def first_kernel(
-    levels, scalars, own, in_weights, features, table, column_features, unit_t, projected
-):
+    unit = unit.astype(jnp.bfloat16)
+    width = projected.shape[1] // 3
+    for i, weight in enumerate(weights):
+        projected[:, i * width : (i + 1) * width] = plain_product(unit, weight[...]).astype(
+            jnp.bfloat16
+        )
+
+
+def tables_kernel(levels, scalars, features, table, column_features):
     rows, level_bias, columns = level_tables_whole(scalars, levels, features.shape[1])
     features[...] = rows
     table[...] = level_bias
     column_features[...] = columns
-    project(own, in_weights, unit_t, projected)
-
-
-def project_kernel(chunk, in_weights, unit_t, projected):
-    project(chunk, in_weights, unit_t, projected)
+
+
+def project_kernel(chunk, query_w, key_w, value_w, unit_t, projected):
+    project(chunk, (query_w, key_w, value_w), unit_t, projected)
 
 
 def forward_kernel(
-    place, scalars, own_t, own, near_t, near, far_t, far, last_states, in_weights,
-    hidden, features, table, column_features,
+    place, scalars, own_states, own_t, own, near_states, near_t, near,
+    far_states, far_t, far, last_states, query_w, key_w, value_w, features, table, column_features,
     normed_t, projected, probs, mixed, mixed_t,
     row_table, key_table, last_t, last,
 ):
     total, width = mixed.shape
     rows = own.shape[0]
     scale = HEAD ** (-0.5)
-    project(last_states, in_weights, last_t, last)
+    project(last_states, (query_w, key_w, value_w), last_t, last)
     chunks = ((own_t, own), (near_t, near), (far_t, far), (last_t, last))
     for index, (unit_t, chunk) in enumerate(chunks):
         at = pl.ds(pl.multiple_of((place[0] ^ index) * rows, rows), rows)
         normed_t[:, at] = unit_t[...]
         projected[at, :] = chunk[...]
+    slots = lax.broadcasted_iota(jnp.int32, (SLOTS, HEADS * LANES), 0)
+    hidden = jnp.zeros((SLOTS, HEADS * LANES), jnp.float32)
+    for index, part in enumerate((own_states, near_states, far_states, last_states)):
+        tile = part[rows:, :].astype(jnp.float32)
+        for block in range(rows // BLOCK):
+            at = (place[0] ^ index) * (rows // BLOCK) + block
+            hidden = jnp.where(slots == at, tile[block : block + 1, :], hidden)
     row_table[...] = transposed_product(
-        features[...], jnp.concatenate([table[...], hidden[...]], axis=0)
+        features[...], jnp.concatenate([table[...], hidden.astype(jnp.bfloat16)], axis=0)
     ).astype(jnp.bfloat16)
     for pair in range(HEADS // 2):
         key_table[pair, :, :LANES] = projected[:, width + pair * LANES : width + (pair + 1) * LANES]
@@ -332,7 +341,7 @@
         lanes = slice(pair * LANES, (pair + 1) * LANES)
         values = slice(2 * width + pair * LANES, 2 * width + (pair + 1) * LANES)
         self_bias = jnp.where(
-            first_half, scalars[2 * pair * DIST], scalars[(2 * pair + 1) * DIST]
+            first_half, scalars[2 * pair, 0], scalars[2 * pair + 1, 0]
         )
         for tile in range(total // LANES):
             low, high = tile * LANES, (tile + 1) * LANES
@@ -436,18 +445,18 @@
     d_own[...] = grads[pl.ds(pl.multiple_of(place[0] * rows, rows), rows), :]
 
 
-def rows_kernel(place, own, grads_in, mixed, in_weights, out_w, *rest):
+def rows_kernel(place, own, grads_in, mixed, query_w, key_w, value_w, out_w, *rest):
     *d_own, updated, gradient = rest
-    rows = own.shape[0]
+    rows = updated.shape[0]
     width = mixed.shape[1]
-    states, inverse, unit = normalize(own[...])
+    states, inverse, unit = normalize(own[:rows, :])
     here = pl.ds(pl.multiple_of(place[0] * rows, rows), rows)
     updated[...] = (states + plain_product(mixed[here, :], out_w[...])).astype(jnp.bfloat16)
-    inner = jnp.zeros(own.shape, jnp.float32)
+    inner = jnp.zeros(updated.shape, jnp.float32)
     for pair, piece in enumerate(d_own):
-        for i in range(3):
-            lanes = slice(i * width + pair * LANES, i * width + (pair + 1) * LANES)
-            inner += pair_product(piece[:, i * LANES : (i + 1) * LANES], in_weights[:, lanes])
+        lanes = slice(pair * LANES, (pair + 1) * LANES)
+        for i, weight in enumerate((query_w, key_w, value_w)):
+            inner += pair_product(piece[:, i * LANES : (i + 1) * LANES], weight[:, lanes])
     gradient[...] = (
         grads_in[...].astype(jnp.float32)
         + inverse * (inner - unit * jnp.mean(inner * unit, axis=1, keepdims=True))
@@ -521,47 +530,42 @@
     half = jnp.bfloat16
     wide = jnp.float32
 
-    far = swap(states, "node", 2)
-    near = swap(states, "node", 1)
-
     local_blocks = blocks.shape[0]
-    slots = jnp.arange(blocks.shape[1], dtype=jnp.int32)
-    live = slots[None, :] < counts[:, None]
-    kinds = jnp.arange(SLOTS, dtype=jnp.int32)
-    listed = jnp.any((blocks[:, :, None] == kinds[None, None, :]) & live[:, :, None], axis=1)
-    hidden = jnp.where(listed, 0.0, NEG).astype(jnp.bfloat16)
-    hidden = jnp.pad(
-        hidden, ((0, 0), (LEVEL_PARTS * SLOTS, LANES - (LEVEL_PARTS + 1) * SLOTS))
-    )
-    hidden = lax.dynamic_update_slice(
-        jnp.zeros((SLOTS, HEADS * LANES), jnp.bfloat16),
-        jnp.tile(hidden, (1, HEADS)),
-        (place[0] * local_blocks, jnp.int32(0)),
-    )
-    hidden = hidden + swap(hidden, "node", 1)
-    hidden = hidden + swap(hidden, "node", 2)
-
+    shape = (local_blocks, blocks.shape[1], HEADS * LANES)
+    kinds = (lax.broadcasted_iota(jnp.int32, shape, 2) & (LANES - 1)) - LEVEL_PARTS * SLOTS
+    slots = lax.broadcasted_iota(jnp.int32, shape, 1)
+    match = (blocks[:, :, None] == kinds) & (slots < counts[:, None, None])
+    match |= (kinds < 0) | (kinds >= SLOTS)
+    hidden = (1.0 - jnp.max(match.astype(wide), axis=1)) * NEG
+    own = jnp.concatenate(
+        [states, jnp.pad(hidden.astype(half), ((0, SLOTS - local_blocks), (0, 0)))], axis=0
+    )
+    far = swap(own, "node", 2)
+    near = swap(own, "node", 1)
     last = swap(far, "node", 1)
-    grads_far = swap(grads_in, "node", 2)
-    grads_near = swap(grads_in, "node", 1)
-    scalars = jnp.concatenate([bias_table.reshape(-1), starts.astype(wide)])
-    in_weights = jnp.concatenate([query_weight, key_weight, value_weight], axis=1)
-    loaded, far = lax.optimization_barrier((states, far))
-    features, table, columns, own_t, own_p = run(
-        functools.partial(first_kernel, starts.shape[0] - 1),
+    grads_sent, near = lax.optimization_barrier((grads_in, near))
+    grads_far = swap(grads_sent, "node", 2)
+    grads_near = swap(grads_sent, "node", 1)
+    scalars = jnp.pad(bias_table, ((0, HEADS), (0, LANES - DIST))) + jnp.pad(
+        starts.astype(wide)[None, :], ((HEADS, HEADS - 1), (0, LANES - starts.shape[0]))
+    )
+    features, table, columns = run(
+        functools.partial(tables_kernel, starts.shape[0] - 1),
         [
             ((2 * SLOTS, total), half),
             ((SLOTS, HEADS * LANES), half),
             ((total, LANES), half),
-            ((model, rows), half),
-            ((rows, 3 * width), half),
         ],
         [scalars],
-        [loaded, in_weights],
-    )
+        [],
+        cost=10,
+    )
+    weights = [query_weight, key_weight, value_weight]
+    table, *weights = lax.optimization_barrier((table, *weights))
     chunk_outs = [((model, rows), half), ((rows, 3 * width), half)]
-    near_t, near_p = run(project_kernel, chunk_outs, [], [near, in_weights])
-    far_t, far_p = run(project_kernel, chunk_outs, [], [far, in_weights])
+    own_t, own_p = run(project_kernel, chunk_outs, [], [own, *weights])
+    near_t, near_p = run(project_kernel, chunk_outs, [], [near, *weights])
+    far_t, far_p = run(project_kernel, chunk_outs, [], [far, *weights])
     grads_far, own_p, near_p, far_p = lax.optimization_barrier((grads_far, own_p, near_p, far_p))
     grads_last = swap(grads_far, "node", 1)
     normed_t, projected, probs, mixed, mixed_t = run(
@@ -575,8 +579,8 @@
         ],
         [place, scalars],
         [
-            own_t, own_p, near_t, near_p, far_t, far_p, last, in_weights,
-            hidden, features, table, columns,
+            own, own_t, own_p, near, near_t, near_p, far, far_t, far_p, last, *weights,
+            features, table, columns,
         ],
         [
             pltpu.VMEM((total, HEADS * LANES), half),
@@ -584,6 +588,7 @@
             pltpu.VMEM((model, rows), half),
             pltpu.VMEM((rows, 3 * width), half),
         ],
+        cost=5,
     )
     d_mixed, out_keep, out_send = run(
         output_kernel,
@@ -626,7 +631,7 @@
         rows_kernel,
         [((rows, model), half)] * 2,
         [place],
-        [loaded, grads_in, mixed, in_weights, out_weight, *d_own],
+        [own, grads_in, mixed, *weights, out_weight, *d_own],
     )
     first, node_state_gradient = lax.optimization_barrier((halves[0][1], node_state_gradient))
     halves[0] = (halves[0][0], first)

time: 53.2 us -> 50.8 us (0.955); the launches traced: 52.2 us -> 50.6 us
  local copies, waits for them, and re-layouts: 3.78 us -> 0.02 us
  waiting for transfers between devices: 13.3 us -> 16.6 us
  starting transfers between devices: 16.6 us -> 14.4 us
  other arithmetic: 2.52 us -> 3.41 us
    ppermute x17 -> x15, waiting for transfers between devices: 13.3 us -> 16.6 us  [swap(): lax.ppermute(array, axis, [(i, i ^ flip) for i in range(lax.axis_size(axi...]
    ppermute x17 -> x15, starting transfers between devices: 16.6 us -> 14.4 us  [swap(): lax.ppermute(array, axis, [(i, i ^ flip) for i in range(lax.axis_size(axi...]
    unnamed x9 -> x10, local copies, waits for them, and re-layouts: 1.96 us -> 0.02 us
    concatenate x1 -> x0, local copies, waits for them, and re-layouts: 0.97 us -> none  [on_device_whole(): jnp.concatenate([query_weight, key_weight, value_weight], axis=1)]
    concatenate x1, other arithmetic: 0.01 us -> 0.92 us  [on_device_whole(): jnp.concatenate([states, jnp.pad(hidden.astype(half), ((0, SLOTS - local_...]
    reduce_max x0 -> x1, other arithmetic: none -> 0.79 us  [on_device_whole(): hidden = (1.0 - jnp.max(match.astype(wide), axis=1)) * NEG]
    reduce_or x1 -> x0, other arithmetic: 0.77 us -> none  [on_device_whole(): jnp.any((blocks[:, :, None] == kinds[None, None, :]) & live[:, :, None],...]
    reshape x1 -> x0, local copies, waits for them, and re-layouts: 0.77 us -> none  [on_device_whole(): scalars = jnp.concatenate([bias_table.reshape(-1), starts.astype(wide)])]
  transfers between devices with their start and end apart: 17 -> 15, of which waited for: 7 -> 9; matrix products, arithmetic and copies ran while one was open for 12% -> 3% of each run, Pallas kernels for 23% -> 25%
where the time goes in v3:
time: 50.8 us; the launch traced here: 50.6 us
  waiting for transfers between devices  16.6 us (33%)
  Pallas kernels  15.4 us (30%)
  starting transfers between devices  14.4 us (28%)
  other arithmetic  3.41 us (7%)
  between operations  0.84 us (2%)
    ppermute x15, waiting for transfers between devices, swap(): lax.ppermute(array, axis, [(i, i ^ flip) for i in range(lax.axis_size(axi...  16.6 us
    pallas_call x10, Pallas kernels, run(): pl.pallas_call(kernel, out_shape=out_shape, in_specs=[pl.BlockSpec(memory...  15.4 us
    ppermute x15, starting transfers between devices, swap(): lax.ppermute(array, axis, [(i, i ^ flip) for i in range(lax.axis_size(axi...  14.4 us
  transfers between devices with their start and end apart: 15, of which 9 were waited for; matrix products, arithmetic and copies ran while one was open for 3% of the time, Pallas kernels for 25%

profile of v3, /device:TPU:0, one launch (start us, length us, event | category | flops | bytes accessed | tf_op | source)
XLA Modules:
  0.0 50.6 jit_solution(5503378307240396484)
XLA Ops:
  0.7 0.8 %convert_reduce_fusion = f32[2,512]{1,0:T(2,128)S(1)} fusion(s32[2]{0:T(128)} %bitcast.14, s32[512]{0:T(512)S(1)} %and_add_fusion, s32[2,8]{1,0:T(2,128)} %bitcast.13, pred[512]{0:T(512)(128)(4,1)S(1)} %compare_or_fusion), kind=kLoop, calls=%fused_computation.9 | loop fusion | flops 48128 | bytes 6728 | tf_op jit(solution)/shard_map/reduce_max | solution.py:539
  1.5 0.9 %fusion.1.chunk.own_states.own = bf16[144,512]{1,0:T(8,128)(2,1)S(1)} fusion(bf16[2,512]{1,0:T(2,128)(2,1)S(1)} %multiply_convert_fusion, bf16[128,512]{1,0:T(8,128)(2,1)} %bitcast.12), kind=kLoop, calls=%fused_computation.8 | loop fusion | flops 442368 | bytes 280576 | tf_op jit(solution)/shard_map/concatenate | solution.py:540
  2.4 3.1 %collective-permute-start = (bf16[144,512]{1,0:T(8,128)(2,1)S(1)}, bf16[144,512]{1,0:T(8,128)(2,1)S(1)}, u32[]{:S(2)}, u32[]{:S(2)}) collective-permute-start(bf16[144,512]{1,0:T(8,128)(2,1)S(1)} %fusion.1.chunk.own_states.own), channel_id=1, source_target_pairs={{0,4},{4,0},{8,12},{12,8},{1,5},{5,1},{9,13},{13,9},{2,6},{6,2},{1... | collective-permute-start | bytes 442376 | tf_op jit(solution)/shard_map/ppermute | solution.py:500
  5.5 2.6 %collective-permute-start.2 = (bf16[144,512]{1,0:T(8,128)(2,1)S(1)}, bf16[144,512]{1,0:T(8,128)(2,1)S(1)}, u32[]{:S(2)}, u32[]{:S(2)}) collective-permute-start(bf16[144,512]{1,0:T(8,128)(2,1)S(1)} %fusion.1.chunk.own_states.own), channel_id=1, source_target_pairs={{0,8},{4,12},{8,0},{12,4},{1,9},{5,13},{9,1},{13,5},{2,10},{6,14},... | collective-permute-start | bytes 442376 | tf_op jit(solution)/shard_map/ppermute | solution.py:500
  9.4 2.5 %collective-permute-done.chunk.near_states = bf16[144,512]{1,0:T(8,128)(2,1)S(1)} collective-permute-done((bf16[144,512]{1,0:T(8,128)(2,1)S(1)}, bf16[144,512]{1,0:T(8,128)(2,1)S(1)}, u32[]{:S(2)}, u32[]{:S(2)}) %collective-permute-start) | collective-permute-done | bytes 147488 | tf_op jit(solution)/shard_map/ppermute | solution.py:500
  11.9 1.4 %collective-permute-start.1 = (bf16[128,512]{1,0:T(8,128)(2,1)}, bf16[128,512]{1,0:T(8,128)(2,1)S(1)}, u32[]{:S(2)}, u32[]{:S(2)}) collective-permute-start(bf16[128,512]{1,0:T(8,128)(2,1)} %bitcast.8), channel_id=1, source_target_pairs={{0,8},{4,12},{8,0},{12,4},{1,9},{5,13},{9,1},{13,5},{2,10},{6,14},... | collective-permute-start | bytes 393224 | tf_op jit(solution)/shard_map/ppermute | solution.py:500
  13.3 1.7 %collective-permute-done.2.chunk.far_states = bf16[144,512]{1,0:T(8,128)(2,1)S(1)} collective-permute-done((bf16[144,512]{1,0:T(8,128)(2,1)S(1)}, bf16[144,512]{1,0:T(8,128)(2,1)S(1)}, u32[]{:S(2)}, u32[]{:S(2)}) %collective-permute-start.2) | collective-permute-done | bytes 147488 | tf_op jit(solution)/shard_map/ppermute | solution.py:500
  15.0 2.2 %collective-permute-start.3 = (bf16[144,512]{1,0:T(8,128)(2,1)S(1)}, bf16[144,512]{1,0:T(8,128)(2,1)S(1)}, u32[]{:S(2)}, u32[]{:S(2)}) collective-permute-start(bf16[144,512]{1,0:T(8,128)(2,1)S(1)} %collective-permute-done.2.chunk.far_states), channel_id=1, source_target_pairs={{0,4},{4,0},{8,12},{12,8},{1,5},{5,1},{9,13},{13,9},{2,6},{6,2},{1... | collective-permute-start | bytes 442376 | tf_op jit(solution)/shard_map/ppermute | solution.py:500
  17.2 0.8 %shard_map.145 = (bf16[32,512]{1,0:T(8,128)(2,1)S(1)}, bf16[16,512]{1,0:T(8,128)(2,1)S(1)}, bf16[512,128]{1,0:T(8,128)(2,1)S(1)}) custom-call(f32[8,128]{1,0:T(8,128)S(1)} %pad_add_fusion.scalars), custom_call_target="tpu_custom_call" | custom-call | flops 10000000000 | tf_op jit(solution)/shard_map/pallas_call | solution.py:485
  19.2 1.4 %collective-permute-done.1.far = bf16[128,512]{1,0:T(8,128)(2,1)S(1)} collective-permute-done((bf16[128,512]{1,0:T(8,128)(2,1)}, bf16[128,512]{1,0:T(8,128)(2,1)S(1)}, u32[]{:S(2)}, u32[]{:S(2)}) %collective-permute-start.1) | collective-permute-done | bytes 131104 | tf_op jit(solution)/shard_map/ppermute | solution.py:500
  20.6 0.7 %collective-permute-start.5 = (bf16[128,512]{1,0:T(8,128)(2,1)S(1)}, bf16[128,512]{1,0:T(8,128)(2,1)S(1)}, u32[]{:S(2)}, u32[]{:S(2)}) collective-permute-start(bf16[128,512]{1,0:T(8,128)(2,1)S(1)} %collective-permute-done.1.far), channel_id=1, source_target_pairs={{0,4},{4,0},{8,12},{12,8},{1,5},{5,1},{9,13},{13,9},{2,6},{6,2},{1... | collective-permute-start | bytes 393224 | tf_op jit(solution)/shard_map/ppermute | solution.py:500
  21.3 1.5 %collective-permute-done.3.last_states = bf16[144,512]{1,0:T(8,128)(2,1)S(1)} collective-permute-done((bf16[144,512]{1,0:T(8,128)(2,1)S(1)}, bf16[144,512]{1,0:T(8,128)(2,1)S(1)}, u32[]{:S(2)}, u32[]{:S(2)}) %collective-permute-start.3) | collective-permute-done | bytes 147488 | tf_op jit(solution)/shard_map/ppermute | solution.py:500
  22.8 4.0 %shard_map.149 = (bf16[512,512]{1,0:T(8,128)(2,1)S(1)}, bf16[512,768]{1,0:T(8,128)(2,1)S(1)}, bf16[2,1024,512]{2,1,0:T(8,128)(2,1)S(1)}, bf16[512,256]{1,0:T(8,128)(2,1)S(1)}, bf16[256,512]{1,0:T(8,128)(2,1)S(1)}) custom-call(s32[2]{0:T(128)S(1)} %pad_add_fusion.1.place, f32[8,128]{1,0:T(8,128)S(1)} %pad_add_fusion.scalars, ...), custom_call_target="tpu_custom_call" | custom-call | flops 5000000000 | tf_op jit(solution)/shard_map/pallas_call | solution.py:485
  27.0 1.0 %shard_map.150 = (bf16[512,256]{1,0:T(8,128)(2,1)S(1)}, f32[128,512]{1,0:T(8,128)S(1)}, bf16[128,512]{1,0:T(8,128)(2,1)S(1)}) custom-call(s32[2]{0:T(128)S(1)} %pad_add_fusion.1.place, bf16[128,512]{1,0:T(8,128)(2,1)S(1)} %bitcast.10, bf16[128,512]{1,0:T(8,128)(2,1)S(1)} %collective-permute-done.4.near, bf16[128,512]{1,0:T(8,128)(2,1)S(1)} %collective-permute-done.1.far, ...), custom_call_target="tpu_custom_call" | custom-call | tf_op jit(solution)/shard_map/pallas_call | solution.py:485
  28.1 2.5 %shard_map.151 = (bf16[128,384]{1,0:T(8,128)(2,1)S(1)}, f32[256,384]{1,0:T(8,128)S(1)}, bf16[256,384]{1,0:T(8,128)(2,1)S(1)}) custom-call(s32[2]{0:T(128)S(1)} %pad_add_fusion.1.place, bf16[512,512]{1,0:T(8,128)(2,1)S(1)} %get-tuple-element.69.normed_t, bf16[512,768]{1,0:T(8,128)(2,1)S(1)} %get-tuple-element.70.projected, ...), custom_call_target="tpu_custom_call" | custom-call | tf_op jit(solution)/shard_map/pallas_call | solution.py:485
  31.2 1.6 %collective-permute-start.8 = (bf16[128,512]{1,0:T(8,128)(2,1)S(1)}, bf16[128,512]{1,0:T(8,128)(2,1)S(1)}, u32[]{:S(2)}, u32[]{:S(2)}) collective-permute-start(bf16[128,512]{1,0:T(8,128)(2,1)S(1)} %add_convert_fusion.5), channel_id=1, source_target_pairs={{0,2},{1,3},{2,0},{3,1},{4,6},{5,7},{6,4},{7,5},{8,10},{9,11},{10,... | collective-permute-start | bytes 393224 | tf_op jit(solution)/shard_map/ppermute | solution.py:500
  32.7 2.5 %shard_map.152 = (bf16[128,384]{1,0:T(8,128)(2,1)S(1)}, f32[256,384]{1,0:T(8,128)S(1)}, bf16[256,384]{1,0:T(8,128)(2,1)S(1)}) custom-call(s32[2]{0:T(128)S(1)} %pad_add_fusion.1.place, bf16[512,512]{1,0:T(8,128)(2,1)S(1)} %get-tuple-element.69.normed_t, bf16[512,768]{1,0:T(8,128)(2,1)S(1)} %get-tuple-element.70.projected, ...), custom_call_target="tpu_custom_call" | custom-call | tf_op jit(solution)/shard_map/pallas_call | solution.py:485
  35.9 0.8 %collective-permute-done.7 = bf16[256,384]{1,0:T(8,128)(2,1)S(1)} collective-permute-done((bf16[256,384]{1,0:T(8,128)(2,1)S(1)}, bf16[256,384]{1,0:T(8,128)(2,1)S(1)}, u32[]{:S(2)}, u32[]{:S(2)}) %collective-permute-start.7) | collective-permute-done | bytes 196640 | tf_op jit(solution)/shard_map/ppermute | solution.py:500
  36.8 0.8 %collective-permute-start.11 = (bf16[256,384]{1,0:T(8,128)(2,1)S(1)}, bf16[256,384]{1,0:T(8,128)(2,1)S(1)}, u32[]{:S(2)}, u32[]{:S(2)}) collective-permute-start(bf16[256,384]{1,0:T(8,128)(2,1)S(1)} %add_convert_fusion.3), channel_id=1, source_target_pairs={{0,2},{1,3},{2,0},{3,1},{4,6},{5,7},{6,4},{7,5},{8,10},{9,11},{10,... | collective-permute-start | bytes 589832 | tf_op jit(solution)/shard_map/ppermute | solution.py:500
  37.6 1.7 %shard_map.153 = (bf16[128,512]{1,0:T(8,128)(2,1)}, bf16[128,512]{1,0:T(8,128)(2,1)}) custom-call(s32[2]{0:T(128)S(1)} %pad_add_fusion.1.place, bf16[144,512]{1,0:T(8,128)(2,1)S(1)} %fusion.1.chunk.own_states.own, bf16[128,512]{1,0:T(8,128)(2,1)S(1)} %bitcast.11, bf16[512,256]{1,0:T(8,128)(2,1)S(1)} %get-tuple-element.68.mixed, ...), custom_call_target="tpu_custom_call" | custom-call | tf_op jit(solution)/shard_map/pallas_call | solution.py:485
  39.3 3.8 %collective-permute-done.10 = bf16[256,384]{1,0:T(8,128)(2,1)S(1)} collective-permute-done((bf16[256,384]{1,0:T(8,128)(2,1)S(1)}, bf16[256,384]{1,0:T(8,128)(2,1)S(1)}, u32[]{:S(2)}, u32[]{:S(2)}) %collective-permute-start.10) | collective-permute-done | bytes 196640 | tf_op jit(solution)/shard_map/ppermute | solution.py:500
  43.2 3.7 %collective-permute-done.11 = bf16[256,384]{1,0:T(8,128)(2,1)S(1)} collective-permute-done((bf16[256,384]{1,0:T(8,128)(2,1)S(1)}, bf16[256,384]{1,0:T(8,128)(2,1)S(1)}, u32[]{:S(2)}, u32[]{:S(2)}) %collective-permute-start.11) | collective-permute-done | bytes 196640 | tf_op jit(solution)/shard_map/ppermute | solution.py:500
  47.6 1.0 %collective-permute-done.12.refs_3_ = bf16[128,512]{1,0:T(8,128)(2,1)S(1)} collective-permute-done((bf16[128,512]{1,0:T(8,128)(2,1)S(1)}, bf16[128,512]{1,0:T(8,128)(2,1)S(1)}, u32[]{:S(2)}, u32[]{:S(2)}) %collective-permute-start.12) | collective-permute-done | bytes 131104 | tf_op jit(solution)/shard_map/ppermute | solution.py:500
  48.7 1.9 %shard_map.154 = (f32[512,256]{1,0:T(8,128)}, f32[512,256]{1,0:T(8,128)}, f32[512,256]{1,0:T(8,128)}, f32[256,512]{1,0:T(8,128)}) custom-call(s32[2]{0:T(128)S(1)} %pad_add_fusion.1.place, bf16[128,512]{1,0:T(8,128)(2,1)S(1)} %add_convert_fusion.4.refs_0_, bf16[256,384]{1,0:T(8,128)(2,1)S(1)} %add_convert_fusion.1.refs_1_, ...), custom_call_target="tpu_custom_call" | custom-call | tf_op jit(solution)/shard_map/pallas_call | solution.py:485
  (40 shorter events, 5.0 us)
Async XLA Ops:
  2.4 9.5 %collective-permute-start = (bf16[144,512]{1,0:T(8,128)(2,1)S(1)}, bf16[144,512]{1,0:T(8,128)(2,1)S(1)}, u32[]{:S(2)}, u32[]{:S(2)}) collective-permute-start(bf16[144,512]{1,0:T(8,128)(2,1)S(1)} %fusion.1.chunk.own_states.own), channel_id=1, source_target_pairs={{0,4},{4,0},{8,12},{12,8},{1,5},{5,1},{9,13},{13,9},{2,6},{6,2},{1... | collective-permute-start | bytes 442376 | tf_op jit(solution)/shard_map/ppermute | solution.py:500
  5.5 9.6 %collective-permute-start.2 = (bf16[144,512]{1,0:T(8,128)(2,1)S(1)}, bf16[144,512]{1,0:T(8,128)(2,1)S(1)}, u32[]{:S(2)}, u32[]{:S(2)}) collective-permute-start(bf16[144,512]{1,0:T(8,128)(2,1)S(1)} %fusion.1.chunk.own_states.own), channel_id=1, source_target_pairs={{0,8},{4,12},{8,0},{12,4},{1,9},{5,13},{9,1},{13,5},{2,10},{6,14},... | collective-permute-start | bytes 442376 | tf_op jit(solution)/shard_map/ppermute | solution.py:500
  11.9 6.2 %copy-start = (bf16[512,256]{1,0:T(8,128)(2,1)S(1)}, bf16[512,256]{1,0:T(8,128)(2,1)}, u32[]{:S(2)}) copy-start(bf16[512,256]{1,0:T(8,128)(2,1)} %query_w.4) | copy-start | bytes 786436
  11.9 6.2 %copy-start.1 = (bf16[512,256]{1,0:T(8,128)(2,1)S(1)}, bf16[512,256]{1,0:T(8,128)(2,1)}, u32[]{:S(2)}) copy-start(bf16[512,256]{1,0:T(8,128)(2,1)} %key_w.4) | copy-start | bytes 786436
  11.9 6.2 %copy-start.2 = (bf16[512,256]{1,0:T(8,128)(2,1)S(1)}, bf16[512,256]{1,0:T(8,128)(2,1)}, u32[]{:S(2)}) copy-start(bf16[512,256]{1,0:T(8,128)(2,1)} %value_w.4) | copy-start | bytes 786436
  11.9 6.6 %copy-start.4 = (bf16[1,128,512]{2,1,0:T(8,128)(2,1)S(1)}, bf16[1,128,512]{2,1,0:T(8,128)(2,1)}, u32[]{:S(2)}) copy-start(bf16[1,128,512]{2,1,0:T(8,128)(2,1)} %param.11) | copy-start | bytes 393220
  11.9 8.7 %collective-permute-start.1 = (bf16[128,512]{1,0:T(8,128)(2,1)}, bf16[128,512]{1,0:T(8,128)(2,1)S(1)}, u32[]{:S(2)}, u32[]{:S(2)}) collective-permute-start(bf16[128,512]{1,0:T(8,128)(2,1)} %bitcast.8), channel_id=1, source_target_pairs={{0,8},{4,12},{8,0},{12,4},{1,9},{5,13},{9,1},{13,5},{2,10},{6,14},... | collective-permute-start | bytes 393224 | tf_op jit(solution)/shard_map/ppermute | solution.py:500
  15.0 7.7 %collective-permute-start.3 = (bf16[144,512]{1,0:T(8,128)(2,1)S(1)}, bf16[144,512]{1,0:T(8,128)(2,1)S(1)}, u32[]{:S(2)}, u32[]{:S(2)}) collective-permute-start(bf16[144,512]{1,0:T(8,128)(2,1)S(1)} %collective-permute-done.2.chunk.far_states), channel_id=1, source_target_pairs={{0,4},{4,0},{8,12},{12,8},{1,5},{5,1},{9,13},{13,9},{2,6},{6,2},{1... | collective-permute-start | bytes 442376 | tf_op jit(solution)/shard_map/ppermute | solution.py:500
  18.5 8.3 %collective-permute-start.4 = (bf16[128,512]{1,0:T(8,128)(2,1)S(1)}, bf16[128,512]{1,0:T(8,128)(2,1)S(1)}, u32[]{:S(2)}, u32[]{:S(2)}) collective-permute-start(bf16[128,512]{1,0:T(8,128)(2,1)S(1)} %bitcast.9), channel_id=1, source_target_pairs={{0,4},{4,0},{8,12},{12,8},{1,5},{5,1},{9,13},{13,9},{2,6},{6,2},{1... | collective-permute-start | bytes 393224 | tf_op jit(solution)/shard_map/ppermute | solution.py:500
  20.6 6.4 %collective-permute-start.5 = (bf16[128,512]{1,0:T(8,128)(2,1)S(1)}, bf16[128,512]{1,0:T(8,128)(2,1)S(1)}, u32[]{:S(2)}, u32[]{:S(2)}) collective-permute-start(bf16[128,512]{1,0:T(8,128)(2,1)S(1)} %collective-permute-done.1.far), channel_id=1, source_target_pairs={{0,4},{4,0},{8,12},{12,8},{1,5},{5,1},{9,13},{13,9},{2,6},{6,2},{1... | collective-permute-start | bytes 393224 | tf_op jit(solution)/shard_map/ppermute | solution.py:500
  22.8 4.2 %copy-start.3 = (bf16[256,512]{1,0:T(8,128)(2,1)S(1)}, bf16[256,512]{1,0:T(8,128)(2,1)}, u32[]{:S(2)}) copy-start(bf16[256,512]{1,0:T(8,128)(2,1)} %out_w.3) | copy-start | bytes 786436
  28.0 3.1 %collective-permute-start.6 = (bf16[128,512]{1,0:T(8,128)(2,1)S(1)}, bf16[128,512]{1,0:T(8,128)(2,1)S(1)}, u32[]{:S(2)}, u32[]{:S(2)}) collective-permute-start(bf16[128,512]{1,0:T(8,128)(2,1)S(1)} %get-tuple-element.77), channel_id=1, source_target_pairs={{0,1},{1,0},{2,3},{3,2},{4,5},{5,4},{6,7},{7,6},{8,9},{9,8},{10,11... | collective-permute-start | bytes 393224 | tf_op jit(solution)/shard_map/ppermute | solution.py:500
  30.6 4.7 %collective-permute-start.9 = (bf16[256,384]{1,0:T(8,128)(2,1)S(1)}, bf16[256,384]{1,0:T(8,128)(2,1)S(1)}, u32[]{:S(2)}, u32[]{:S(2)}) collective-permute-start(bf16[256,384]{1,0:T(8,128)(2,1)S(1)} %get-tuple-element.89), channel_id=1, source_target_pairs={{0,1},{1,0},{2,3},{3,2},{4,5},{5,4},{6,7},{7,6},{8,9},{9,8},{10,11... | collective-permute-start | bytes 589832 | tf_op jit(solution)/shard_map/ppermute | solution.py:500
  31.2 8.1 %collective-permute-start.8 = (bf16[128,512]{1,0:T(8,128)(2,1)S(1)}, bf16[128,512]{1,0:T(8,128)(2,1)S(1)}, u32[]{:S(2)}, u32[]{:S(2)}) collective-permute-start(bf16[128,512]{1,0:T(8,128)(2,1)S(1)} %add_convert_fusion.5), channel_id=1, source_target_pairs={{0,2},{1,3},{2,0},{3,1},{4,6},{5,7},{6,4},{7,5},{8,10},{9,11},{10,... | collective-permute-start | bytes 393224 | tf_op jit(solution)/shard_map/ppermute | solution.py:500
  35.2 1.5 %collective-permute-start.7 = (bf16[256,384]{1,0:T(8,128)(2,1)S(1)}, bf16[256,384]{1,0:T(8,128)(2,1)S(1)}, u32[]{:S(2)}, u32[]{:S(2)}) collective-permute-start(bf16[256,384]{1,0:T(8,128)(2,1)S(1)} %get-tuple-element.81), channel_id=1, source_target_pairs={{0,1},{1,0},{2,3},{3,2},{4,5},{5,4},{6,7},{7,6},{8,9},{9,8},{10,11... | collective-permute-start | bytes 589832 | tf_op jit(solution)/shard_map/ppermute | solution.py:500
  35.3 7.8 %collective-permute-start.10 = (bf16[256,384]{1,0:T(8,128)(2,1)S(1)}, bf16[256,384]{1,0:T(8,128)(2,1)S(1)}, u32[]{:S(2)}, u32[]{:S(2)}) collective-permute-start(bf16[256,384]{1,0:T(8,128)(2,1)S(1)} %add_convert_fusion.2), channel_id=1, source_target_pairs={{0,2},{1,3},{2,0},{3,1},{4,6},{5,7},{6,4},{7,5},{8,10},{9,11},{10,... | collective-permute-start | bytes 589832 | tf_op jit(solution)/shard_map/ppermute | solution.py:500
  36.8 10.1 %collective-permute-start.11 = (bf16[256,384]{1,0:T(8,128)(2,1)S(1)}, bf16[256,384]{1,0:T(8,128)(2,1)S(1)}, u32[]{:S(2)}, u32[]{:S(2)}) collective-permute-start(bf16[256,384]{1,0:T(8,128)(2,1)S(1)} %add_convert_fusion.3), channel_id=1, source_target_pairs={{0,2},{1,3},{2,0},{3,1},{4,6},{5,7},{6,4},{7,5},{8,10},{9,11},{10,... | collective-permute-start | bytes 589832 | tf_op jit(solution)/shard_map/ppermute | solution.py:500
  43.2 5.5 %collective-permute-start.13 = (bf16[256,384]{1,0:T(8,128)(2,1)S(1)}, bf16[256,384]{1,0:T(8,128)(2,1)S(1)}, u32[]{:S(2)}, u32[]{:S(2)}) collective-permute-start(bf16[256,384]{1,0:T(8,128)(2,1)S(1)} %add_convert_fusion.1.refs_1_), channel_id=1, source_target_pairs={{0,1},{1,0},{2,3},{3,2},{4,5},{5,4},{6,7},{7,6},{8,9},{9,8},{10,11... | collective-permute-start | bytes 589832 | tf_op jit(solution)/shard_map/ppermute | solution.py:500
  47.0 1.7 %collective-permute-start.14 = (bf16[256,384]{1,0:T(8,128)(2,1)S(1)}, bf16[256,384]{1,0:T(8,128)(2,1)S(1)}, u32[]{:S(2)}, u32[]{:S(2)}) collective-permute-start(bf16[256,384]{1,0:T(8,128)(2,1)S(1)} %add_convert_fusion.refs_2_), channel_id=1, source_target_pairs={{0,1},{1,0},{2,3},{3,2},{4,5},{5,4},{6,7},{7,6},{8,9},{9,8},{10,11... | collective-permute-start | bytes 589832 | tf_op jit(solution)/shard_map/ppermute | solution.py:500
  47.1 1.6 %collective-permute-start.12 = (bf16[128,512]{1,0:T(8,128)(2,1)S(1)}, bf16[128,512]{1,0:T(8,128)(2,1)S(1)}, u32[]{:S(2)}, u32[]{:S(2)}) collective-permute-start(bf16[128,512]{1,0:T(8,128)(2,1)S(1)} %add_convert_fusion.4.refs_0_), channel_id=1, source_target_pairs={{0,1},{1,0},{2,3},{3,2},{4,5},{5,4},{6,7},{7,6},{8,9},{9,8},{10,11... | collective-permute-start | bytes 393224 | tf_op jit(solution)/shard_map/ppermute | solution.py:500

commit v4 on v3

--- a/solution.py
+++ b/solution.py
@@ -393,15 +393,16 @@
     )
 
 
-def output_kernel(
-    place, own, near, far, last, mixed_t, out_w, d_mixed, keep, send, gathered, full
-):
+def mix_kernel(place, own, near, far, last, out_w, gathered, d_mixed):
     rows = own.shape[0]
     for index, chunk in enumerate((own, near, far, last)):
         at = pl.ds(pl.multiple_of((place[0] ^ index) * rows, rows), rows)
         gathered[at, :] = chunk[...]
+    d_mixed[...] = pair_product(gathered[...], out_w[...]).astype(jnp.bfloat16)
+
+
+def output_kernel(place, gathered, mixed_t, keep, send, full):
     store_halves(place, plain_product(mixed_t[...], gathered[...]), keep, send, full)
-    d_mixed[...] = pair_product(gathered[...], out_w[...]).astype(jnp.bfloat16)
 
 
 def backward_kernel(
@@ -590,24 +591,27 @@
         ],
         cost=5,
     )
-    d_mixed, out_keep, out_send = run(
-        output_kernel,
-        [
-            ((total, width), half),
-            ((width // 2, model), wide),
-            ((width // 2, model), half),
-        ],
+    gathered, d_mixed = run(
+        mix_kernel,
+        [((total, model), half), ((total, width), half)],
         [place],
-        [grads_in, grads_near, grads_far, grads_last, mixed_t, out_weight],
-        [pltpu.VMEM((total, model), half), pltpu.VMEM((width, model), wide)],
-    )
-    local, across = sum_over_chips(out_keep, out_send)
-    halves = [(local, across)]
+        [grads_in, grads_near, grads_far, grads_last, out_weight],
+    )
+    halves = []
     d_own = []
     for pair in range(HEADS // 2):
-        if pair:
-            d_mixed, local = lax.optimization_barrier((d_mixed, local))
-            halves[0] = (local, halves[0][1])
+        if pair == 1:
+            local, across = halves[0]
+            gathered, keep = lax.optimization_barrier((gathered, keep))
+            out_keep, out_send = run(
+                output_kernel,
+                [((width // 2, model), wide), ((width // 2, model), half)],
+                [place],
+                [gathered, mixed_t],
+                [pltpu.VMEM((width, model), wide)],
+            )
+            d_mixed, local, out_send = lax.optimization_barrier((d_mixed, local, out_send))
+            halves[0] = (local, across)
         own_grads, keep, send = run(
             functools.partial(backward_kernel, pair),
             [
@@ -626,7 +630,8 @@
         )
         d_own.append(own_grads)
         halves.append(sum_over_chips(keep, send))
-    d_own[-1], _ = lax.optimization_barrier((d_own[-1], halves[-1][0]))
+    halves.append(sum_over_chips(out_keep, out_send))
+    d_own[-1], _ = lax.optimization_barrier((d_own[-1], halves[1][0]))
     updated, node_state_gradient = run(
         rows_kernel,
         [((rows, model), half)] * 2,
@@ -643,7 +648,7 @@
         join_kernel,
         [((model, width), wide)] * 3 + [((width, model), wide)],
         [place],
-        [*mine, *other],
+        [mine[-1], *mine[:-1], other[-1], *other[:-1]],
     )
     return (
         updated[None],

time: 50.8 us -> 50.3 us (level)
  waiting for transfers between devices: 16.6 us -> 15.6 us
  Pallas kernels: 15.4 us -> 16.2 us
    ppermute x15, waiting for transfers between devices: 16.6 us -> 15.6 us  [swap(): lax.ppermute(array, axis, [(i, i ^ flip) for i in range(lax.axis_size(axi...]
    pallas_call x10 -> x11, Pallas kernels: 15.4 us -> 16.2 us  [run(): pl.pallas_call(kernel, out_shape=out_shape, in_specs=[pl.BlockSpec(memory...]
  transfers between devices with their start and end apart: 15 -> 15, of which waited for: 9 -> 9; matrix products, arithmetic and copies ran while one was open for 3% -> 3% of each run, Pallas kernels for 25% -> 22%
where the time goes in v4:
time: 50.3 us; the launch traced here: 50.1 us
  Pallas kernels  16.2 us (32%)
  waiting for transfers between devices  15.6 us (31%)
  starting transfers between devices  14.1 us (28%)
  other arithmetic  3.41 us (7%)
  between operations  0.84 us (2%)
    pallas_call x11, Pallas kernels, run(): pl.pallas_call(kernel, out_shape=out_shape, in_specs=[pl.BlockSpec(memory...  16.2 us
    ppermute x15, waiting for transfers between devices, swap(): lax.ppermute(array, axis, [(i, i ^ flip) for i in range(lax.axis_size(axi...  15.6 us
    ppermute x15, starting transfers between devices, swap(): lax.ppermute(array, axis, [(i, i ^ flip) for i in range(lax.axis_size(axi...  14.1 us
  transfers between devices with their start and end apart: 15, of which 9 were waited for; matrix products, arithmetic and copies ran while one was open for 3% of the time, Pallas kernels for 22%

profile of v4, /device:TPU:0, one launch (start us, length us, event | category | flops | bytes accessed | tf_op | source)
XLA Modules:
  0.0 50.1 jit_solution(1054049134258444802)
XLA Ops:
  0.7 0.8 %convert_reduce_fusion = f32[2,512]{1,0:T(2,128)S(1)} fusion(s32[2]{0:T(128)} %bitcast.14, s32[512]{0:T(512)S(1)} %and_add_fusion, s32[2,8]{1,0:T(2,128)} %bitcast.13, pred[512]{0:T(512)(128)(4,1)S(1)} %compare_or_fusion), kind=kLoop, calls=%fused_computation.9 | loop fusion | flops 48128 | bytes 6728 | tf_op jit(solution)/shard_map/reduce_max | solution.py:540
  1.5 0.9 %fusion.1.chunk.own_states.own = bf16[144,512]{1,0:T(8,128)(2,1)S(1)} fusion(bf16[2,512]{1,0:T(2,128)(2,1)S(1)} %multiply_convert_fusion, bf16[128,512]{1,0:T(8,128)(2,1)} %bitcast.12), kind=kLoop, calls=%fused_computation.8 | loop fusion | flops 442368 | bytes 280576 | tf_op jit(solution)/shard_map/concatenate | solution.py:541
  2.4 3.1 %collective-permute-start = (bf16[144,512]{1,0:T(8,128)(2,1)S(1)}, bf16[144,512]{1,0:T(8,128)(2,1)S(1)}, u32[]{:S(2)}, u32[]{:S(2)}) collective-permute-start(bf16[144,512]{1,0:T(8,128)(2,1)S(1)} %fusion.1.chunk.own_states.own), channel_id=1, source_target_pairs={{0,4},{4,0},{8,12},{12,8},{1,5},{5,1},{9,13},{13,9},{2,6},{6,2},{1... | collective-permute-start | bytes 442376 | tf_op jit(solution)/shard_map/ppermute | solution.py:501
  5.5 2.6 %collective-permute-start.2 = (bf16[144,512]{1,0:T(8,128)(2,1)S(1)}, bf16[144,512]{1,0:T(8,128)(2,1)S(1)}, u32[]{:S(2)}, u32[]{:S(2)}) collective-permute-start(bf16[144,512]{1,0:T(8,128)(2,1)S(1)} %fusion.1.chunk.own_states.own), channel_id=1, source_target_pairs={{0,8},{4,12},{8,0},{12,4},{1,9},{5,13},{9,1},{13,5},{2,10},{6,14},... | collective-permute-start | bytes 442376 | tf_op jit(solution)/shard_map/ppermute | solution.py:501
  9.4 2.5 %collective-permute-done.chunk.near_states = bf16[144,512]{1,0:T(8,128)(2,1)S(1)} collective-permute-done((bf16[144,512]{1,0:T(8,128)(2,1)S(1)}, bf16[144,512]{1,0:T(8,128)(2,1)S(1)}, u32[]{:S(2)}, u32[]{:S(2)}) %collective-permute-start) | collective-permute-done | bytes 147488 | tf_op jit(solution)/shard_map/ppermute | solution.py:501
  11.9 1.4 %collective-permute-start.1 = (bf16[128,512]{1,0:T(8,128)(2,1)}, bf16[128,512]{1,0:T(8,128)(2,1)S(1)}, u32[]{:S(2)}, u32[]{:S(2)}) collective-permute-start(bf16[128,512]{1,0:T(8,128)(2,1)} %bitcast.8), channel_id=1, source_target_pairs={{0,8},{4,12},{8,0},{12,4},{1,9},{5,13},{9,1},{13,5},{2,10},{6,14},... | collective-permute-start | bytes 393224 | tf_op jit(solution)/shard_map/ppermute | solution.py:501
  13.3 1.7 %collective-permute-done.2.chunk.far_states = bf16[144,512]{1,0:T(8,128)(2,1)S(1)} collective-permute-done((bf16[144,512]{1,0:T(8,128)(2,1)S(1)}, bf16[144,512]{1,0:T(8,128)(2,1)S(1)}, u32[]{:S(2)}, u32[]{:S(2)}) %collective-permute-start.2) | collective-permute-done | bytes 147488 | tf_op jit(solution)/shard_map/ppermute | solution.py:501
  15.0 2.2 %collective-permute-start.3 = (bf16[144,512]{1,0:T(8,128)(2,1)S(1)}, bf16[144,512]{1,0:T(8,128)(2,1)S(1)}, u32[]{:S(2)}, u32[]{:S(2)}) collective-permute-start(bf16[144,512]{1,0:T(8,128)(2,1)S(1)} %collective-permute-done.2.chunk.far_states), channel_id=1, source_target_pairs={{0,4},{4,0},{8,12},{12,8},{1,5},{5,1},{9,13},{13,9},{2,6},{6,2},{1... | collective-permute-start | bytes 442376 | tf_op jit(solution)/shard_map/ppermute | solution.py:501
  17.2 0.8 %shard_map.145 = (bf16[32,512]{1,0:T(8,128)(2,1)S(1)}, bf16[16,512]{1,0:T(8,128)(2,1)S(1)}, bf16[512,128]{1,0:T(8,128)(2,1)S(1)}) custom-call(f32[8,128]{1,0:T(8,128)S(1)} %pad_add_fusion.scalars), custom_call_target="tpu_custom_call" | custom-call | flops 10000000000 | tf_op jit(solution)/shard_map/pallas_call | solution.py:486
  19.2 1.4 %collective-permute-done.1.far = bf16[128,512]{1,0:T(8,128)(2,1)S(1)} collective-permute-done((bf16[128,512]{1,0:T(8,128)(2,1)}, bf16[128,512]{1,0:T(8,128)(2,1)S(1)}, u32[]{:S(2)}, u32[]{:S(2)}) %collective-permute-start.1) | collective-permute-done | bytes 131104 | tf_op jit(solution)/shard_map/ppermute | solution.py:501
  20.6 0.7 %collective-permute-start.5 = (bf16[128,512]{1,0:T(8,128)(2,1)S(1)}, bf16[128,512]{1,0:T(8,128)(2,1)S(1)}, u32[]{:S(2)}, u32[]{:S(2)}) collective-permute-start(bf16[128,512]{1,0:T(8,128)(2,1)S(1)} %collective-permute-done.1.far), channel_id=1, source_target_pairs={{0,4},{4,0},{8,12},{12,8},{1,5},{5,1},{9,13},{13,9},{2,6},{6,2},{1... | collective-permute-start | bytes 393224 | tf_op jit(solution)/shard_map/ppermute | solution.py:501
  21.3 1.5 %collective-permute-done.3.last_states = bf16[144,512]{1,0:T(8,128)(2,1)S(1)} collective-permute-done((bf16[144,512]{1,0:T(8,128)(2,1)S(1)}, bf16[144,512]{1,0:T(8,128)(2,1)S(1)}, u32[]{:S(2)}, u32[]{:S(2)}) %collective-permute-start.3) | collective-permute-done | bytes 147488 | tf_op jit(solution)/shard_map/ppermute | solution.py:501
  22.8 4.0 %shard_map.149 = (bf16[512,512]{1,0:T(8,128)(2,1)S(1)}, bf16[512,768]{1,0:T(8,128)(2,1)S(1)}, bf16[2,1024,512]{2,1,0:T(8,128)(2,1)S(1)}, bf16[512,256]{1,0:T(8,128)(2,1)S(1)}, bf16[256,512]{1,0:T(8,128)(2,1)S(1)}) custom-call(s32[2]{0:T(128)S(1)} %pad_add_fusion.1.place, f32[8,128]{1,0:T(8,128)S(1)} %pad_add_fusion.scalars, ...), custom_call_target="tpu_custom_call" | custom-call | flops 5000000000 | tf_op jit(solution)/shard_map/pallas_call | solution.py:486
  27.0 0.9 %shard_map.150 = (bf16[512,512]{1,0:T(8,128)(2,1)S(1)}, bf16[512,256]{1,0:T(8,128)(2,1)S(1)}) custom-call(s32[2]{0:T(128)S(1)} %pad_add_fusion.1.place, bf16[128,512]{1,0:T(8,128)(2,1)S(1)} %bitcast.10, bf16[128,512]{1,0:T(8,128)(2,1)S(1)} %collective-permute-done.4.near, bf16[128,512]{1,0:T(8,128)(2,1)S(1)} %collective-permute-done.1.far, ...), custom_call_target="tpu_custom_call" | custom-call | tf_op jit(solution)/shard_map/pallas_call | solution.py:486
  27.9 2.5 %shard_map.151 = (bf16[128,384]{1,0:T(8,128)(2,1)S(1)}, f32[256,384]{1,0:T(8,128)S(1)}, bf16[256,384]{1,0:T(8,128)(2,1)S(1)}) custom-call(s32[2]{0:T(128)S(1)} %pad_add_fusion.1.place, bf16[512,512]{1,0:T(8,128)(2,1)S(1)} %get-tuple-element.72.normed_t, bf16[512,768]{1,0:T(8,128)(2,1)S(1)} %get-tuple-element.73.projected, ...), custom_call_target="tpu_custom_call" | custom-call | tf_op jit(solution)/shard_map/pallas_call | solution.py:486
  30.4 0.9 %shard_map.152 = (f32[128,512]{1,0:T(8,128)S(1)}, bf16[128,512]{1,0:T(8,128)(2,1)S(1)}) custom-call(s32[2]{0:T(128)S(1)} %pad_add_fusion.1.place, bf16[512,512]{1,0:T(8,128)(2,1)S(1)} %get-tuple-element.81.gathered, bf16[256,512]{1,0:T(8,128)(2,1)S(1)} %get-tuple-element.82.mixed_t), custom_call_target="tpu_custom_call" | custom-call | tf_op jit(solution)/shard_map/pallas_call | solution.py:486
  32.1 1.5 %collective-permute-start.8 = (bf16[256,384]{1,0:T(8,128)(2,1)S(1)}, bf16[256,384]{1,0:T(8,128)(2,1)S(1)}, u32[]{:S(2)}, u32[]{:S(2)}) collective-permute-start(bf16[256,384]{1,0:T(8,128)(2,1)S(1)} %add_convert_fusion.3), channel_id=1, source_target_pairs={{0,2},{1,3},{2,0},{3,1},{4,6},{5,7},{6,4},{7,5},{8,10},{9,11},{10,... | collective-permute-start | bytes 589832 | tf_op jit(solution)/shard_map/ppermute | solution.py:501
  33.6 2.5 %shard_map.153 = (bf16[128,384]{1,0:T(8,128)(2,1)S(1)}, f32[256,384]{1,0:T(8,128)S(1)}, bf16[256,384]{1,0:T(8,128)(2,1)S(1)}) custom-call(s32[2]{0:T(128)S(1)} %pad_add_fusion.1.place, bf16[512,512]{1,0:T(8,128)(2,1)S(1)} %get-tuple-element.72.normed_t, bf16[512,768]{1,0:T(8,128)(2,1)S(1)} %get-tuple-element.73.projected, ...), custom_call_target="tpu_custom_call" | custom-call | tf_op jit(solution)/shard_map/pallas_call | solution.py:486
  36.9 0.7 %collective-permute-done.7 = bf16[256,384]{1,0:T(8,128)(2,1)S(1)} collective-permute-done((bf16[256,384]{1,0:T(8,128)(2,1)S(1)}, bf16[256,384]{1,0:T(8,128)(2,1)S(1)}, u32[]{:S(2)}, u32[]{:S(2)}) %collective-permute-start.7) | collective-permute-done | bytes 196640 | tf_op jit(solution)/shard_map/ppermute | solution.py:501
  37.6 0.8 %collective-permute-start.11 = (bf16[256,384]{1,0:T(8,128)(2,1)S(1)}, bf16[256,384]{1,0:T(8,128)(2,1)S(1)}, u32[]{:S(2)}, u32[]{:S(2)}) collective-permute-start(bf16[256,384]{1,0:T(8,128)(2,1)S(1)} %add_convert_fusion.2), channel_id=1, source_target_pairs={{0,2},{1,3},{2,0},{3,1},{4,6},{5,7},{6,4},{7,5},{8,10},{9,11},{10,... | collective-permute-start | bytes 589832 | tf_op jit(solution)/shard_map/ppermute | solution.py:501
  38.5 1.7 %shard_map.154 = (bf16[128,512]{1,0:T(8,128)(2,1)}, bf16[128,512]{1,0:T(8,128)(2,1)}) custom-call(s32[2]{0:T(128)S(1)} %pad_add_fusion.1.place, bf16[144,512]{1,0:T(8,128)(2,1)S(1)} %fusion.1.chunk.own_states.own, bf16[128,512]{1,0:T(8,128)(2,1)S(1)} %bitcast.11, bf16[512,256]{1,0:T(8,128)(2,1)S(1)} %get-tuple-element.71.mixed, ...), custom_call_target="tpu_custom_call" | custom-call | tf_op jit(solution)/shard_map/pallas_call | solution.py:486
  40.3 6.1 %collective-permute-done.11 = bf16[256,384]{1,0:T(8,128)(2,1)S(1)} collective-permute-done((bf16[256,384]{1,0:T(8,128)(2,1)S(1)}, bf16[256,384]{1,0:T(8,128)(2,1)S(1)}, u32[]{:S(2)}, u32[]{:S(2)}) %collective-permute-start.11) | collective-permute-done | bytes 196640 | tf_op jit(solution)/shard_map/ppermute | solution.py:501
  47.1 1.0 %collective-permute-done.12.refs_3_ = bf16[128,512]{1,0:T(8,128)(2,1)S(1)} collective-permute-done((bf16[128,512]{1,0:T(8,128)(2,1)S(1)}, bf16[128,512]{1,0:T(8,128)(2,1)S(1)}, u32[]{:S(2)}, u32[]{:S(2)}) %collective-permute-start.12) | collective-permute-done | bytes 131104 | tf_op jit(solution)/shard_map/ppermute | solution.py:501
  48.1 1.9 %shard_map.155 = (f32[512,256]{1,0:T(8,128)}, f32[512,256]{1,0:T(8,128)}, f32[512,256]{1,0:T(8,128)}, f32[256,512]{1,0:T(8,128)}) custom-call(s32[2]{0:T(128)S(1)} %pad_add_fusion.1.place, bf16[128,512]{1,0:T(8,128)(2,1)S(1)} %add_convert_fusion.4.refs_0_, bf16[256,384]{1,0:T(8,128)(2,1)S(1)} %add_convert_fusion.1.refs_1_, ...), custom_call_target="tpu_custom_call" | custom-call | tf_op jit(solution)/shard_map/pallas_call | solution.py:486
  (41 shorter events, 5.2 us)
Async XLA Ops:
  2.4 9.5 %collective-permute-start = (bf16[144,512]{1,0:T(8,128)(2,1)S(1)}, bf16[144,512]{1,0:T(8,128)(2,1)S(1)}, u32[]{:S(2)}, u32[]{:S(2)}) collective-permute-start(bf16[144,512]{1,0:T(8,128)(2,1)S(1)} %fusion.1.chunk.own_states.own), channel_id=1, source_target_pairs={{0,4},{4,0},{8,12},{12,8},{1,5},{5,1},{9,13},{13,9},{2,6},{6,2},{1... | collective-permute-start | bytes 442376 | tf_op jit(solution)/shard_map/ppermute | solution.py:501
  5.5 9.6 %collective-permute-start.2 = (bf16[144,512]{1,0:T(8,128)(2,1)S(1)}, bf16[144,512]{1,0:T(8,128)(2,1)S(1)}, u32[]{:S(2)}, u32[]{:S(2)}) collective-permute-start(bf16[144,512]{1,0:T(8,128)(2,1)S(1)} %fusion.1.chunk.own_states.own), channel_id=1, source_target_pairs={{0,8},{4,12},{8,0},{12,4},{1,9},{5,13},{9,1},{13,5},{2,10},{6,14},... | collective-permute-start | bytes 442376 | tf_op jit(solution)/shard_map/ppermute | solution.py:501
  11.9 6.2 %copy-start = (bf16[512,256]{1,0:T(8,128)(2,1)S(1)}, bf16[512,256]{1,0:T(8,128)(2,1)}, u32[]{:S(2)}) copy-start(bf16[512,256]{1,0:T(8,128)(2,1)} %query_w.4) | copy-start | bytes 786436
  11.9 6.2 %copy-start.1 = (bf16[512,256]{1,0:T(8,128)(2,1)S(1)}, bf16[512,256]{1,0:T(8,128)(2,1)}, u32[]{:S(2)}) copy-start(bf16[512,256]{1,0:T(8,128)(2,1)} %key_w.4) | copy-start | bytes 786436
  11.9 6.2 %copy-start.2 = (bf16[512,256]{1,0:T(8,128)(2,1)S(1)}, bf16[512,256]{1,0:T(8,128)(2,1)}, u32[]{:S(2)}) copy-start(bf16[512,256]{1,0:T(8,128)(2,1)} %value_w.4) | copy-start | bytes 786436
  11.9 6.6 %copy-start.4 = (bf16[1,128,512]{2,1,0:T(8,128)(2,1)S(1)}, bf16[1,128,512]{2,1,0:T(8,128)(2,1)}, u32[]{:S(2)}) copy-start(bf16[1,128,512]{2,1,0:T(8,128)(2,1)} %param.11) | copy-start | bytes 393220
  11.9 8.7 %collective-permute-start.1 = (bf16[128,512]{1,0:T(8,128)(2,1)}, bf16[128,512]{1,0:T(8,128)(2,1)S(1)}, u32[]{:S(2)}, u32[]{:S(2)}) collective-permute-start(bf16[128,512]{1,0:T(8,128)(2,1)} %bitcast.8), channel_id=1, source_target_pairs={{0,8},{4,12},{8,0},{12,4},{1,9},{5,13},{9,1},{13,5},{2,10},{6,14},... | collective-permute-start | bytes 393224 | tf_op jit(solution)/shard_map/ppermute | solution.py:501
  15.0 7.7 %collective-permute-start.3 = (bf16[144,512]{1,0:T(8,128)(2,1)S(1)}, bf16[144,512]{1,0:T(8,128)(2,1)S(1)}, u32[]{:S(2)}, u32[]{:S(2)}) collective-permute-start(bf16[144,512]{1,0:T(8,128)(2,1)S(1)} %collective-permute-done.2.chunk.far_states), channel_id=1, source_target_pairs={{0,4},{4,0},{8,12},{12,8},{1,5},{5,1},{9,13},{13,9},{2,6},{6,2},{1... | collective-permute-start | bytes 442376 | tf_op jit(solution)/shard_map/ppermute | solution.py:501
  18.5 8.3 %collective-permute-start.4 = (bf16[128,512]{1,0:T(8,128)(2,1)S(1)}, bf16[128,512]{1,0:T(8,128)(2,1)S(1)}, u32[]{:S(2)}, u32[]{:S(2)}) collective-permute-start(bf16[128,512]{1,0:T(8,128)(2,1)S(1)} %bitcast.9), channel_id=1, source_target_pairs={{0,4},{4,0},{8,12},{12,8},{1,5},{5,1},{9,13},{13,9},{2,6},{6,2},{1... | collective-permute-start | bytes 393224 | tf_op jit(solution)/shard_map/ppermute | solution.py:501
  20.6 6.4 %collective-permute-start.5 = (bf16[128,512]{1,0:T(8,128)(2,1)S(1)}, bf16[128,512]{1,0:T(8,128)(2,1)S(1)}, u32[]{:S(2)}, u32[]{:S(2)}) collective-permute-start(bf16[128,512]{1,0:T(8,128)(2,1)S(1)} %collective-permute-done.1.far), channel_id=1, source_target_pairs={{0,4},{4,0},{8,12},{12,8},{1,5},{5,1},{9,13},{13,9},{2,6},{6,2},{1... | collective-permute-start | bytes 393224 | tf_op jit(solution)/shard_map/ppermute | solution.py:501
  22.8 4.2 %copy-start.3 = (bf16[256,512]{1,0:T(8,128)(2,1)S(1)}, bf16[256,512]{1,0:T(8,128)(2,1)}, u32[]{:S(2)}) copy-start(bf16[256,512]{1,0:T(8,128)(2,1)} %out_w.3) | copy-start | bytes 786436
  30.4 1.5 %collective-permute-start.6 = (bf16[256,384]{1,0:T(8,128)(2,1)S(1)}, bf16[256,384]{1,0:T(8,128)(2,1)S(1)}, u32[]{:S(2)}, u32[]{:S(2)}) collective-permute-start(bf16[256,384]{1,0:T(8,128)(2,1)S(1)} %get-tuple-element.79), channel_id=1, source_target_pairs={{0,1},{1,0},{2,3},{3,2},{4,5},{5,4},{6,7},{7,6},{8,9},{9,8},{10,11... | collective-permute-start | bytes 589832 | tf_op jit(solution)/shard_map/ppermute | solution.py:501
  31.9 4.3 %collective-permute-start.9 = (bf16[128,512]{1,0:T(8,128)(2,1)S(1)}, bf16[128,512]{1,0:T(8,128)(2,1)S(1)}, u32[]{:S(2)}, u32[]{:S(2)}) collective-permute-start(bf16[128,512]{1,0:T(8,128)(2,1)S(1)} %get-tuple-element.93), channel_id=1, source_target_pairs={{0,1},{1,0},{2,3},{3,2},{4,5},{5,4},{6,7},{7,6},{8,9},{9,8},{10,11... | collective-permute-start | bytes 393224 | tf_op jit(solution)/shard_map/ppermute | solution.py:501
  32.1 8.1 %collective-permute-start.8 = (bf16[256,384]{1,0:T(8,128)(2,1)S(1)}, bf16[256,384]{1,0:T(8,128)(2,1)S(1)}, u32[]{:S(2)}, u32[]{:S(2)}) collective-permute-start(bf16[256,384]{1,0:T(8,128)(2,1)S(1)} %add_convert_fusion.3), channel_id=1, source_target_pairs={{0,2},{1,3},{2,0},{3,1},{4,6},{5,7},{6,4},{7,5},{8,10},{9,11},{10,... | collective-permute-start | bytes 589832 | tf_op jit(solution)/shard_map/ppermute | solution.py:501
  36.1 1.5 %collective-permute-start.7 = (bf16[256,384]{1,0:T(8,128)(2,1)S(1)}, bf16[256,384]{1,0:T(8,128)(2,1)S(1)}, u32[]{:S(2)}, u32[]{:S(2)}) collective-permute-start(bf16[256,384]{1,0:T(8,128)(2,1)S(1)} %get-tuple-element.87), channel_id=1, source_target_pairs={{0,1},{1,0},{2,3},{3,2},{4,5},{5,4},{6,7},{7,6},{8,9},{9,8},{10,11... | collective-permute-start | bytes 589832 | tf_op jit(solution)/shard_map/ppermute | solution.py:501
  36.3 10.3 %collective-permute-start.10 = (bf16[128,512]{1,0:T(8,128)(2,1)S(1)}, bf16[128,512]{1,0:T(8,128)(2,1)S(1)}, u32[]{:S(2)}, u32[]{:S(2)}) collective-permute-start(bf16[128,512]{1,0:T(8,128)(2,1)S(1)} %add_convert_fusion.5), channel_id=1, source_target_pairs={{0,2},{1,3},{2,0},{3,1},{4,6},{5,7},{6,4},{7,5},{8,10},{9,11},{10,... | collective-permute-start | bytes 393224 | tf_op jit(solution)/shard_map/ppermute | solution.py:501
  37.6 8.7 %collective-permute-start.11 = (bf16[256,384]{1,0:T(8,128)(2,1)S(1)}, bf16[256,384]{1,0:T(8,128)(2,1)S(1)}, u32[]{:S(2)}, u32[]{:S(2)}) collective-permute-start(bf16[256,384]{1,0:T(8,128)(2,1)S(1)} %add_convert_fusion.2), channel_id=1, source_target_pairs={{0,2},{1,3},{2,0},{3,1},{4,6},{5,7},{6,4},{7,5},{8,10},{9,11},{10,... | collective-permute-start | bytes 589832 | tf_op jit(solution)/shard_map/ppermute | solution.py:501
  40.2 7.9 %collective-permute-start.13 = (bf16[256,384]{1,0:T(8,128)(2,1)S(1)}, bf16[256,384]{1,0:T(8,128)(2,1)S(1)}, u32[]{:S(2)}, u32[]{:S(2)}) collective-permute-start(bf16[256,384]{1,0:T(8,128)(2,1)S(1)} %add_convert_fusion.1.refs_1_), channel_id=1, source_target_pairs={{0,1},{1,0},{2,3},{3,2},{4,5},{5,4},{6,7},{7,6},{8,9},{9,8},{10,11... | collective-permute-start | bytes 589832 | tf_op jit(solution)/shard_map/ppermute | solution.py:501
  46.4 1.7 %collective-permute-start.14 = (bf16[256,384]{1,0:T(8,128)(2,1)S(1)}, bf16[256,384]{1,0:T(8,128)(2,1)S(1)}, u32[]{:S(2)}, u32[]{:S(2)}) collective-permute-start(bf16[256,384]{1,0:T(8,128)(2,1)S(1)} %add_convert_fusion.refs_2_), channel_id=1, source_target_pairs={{0,1},{1,0},{2,3},{3,2},{4,5},{5,4},{6,7},{7,6},{8,9},{9,8},{10,11... | collective-permute-start | bytes 589832 | tf_op jit(solution)/shard_map/ppermute | solution.py:501
  46.6 1.6 %collective-permute-start.12 = (bf16[128,512]{1,0:T(8,128)(2,1)S(1)}, bf16[128,512]{1,0:T(8,128)(2,1)S(1)}, u32[]{:S(2)}, u32[]{:S(2)}) collective-permute-start(bf16[128,512]{1,0:T(8,128)(2,1)S(1)} %add_convert_fusion.4.refs_0_), channel_id=1, source_target_pairs={{0,1},{1,0},{2,3},{3,2},{4,5},{5,4},{6,7},{7,6},{8,9},{9,8},{10,11... | collective-permute-start | bytes 393224 | tf_op jit(solution)/shard_map/ppermute | solution.py:501

commit v5 on v4

--- a/solution.py
+++ b/solution.py
@@ -201,6 +201,7 @@
 LANES = 128
 SLOTS = 16
 LEVEL_PARTS = 3
+TILE_ROWS = 8
 VMEM_LIMIT = 24 * 1024 * 1024
 
 
@@ -384,13 +385,12 @@
             mixed_t[lanes, low:high] = both.T.astype(jnp.bfloat16)
 
 
-def store_halves(place, value, keep, send, full):
+def product_halves(place, left, right, keep, send):
     half = keep.shape[0]
-    full[...] = value
-    keep[...] = full[pl.ds(pl.multiple_of(place[1] * half, half), half), :]
-    send[...] = full[pl.ds(pl.multiple_of((1 - place[1]) * half, half), half), :].astype(
-        jnp.bfloat16
-    )
+    mine = pl.ds(pl.multiple_of(place[1] * half, half), half)
+    other = pl.ds(pl.multiple_of((1 - place[1]) * half, half), half)
+    send[...] = plain_product(left[other, :], right).astype(jnp.bfloat16)
+    keep[...] = plain_product(left[mine, :], right)
 
 
 def mix_kernel(place, own, near, far, last, out_w, gathered, d_mixed):
@@ -401,14 +401,14 @@
     d_mixed[...] = pair_product(gathered[...], out_w[...]).astype(jnp.bfloat16)
 
 
-def output_kernel(place, gathered, mixed_t, keep, send, full):
-    store_halves(place, plain_product(mixed_t[...], gathered[...]), keep, send, full)
+def output_kernel(place, gathered, mixed_t, keep, send):
+    product_halves(place, mixed_t, gathered[...], keep, send)
 
 
 def backward_kernel(
     pair, place, normed_t, projected, probs, mixed, d_mixed,
     d_own, keep, send,
-    grads, key_sum, value_sum, full,
+    grads, key_sum, value_sum,
 ):
     total, width = mixed.shape
     rows = d_own.shape[0]
@@ -442,7 +442,7 @@
             value_sum[:high, :] += value_term
     grads[:, LANES : 2 * LANES] = (key_sum[...] * scale).astype(jnp.bfloat16)
     grads[:, 2 * LANES :] = value_sum[...].astype(jnp.bfloat16)
-    store_halves(place, plain_product(normed_t[...], grads[...]), keep, send, full)
+    product_halves(place, normed_t, grads[...], keep, send)
     d_own[...] = grads[pl.ds(pl.multiple_of(place[0] * rows, rows), rows), :]
 
 
@@ -539,7 +539,7 @@
     match |= (kinds < 0) | (kinds >= SLOTS)
     hidden = (1.0 - jnp.max(match.astype(wide), axis=1)) * NEG
     own = jnp.concatenate(
-        [states, jnp.pad(hidden.astype(half), ((0, SLOTS - local_blocks), (0, 0)))], axis=0
+        [states, jnp.pad(hidden.astype(half), ((0, TILE_ROWS - local_blocks), (0, 0)))], axis=0
     )
     far = swap(own, "node", 2)
     near = swap(own, "node", 1)
@@ -608,7 +608,6 @@
                 [((width // 2, model), wide), ((width // 2, model), half)],
                 [place],
                 [gathered, mixed_t],
-                [pltpu.VMEM((width, model), wide)],
             )
             d_mixed, local, out_send = lax.optimization_barrier((d_mixed, local, out_send))
             halves[0] = (local, across)
@@ -625,7 +624,6 @@
                 pltpu.VMEM((total, 3 * LANES), half),
                 pltpu.VMEM((total, LANES), wide),
                 pltpu.VMEM((total, LANES), wide),
-                pltpu.VMEM((model, 3 * LANES), wide),
             ],
         )
         d_own.append(own_grads)

time: 50.3 us -> 49.8 us (0.990)
  no operation moved by 1% of the time
where the time goes in v5:
time: 49.8 us; the launch traced here: 49.6 us
  Pallas kernels  16 us (32%)
  waiting for transfers between devices  15.2 us (31%)
  starting transfers between devices  14.1 us (28%)
  other arithmetic  3.41 us (7%)
  between operations  0.83 us (2%)
    pallas_call x11, Pallas kernels, run(): pl.pallas_call(kernel, out_shape=out_shape, in_specs=[pl.BlockSpec(memory...  16 us
    ppermute x15, waiting for transfers between devices, swap(): lax.ppermute(array, axis, [(i, i ^ flip) for i in range(lax.axis_size(axi...  15.2 us
    ppermute x15, starting transfers between devices, swap(): lax.ppermute(array, axis, [(i, i ^ flip) for i in range(lax.axis_size(axi...  14.1 us
  transfers between devices with their start and end apart: 15, of which 9 were waited for; matrix products, arithmetic and copies ran while one was open for 3% of the time, Pallas kernels for 22%

profile of v5, /device:TPU:0, one launch (start us, length us, event | category | flops | bytes accessed | tf_op | source)
XLA Modules:
  0.0 49.6 jit_solution(13276316853213081758)
XLA Ops:
  0.7 0.8 %convert_reduce_fusion = f32[2,512]{1,0:T(2,128)S(1)} fusion(s32[2]{0:T(128)} %bitcast.14, s32[512]{0:T(512)S(1)} %and_add_fusion, s32[2,8]{1,0:T(2,128)} %bitcast.13, pred[512]{0:T(512)(128)(4,1)S(1)} %compare_or_fusion), kind=kLoop, calls=%fused_computation.9 | loop fusion | flops 48128 | bytes 6728 | tf_op jit(solution)/shard_map/reduce_max | solution.py:540
  1.5 0.9 %fusion.1.chunk.own_states.own = bf16[136,512]{1,0:T(8,128)(2,1)S(1)} fusion(bf16[2,512]{1,0:T(2,128)(2,1)S(1)} %multiply_convert_fusion, bf16[128,512]{1,0:T(8,128)(2,1)} %bitcast.12), kind=kLoop, calls=%fused_computation.8 | loop fusion | flops 417792 | bytes 272384 | tf_op jit(solution)/shard_map/concatenate | solution.py:541
  2.4 3.1 %collective-permute-start = (bf16[136,512]{1,0:T(8,128)(2,1)S(1)}, bf16[136,512]{1,0:T(8,128)(2,1)S(1)}, u32[]{:S(2)}, u32[]{:S(2)}) collective-permute-start(bf16[136,512]{1,0:T(8,128)(2,1)S(1)} %fusion.1.chunk.own_states.own), channel_id=1, source_target_pairs={{0,4},{4,0},{8,12},{12,8},{1,5},{5,1},{9,13},{13,9},{2,6},{6,2},{1... | collective-permute-start | bytes 417800 | tf_op jit(solution)/shard_map/ppermute | solution.py:501
  5.5 2.6 %collective-permute-start.2 = (bf16[136,512]{1,0:T(8,128)(2,1)S(1)}, bf16[136,512]{1,0:T(8,128)(2,1)S(1)}, u32[]{:S(2)}, u32[]{:S(2)}) collective-permute-start(bf16[136,512]{1,0:T(8,128)(2,1)S(1)} %fusion.1.chunk.own_states.own), channel_id=1, source_target_pairs={{0,8},{4,12},{8,0},{12,4},{1,9},{5,13},{9,1},{13,5},{2,10},{6,14},... | collective-permute-start | bytes 417800 | tf_op jit(solution)/shard_map/ppermute | solution.py:501
  8.7 0.7 %pad_add_fusion.scalars = f32[8,128]{1,0:T(8,128)S(1)} fusion(f32[1,17]{1,0:T(1,128)S(1)} %convert_element_type.63, f32[4,32]{1,0:T(4,128)} %param.19), kind=kLoop, calls=%fused_computation.13 | loop fusion | flops 1024 | bytes 4676 | tf_op jit(solution)/shard_map/add | solution.py:550
  9.4 1.9 %collective-permute-done.chunk.near_states = bf16[136,512]{1,0:T(8,128)(2,1)S(1)} collective-permute-done((bf16[136,512]{1,0:T(8,128)(2,1)S(1)}, bf16[136,512]{1,0:T(8,128)(2,1)S(1)}, u32[]{:S(2)}, u32[]{:S(2)}) %collective-permute-start) | collective-permute-done | bytes 139296 | tf_op jit(solution)/shard_map/ppermute | solution.py:501
  11.3 1.8 %collective-permute-start.1 = (bf16[128,512]{1,0:T(8,128)(2,1)}, bf16[128,512]{1,0:T(8,128)(2,1)S(1)}, u32[]{:S(2)}, u32[]{:S(2)}) collective-permute-start(bf16[128,512]{1,0:T(8,128)(2,1)} %bitcast.8), channel_id=1, source_target_pairs={{0,8},{4,12},{8,0},{12,4},{1,9},{5,13},{9,1},{13,5},{2,10},{6,14},... | collective-permute-start | bytes 393224 | tf_op jit(solution)/shard_map/ppermute | solution.py:501
  13.1 1.6 %collective-permute-done.2.chunk.far_states = bf16[136,512]{1,0:T(8,128)(2,1)S(1)} collective-permute-done((bf16[136,512]{1,0:T(8,128)(2,1)S(1)}, bf16[136,512]{1,0:T(8,128)(2,1)S(1)}, u32[]{:S(2)}, u32[]{:S(2)}) %collective-permute-start.2) | collective-permute-done | bytes 139296 | tf_op jit(solution)/shard_map/ppermute | solution.py:501
  14.7 2.0 %collective-permute-start.3 = (bf16[136,512]{1,0:T(8,128)(2,1)S(1)}, bf16[136,512]{1,0:T(8,128)(2,1)S(1)}, u32[]{:S(2)}, u32[]{:S(2)}) collective-permute-start(bf16[136,512]{1,0:T(8,128)(2,1)S(1)} %collective-permute-done.2.chunk.far_states), channel_id=1, source_target_pairs={{0,4},{4,0},{8,12},{12,8},{1,5},{5,1},{9,13},{13,9},{2,6},{6,2},{1... | collective-permute-start | bytes 417800 | tf_op jit(solution)/shard_map/ppermute | solution.py:501
  16.7 0.8 %shard_map.145 = (bf16[32,512]{1,0:T(8,128)(2,1)S(1)}, bf16[16,512]{1,0:T(8,128)(2,1)S(1)}, bf16[512,128]{1,0:T(8,128)(2,1)S(1)}) custom-call(f32[8,128]{1,0:T(8,128)S(1)} %pad_add_fusion.scalars), custom_call_target="tpu_custom_call" | custom-call | flops 10000000000 | tf_op jit(solution)/shard_map/pallas_call | solution.py:486
  18.7 1.5 %collective-permute-done.1.far = bf16[128,512]{1,0:T(8,128)(2,1)S(1)} collective-permute-done((bf16[128,512]{1,0:T(8,128)(2,1)}, bf16[128,512]{1,0:T(8,128)(2,1)S(1)}, u32[]{:S(2)}, u32[]{:S(2)}) %collective-permute-start.1) | collective-permute-done | bytes 131104 | tf_op jit(solution)/shard_map/ppermute | solution.py:501
  20.8 1.6 %collective-permute-done.3.last_states = bf16[136,512]{1,0:T(8,128)(2,1)S(1)} collective-permute-done((bf16[136,512]{1,0:T(8,128)(2,1)S(1)}, bf16[136,512]{1,0:T(8,128)(2,1)S(1)}, u32[]{:S(2)}, u32[]{:S(2)}) %collective-permute-start.3) | collective-permute-done | bytes 139296 | tf_op jit(solution)/shard_map/ppermute | solution.py:501
  22.3 4.0 %shard_map.149 = (bf16[512,512]{1,0:T(8,128)(2,1)S(1)}, bf16[512,768]{1,0:T(8,128)(2,1)S(1)}, bf16[2,1024,512]{2,1,0:T(8,128)(2,1)S(1)}, bf16[512,256]{1,0:T(8,128)(2,1)S(1)}, bf16[256,512]{1,0:T(8,128)(2,1)S(1)}) custom-call(s32[2]{0:T(128)S(1)} %pad_add_fusion.1.place, f32[8,128]{1,0:T(8,128)S(1)} %pad_add_fusion.scalars, ...), custom_call_target="tpu_custom_call" | custom-call | flops 5000000000 | tf_op jit(solution)/shard_map/pallas_call | solution.py:486
  26.6 0.9 %shard_map.150 = (bf16[512,512]{1,0:T(8,128)(2,1)S(1)}, bf16[512,256]{1,0:T(8,128)(2,1)S(1)}) custom-call(s32[2]{0:T(128)S(1)} %pad_add_fusion.1.place, bf16[128,512]{1,0:T(8,128)(2,1)S(1)} %bitcast.10, bf16[128,512]{1,0:T(8,128)(2,1)S(1)} %collective-permute-done.4.near, bf16[128,512]{1,0:T(8,128)(2,1)S(1)} %collective-permute-done.1.far, ...), custom_call_target="tpu_custom_call" | custom-call | tf_op jit(solution)/shard_map/pallas_call | solution.py:486
  27.4 2.4 %shard_map.151 = (bf16[128,384]{1,0:T(8,128)(2,1)S(1)}, f32[256,384]{1,0:T(8,128)S(1)}, bf16[256,384]{1,0:T(8,128)(2,1)S(1)}) custom-call(s32[2]{0:T(128)S(1)} %pad_add_fusion.1.place, bf16[512,512]{1,0:T(8,128)(2,1)S(1)} %get-tuple-element.72.normed_t, bf16[512,768]{1,0:T(8,128)(2,1)S(1)} %get-tuple-element.73.projected, ...), custom_call_target="tpu_custom_call" | custom-call | tf_op jit(solution)/shard_map/pallas_call | solution.py:486
  29.9 0.8 %shard_map.152 = (f32[128,512]{1,0:T(8,128)S(1)}, bf16[128,512]{1,0:T(8,128)(2,1)S(1)}) custom-call(s32[2]{0:T(128)S(1)} %pad_add_fusion.1.place, bf16[512,512]{1,0:T(8,128)(2,1)S(1)} %get-tuple-element.81.gathered, bf16[256,512]{1,0:T(8,128)(2,1)S(1)} %get-tuple-element.82.mixed_t), custom_call_target="tpu_custom_call" | custom-call | tf_op jit(solution)/shard_map/pallas_call | solution.py:486
  31.6 1.5 %collective-permute-start.8 = (bf16[256,384]{1,0:T(8,128)(2,1)S(1)}, bf16[256,384]{1,0:T(8,128)(2,1)S(1)}, u32[]{:S(2)}, u32[]{:S(2)}) collective-permute-start(bf16[256,384]{1,0:T(8,128)(2,1)S(1)} %add_convert_fusion.3), channel_id=1, source_target_pairs={{0,2},{1,3},{2,0},{3,1},{4,6},{5,7},{6,4},{7,5},{8,10},{9,11},{10,... | collective-permute-start | bytes 589832 | tf_op jit(solution)/shard_map/ppermute | solution.py:501
  33.1 2.4 %shard_map.153 = (bf16[128,384]{1,0:T(8,128)(2,1)S(1)}, f32[256,384]{1,0:T(8,128)S(1)}, bf16[256,384]{1,0:T(8,128)(2,1)S(1)}) custom-call(s32[2]{0:T(128)S(1)} %pad_add_fusion.1.place, bf16[512,512]{1,0:T(8,128)(2,1)S(1)} %get-tuple-element.72.normed_t, bf16[512,768]{1,0:T(8,128)(2,1)S(1)} %get-tuple-element.73.projected, ...), custom_call_target="tpu_custom_call" | custom-call | tf_op jit(solution)/shard_map/pallas_call | solution.py:486
  36.3 0.7 %collective-permute-done.7 = bf16[256,384]{1,0:T(8,128)(2,1)S(1)} collective-permute-done((bf16[256,384]{1,0:T(8,128)(2,1)S(1)}, bf16[256,384]{1,0:T(8,128)(2,1)S(1)}, u32[]{:S(2)}, u32[]{:S(2)}) %collective-permute-start.7) | collective-permute-done | bytes 196640 | tf_op jit(solution)/shard_map/ppermute | solution.py:501
  37.1 0.8 %collective-permute-start.11 = (bf16[256,384]{1,0:T(8,128)(2,1)S(1)}, bf16[256,384]{1,0:T(8,128)(2,1)S(1)}, u32[]{:S(2)}, u32[]{:S(2)}) collective-permute-start(bf16[256,384]{1,0:T(8,128)(2,1)S(1)} %add_convert_fusion.2), channel_id=1, source_target_pairs={{0,2},{1,3},{2,0},{3,1},{4,6},{5,7},{6,4},{7,5},{8,10},{9,11},{10,... | collective-permute-start | bytes 589832 | tf_op jit(solution)/shard_map/ppermute | solution.py:501
  37.9 1.7 %shard_map.154 = (bf16[128,512]{1,0:T(8,128)(2,1)}, bf16[128,512]{1,0:T(8,128)(2,1)}) custom-call(s32[2]{0:T(128)S(1)} %pad_add_fusion.1.place, bf16[136,512]{1,0:T(8,128)(2,1)S(1)} %fusion.1.chunk.own_states.own, bf16[128,512]{1,0:T(8,128)(2,1)S(1)} %bitcast.11, bf16[512,256]{1,0:T(8,128)(2,1)S(1)} %get-tuple-element.71.mixed, ...), custom_call_target="tpu_custom_call" | custom-call | tf_op jit(solution)/shard_map/pallas_call | solution.py:486
  39.8 6.1 %collective-permute-done.11 = bf16[256,384]{1,0:T(8,128)(2,1)S(1)} collective-permute-done((bf16[256,384]{1,0:T(8,128)(2,1)S(1)}, bf16[256,384]{1,0:T(8,128)(2,1)S(1)}, u32[]{:S(2)}, u32[]{:S(2)}) %collective-permute-start.11) | collective-permute-done | bytes 196640 | tf_op jit(solution)/shard_map/ppermute | solution.py:501
  46.6 1.0 %collective-permute-done.12.refs_3_ = bf16[128,512]{1,0:T(8,128)(2,1)S(1)} collective-permute-done((bf16[128,512]{1,0:T(8,128)(2,1)S(1)}, bf16[128,512]{1,0:T(8,128)(2,1)S(1)}, u32[]{:S(2)}, u32[]{:S(2)}) %collective-permute-start.12) | collective-permute-done | bytes 131104 | tf_op jit(solution)/shard_map/ppermute | solution.py:501
  47.6 1.9 %shard_map.155 = (f32[512,256]{1,0:T(8,128)}, f32[512,256]{1,0:T(8,128)}, f32[512,256]{1,0:T(8,128)}, f32[256,512]{1,0:T(8,128)}) custom-call(s32[2]{0:T(128)S(1)} %pad_add_fusion.1.place, bf16[128,512]{1,0:T(8,128)(2,1)S(1)} %add_convert_fusion.4.refs_0_, bf16[256,384]{1,0:T(8,128)(2,1)S(1)} %add_convert_fusion.1.refs_1_, ...), custom_call_target="tpu_custom_call" | custom-call | tf_op jit(solution)/shard_map/pallas_call | solution.py:486
  (41 shorter events, 5.1 us)
Async XLA Ops:
  2.4 9.0 %collective-permute-start = (bf16[136,512]{1,0:T(8,128)(2,1)S(1)}, bf16[136,512]{1,0:T(8,128)(2,1)S(1)}, u32[]{:S(2)}, u32[]{:S(2)}) collective-permute-start(bf16[136,512]{1,0:T(8,128)(2,1)S(1)} %fusion.1.chunk.own_states.own), channel_id=1, source_target_pairs={{0,4},{4,0},{8,12},{12,8},{1,5},{5,1},{9,13},{13,9},{2,6},{6,2},{1... | collective-permute-start | bytes 417800 | tf_op jit(solution)/shard_map/ppermute | solution.py:501
  5.5 9.2 %collective-permute-start.2 = (bf16[136,512]{1,0:T(8,128)(2,1)S(1)}, bf16[136,512]{1,0:T(8,128)(2,1)S(1)}, u32[]{:S(2)}, u32[]{:S(2)}) collective-permute-start(bf16[136,512]{1,0:T(8,128)(2,1)S(1)} %fusion.1.chunk.own_states.own), channel_id=1, source_target_pairs={{0,8},{4,12},{8,0},{12,4},{1,9},{5,13},{9,1},{13,5},{2,10},{6,14},... | collective-permute-start | bytes 417800 | tf_op jit(solution)/shard_map/ppermute | solution.py:501
  11.3 6.2 %copy-start = (bf16[512,256]{1,0:T(8,128)(2,1)S(1)}, bf16[512,256]{1,0:T(8,128)(2,1)}, u32[]{:S(2)}) copy-start(bf16[512,256]{1,0:T(8,128)(2,1)} %query_w.4) | copy-start | bytes 786436
  11.3 6.2 %copy-start.1 = (bf16[512,256]{1,0:T(8,128)(2,1)S(1)}, bf16[512,256]{1,0:T(8,128)(2,1)}, u32[]{:S(2)}) copy-start(bf16[512,256]{1,0:T(8,128)(2,1)} %key_w.4) | copy-start | bytes 786436
  11.3 6.2 %copy-start.2 = (bf16[512,256]{1,0:T(8,128)(2,1)S(1)}, bf16[512,256]{1,0:T(8,128)(2,1)}, u32[]{:S(2)}) copy-start(bf16[512,256]{1,0:T(8,128)(2,1)} %value_w.4) | copy-start | bytes 786436
  11.3 6.6 %copy-start.4 = (bf16[1,128,512]{2,1,0:T(8,128)(2,1)S(1)}, bf16[1,128,512]{2,1,0:T(8,128)(2,1)}, u32[]{:S(2)}) copy-start(bf16[1,128,512]{2,1,0:T(8,128)(2,1)} %param.11) | copy-start | bytes 393220
  11.3 8.9 %collective-permute-start.1 = (bf16[128,512]{1,0:T(8,128)(2,1)}, bf16[128,512]{1,0:T(8,128)(2,1)S(1)}, u32[]{:S(2)}, u32[]{:S(2)}) collective-permute-start(bf16[128,512]{1,0:T(8,128)(2,1)} %bitcast.8), channel_id=1, source_target_pairs={{0,8},{4,12},{8,0},{12,4},{1,9},{5,13},{9,1},{13,5},{2,10},{6,14},... | collective-permute-start | bytes 393224 | tf_op jit(solution)/shard_map/ppermute | solution.py:501
  14.7 7.7 %collective-permute-start.3 = (bf16[136,512]{1,0:T(8,128)(2,1)S(1)}, bf16[136,512]{1,0:T(8,128)(2,1)S(1)}, u32[]{:S(2)}, u32[]{:S(2)}) collective-permute-start(bf16[136,512]{1,0:T(8,128)(2,1)S(1)} %collective-permute-done.2.chunk.far_states), channel_id=1, source_target_pairs={{0,4},{4,0},{8,12},{12,8},{1,5},{5,1},{9,13},{13,9},{2,6},{6,2},{1... | collective-permute-start | bytes 417800 | tf_op jit(solution)/shard_map/ppermute | solution.py:501
  18.0 8.3 %collective-permute-start.4 = (bf16[128,512]{1,0:T(8,128)(2,1)S(1)}, bf16[128,512]{1,0:T(8,128)(2,1)S(1)}, u32[]{:S(2)}, u32[]{:S(2)}) collective-permute-start(bf16[128,512]{1,0:T(8,128)(2,1)S(1)} %bitcast.9), channel_id=1, source_target_pairs={{0,4},{4,0},{8,12},{12,8},{1,5},{5,1},{9,13},{13,9},{2,6},{6,2},{1... | collective-permute-start | bytes 393224 | tf_op jit(solution)/shard_map/ppermute | solution.py:501
  20.2 6.3 %collective-permute-start.5 = (bf16[128,512]{1,0:T(8,128)(2,1)S(1)}, bf16[128,512]{1,0:T(8,128)(2,1)S(1)}, u32[]{:S(2)}, u32[]{:S(2)}) collective-permute-start(bf16[128,512]{1,0:T(8,128)(2,1)S(1)} %collective-permute-done.1.far), channel_id=1, source_target_pairs={{0,4},{4,0},{8,12},{12,8},{1,5},{5,1},{9,13},{13,9},{2,6},{6,2},{1... | collective-permute-start | bytes 393224 | tf_op jit(solution)/shard_map/ppermute | solution.py:501
  22.3 4.2 %copy-start.3 = (bf16[256,512]{1,0:T(8,128)(2,1)S(1)}, bf16[256,512]{1,0:T(8,128)(2,1)}, u32[]{:S(2)}) copy-start(bf16[256,512]{1,0:T(8,128)(2,1)} %out_w.3) | copy-start | bytes 786436
  29.9 1.5 %collective-permute-start.6 = (bf16[256,384]{1,0:T(8,128)(2,1)S(1)}, bf16[256,384]{1,0:T(8,128)(2,1)S(1)}, u32[]{:S(2)}, u32[]{:S(2)}) collective-permute-start(bf16[256,384]{1,0:T(8,128)(2,1)S(1)} %get-tuple-element.79), channel_id=1, source_target_pairs={{0,1},{1,0},{2,3},{3,2},{4,5},{5,4},{6,7},{7,6},{8,9},{9,8},{10,11... | collective-permute-start | bytes 589832 | tf_op jit(solution)/shard_map/ppermute | solution.py:501
  31.4 4.3 %collective-permute-start.9 = (bf16[128,512]{1,0:T(8,128)(2,1)S(1)}, bf16[128,512]{1,0:T(8,128)(2,1)S(1)}, u32[]{:S(2)}, u32[]{:S(2)}) collective-permute-start(bf16[128,512]{1,0:T(8,128)(2,1)S(1)} %get-tuple-element.93), channel_id=1, source_target_pairs={{0,1},{1,0},{2,3},{3,2},{4,5},{5,4},{6,7},{7,6},{8,9},{9,8},{10,11... | collective-permute-start | bytes 393224 | tf_op jit(solution)/shard_map/ppermute | solution.py:501
  31.6 8.0 %collective-permute-start.8 = (bf16[256,384]{1,0:T(8,128)(2,1)S(1)}, bf16[256,384]{1,0:T(8,128)(2,1)S(1)}, u32[]{:S(2)}, u32[]{:S(2)}) collective-permute-start(bf16[256,384]{1,0:T(8,128)(2,1)S(1)} %add_convert_fusion.3), channel_id=1, source_target_pairs={{0,2},{1,3},{2,0},{3,1},{4,6},{5,7},{6,4},{7,5},{8,10},{9,11},{10,... | collective-permute-start | bytes 589832 | tf_op jit(solution)/shard_map/ppermute | solution.py:501
  35.5 1.5 %collective-permute-start.7 = (bf16[256,384]{1,0:T(8,128)(2,1)S(1)}, bf16[256,384]{1,0:T(8,128)(2,1)S(1)}, u32[]{:S(2)}, u32[]{:S(2)}) collective-permute-start(bf16[256,384]{1,0:T(8,128)(2,1)S(1)} %get-tuple-element.87), channel_id=1, source_target_pairs={{0,1},{1,0},{2,3},{3,2},{4,5},{5,4},{6,7},{7,6},{8,9},{9,8},{10,11... | collective-permute-start | bytes 589832 | tf_op jit(solution)/shard_map/ppermute | solution.py:501
  35.7 10.3 %collective-permute-start.10 = (bf16[128,512]{1,0:T(8,128)(2,1)S(1)}, bf16[128,512]{1,0:T(8,128)(2,1)S(1)}, u32[]{:S(2)}, u32[]{:S(2)}) collective-permute-start(bf16[128,512]{1,0:T(8,128)(2,1)S(1)} %add_convert_fusion.5), channel_id=1, source_target_pairs={{0,2},{1,3},{2,0},{3,1},{4,6},{5,7},{6,4},{7,5},{8,10},{9,11},{10,... | collective-permute-start | bytes 393224 | tf_op jit(solution)/shard_map/ppermute | solution.py:501
  37.1 8.8 %collective-permute-start.11 = (bf16[256,384]{1,0:T(8,128)(2,1)S(1)}, bf16[256,384]{1,0:T(8,128)(2,1)S(1)}, u32[]{:S(2)}, u32[]{:S(2)}) collective-permute-start(bf16[256,384]{1,0:T(8,128)(2,1)S(1)} %add_convert_fusion.2), channel_id=1, source_target_pairs={{0,2},{1,3},{2,0},{3,1},{4,6},{5,7},{6,4},{7,5},{8,10},{9,11},{10,... | collective-permute-start | bytes 589832 | tf_op jit(solution)/shard_map/ppermute | solution.py:501
  39.7 7.9 %collective-permute-start.13 = (bf16[256,384]{1,0:T(8,128)(2,1)S(1)}, bf16[256,384]{1,0:T(8,128)(2,1)S(1)}, u32[]{:S(2)}, u32[]{:S(2)}) collective-permute-start(bf16[256,384]{1,0:T(8,128)(2,1)S(1)} %add_convert_fusion.1.refs_1_), channel_id=1, source_target_pairs={{0,1},{1,0},{2,3},{3,2},{4,5},{5,4},{6,7},{7,6},{8,9},{9,8},{10,11... | collective-permute-start | bytes 589832 | tf_op jit(solution)/shard_map/ppermute | solution.py:501
  45.9 1.7 %collective-permute-start.14 = (bf16[256,384]{1,0:T(8,128)(2,1)S(1)}, bf16[256,384]{1,0:T(8,128)(2,1)S(1)}, u32[]{:S(2)}, u32[]{:S(2)}) collective-permute-start(bf16[256,384]{1,0:T(8,128)(2,1)S(1)} %add_convert_fusion.refs_2_), channel_id=1, source_target_pairs={{0,1},{1,0},{2,3},{3,2},{4,5},{5,4},{6,7},{7,6},{8,9},{9,8},{10,11... | collective-permute-start | bytes 589832 | tf_op jit(solution)/shard_map/ppermute | solution.py:501
  46.0 1.6 %collective-permute-start.12 = (bf16[128,512]{1,0:T(8,128)(2,1)S(1)}, bf16[128,512]{1,0:T(8,128)(2,1)S(1)}, u32[]{:S(2)}, u32[]{:S(2)}) collective-permute-start(bf16[128,512]{1,0:T(8,128)(2,1)S(1)} %add_convert_fusion.4.refs_0_), channel_id=1, source_target_pairs={{0,1},{1,0},{2,3},{3,2},{4,5},{5,4},{6,7},{7,6},{8,9},{9,8},{10,11... | collective-permute-start | bytes 393224 | tf_op jit(solution)/shard_map/ppermute | solution.py:501

commit v6 on v5

--- a/solution.py
+++ b/solution.py
@@ -544,9 +544,9 @@
     far = swap(own, "node", 2)
     near = swap(own, "node", 1)
     last = swap(far, "node", 1)
+    grads_near = swap(grads_in, "node", 1)
     grads_sent, near = lax.optimization_barrier((grads_in, near))
     grads_far = swap(grads_sent, "node", 2)
-    grads_near = swap(grads_sent, "node", 1)
     scalars = jnp.pad(bias_table, ((0, HEADS), (0, LANES - DIST))) + jnp.pad(
         starts.astype(wide)[None, :], ((HEADS, HEADS - 1), (0, LANES - starts.shape[0]))
     )

time: 49.8 us -> 49 us (0.984)
  waiting for transfers between devices: 15.2 us -> 11.9 us
  starting transfers between devices: 14.1 us -> 16.6 us
    ppermute x15, waiting for transfers between devices: 15.2 us -> 11.9 us  [swap(): lax.ppermute(array, axis, [(i, i ^ flip) for i in range(lax.axis_size(axi...]
    ppermute x15, starting transfers between devices: 14.1 us -> 16.6 us  [swap(): lax.ppermute(array, axis, [(i, i ^ flip) for i in range(lax.axis_size(axi...]
  transfers between devices with their start and end apart: 15 -> 15, of which waited for: 9 -> 6; matrix products, arithmetic and copies ran while one was open for 3% -> 3% of each run, Pallas kernels for 22% -> 22%
where the time goes in v6:
time: 49 us; the launch traced here: 48.8 us
  starting transfers between devices  16.6 us (34%)
  Pallas kernels  16 us (33%)
  waiting for transfers between devices  11.9 us (24%)
  other arithmetic  3.41 us (7%)
  between operations  0.86 us (2%)
    ppermute x15, starting transfers between devices, swap(): lax.ppermute(array, axis, [(i, i ^ flip) for i in range(lax.axis_size(axi...  16.6 us
    pallas_call x11, Pallas kernels, run(): pl.pallas_call(kernel, out_shape=out_shape, in_specs=[pl.BlockSpec(memory...  16 us
    ppermute x15, waiting for transfers between devices, swap(): lax.ppermute(array, axis, [(i, i ^ flip) for i in range(lax.axis_size(axi...  11.9 us
  transfers between devices with their start and end apart: 15, of which 6 were waited for; matrix products, arithmetic and copies ran while one was open for 3% of the time, Pallas kernels for 22%

profile of v6, /device:TPU:0, one launch (start us, length us, event | category | flops | bytes accessed | tf_op | source)
XLA Modules:
  0.0 48.8 jit_solution(6669709030099980169)
XLA Ops:
  0.7 0.8 %convert_reduce_fusion = f32[2,512]{1,0:T(2,128)S(1)} fusion(s32[2]{0:T(128)} %bitcast.14, s32[512]{0:T(512)S(1)} %and_add_fusion, s32[2,8]{1,0:T(2,128)} %bitcast.13, pred[512]{0:T(512)(128)(4,1)S(1)} %compare_or_fusion), kind=kLoop, calls=%fused_computation.9 | loop fusion | flops 48128 | bytes 6728 | tf_op jit(solution)/shard_map/reduce_max | solution.py:540
  1.5 0.9 %fusion.1.chunk.own_states.own = bf16[136,512]{1,0:T(8,128)(2,1)S(1)} fusion(bf16[2,512]{1,0:T(2,128)(2,1)S(1)} %multiply_convert_fusion, bf16[128,512]{1,0:T(8,128)(2,1)} %bitcast.12), kind=kLoop, calls=%fused_computation.8 | loop fusion | flops 417792 | bytes 272384 | tf_op jit(solution)/shard_map/concatenate | solution.py:541
  2.4 3.1 %collective-permute-start = (bf16[136,512]{1,0:T(8,128)(2,1)S(1)}, bf16[136,512]{1,0:T(8,128)(2,1)S(1)}, u32[]{:S(2)}, u32[]{:S(2)}) collective-permute-start(bf16[136,512]{1,0:T(8,128)(2,1)S(1)} %fusion.1.chunk.own_states.own), channel_id=1, source_target_pairs={{0,4},{4,0},{8,12},{12,8},{1,5},{5,1},{9,13},{13,9},{2,6},{6,2},{1... | collective-permute-start | bytes 417800 | tf_op jit(solution)/shard_map/ppermute | solution.py:501
  5.5 2.6 %collective-permute-start.2 = (bf16[136,512]{1,0:T(8,128)(2,1)S(1)}, bf16[136,512]{1,0:T(8,128)(2,1)S(1)}, u32[]{:S(2)}, u32[]{:S(2)}) collective-permute-start(bf16[136,512]{1,0:T(8,128)(2,1)S(1)} %fusion.1.chunk.own_states.own), channel_id=1, source_target_pairs={{0,8},{4,12},{8,0},{12,4},{1,9},{5,13},{9,1},{13,5},{2,10},{6,14},... | collective-permute-start | bytes 417800 | tf_op jit(solution)/shard_map/ppermute | solution.py:501
  8.5 0.7 %convert_element_type.63 = f32[1,17]{1,0:T(1,128)S(1)} convert(s32[1,17]{1,0:T(1,128)} %param.14) | non-fusion elementwise | flops 17 | bytes 136 | tf_op jit(solution)/shard_map/convert_element_type | solution.py:551
  9.2 0.7 %pad_add_fusion.scalars = f32[8,128]{1,0:T(8,128)S(1)} fusion(f32[1,17]{1,0:T(1,128)S(1)} %convert_element_type.63, f32[4,32]{1,0:T(4,128)} %param.19), kind=kLoop, calls=%fused_computation.13 | loop fusion | flops 1024 | bytes 4676 | tf_op jit(solution)/shard_map/add | solution.py:550
  9.9 2.4 %collective-permute-done.chunk.near_states = bf16[136,512]{1,0:T(8,128)(2,1)S(1)} collective-permute-done((bf16[136,512]{1,0:T(8,128)(2,1)S(1)}, bf16[136,512]{1,0:T(8,128)(2,1)S(1)}, u32[]{:S(2)}, u32[]{:S(2)}) %collective-permute-start) | collective-permute-done | bytes 139296 | tf_op jit(solution)/shard_map/ppermute | solution.py:501
  12.2 1.9 %collective-permute-start.1 = (bf16[128,512]{1,0:T(8,128)(2,1)}, bf16[128,512]{1,0:T(8,128)(2,1)S(1)}, u32[]{:S(2)}, u32[]{:S(2)}) collective-permute-start(bf16[128,512]{1,0:T(8,128)(2,1)} %bitcast.9), channel_id=1, source_target_pairs={{0,8},{4,12},{8,0},{12,4},{1,9},{5,13},{9,1},{13,5},{2,10},{6,14},... | collective-permute-start | bytes 393224 | tf_op jit(solution)/shard_map/ppermute | solution.py:501
  14.1 3.0 %collective-permute-start.3 = (bf16[136,512]{1,0:T(8,128)(2,1)S(1)}, bf16[136,512]{1,0:T(8,128)(2,1)S(1)}, u32[]{:S(2)}, u32[]{:S(2)}) collective-permute-start(bf16[136,512]{1,0:T(8,128)(2,1)S(1)} %collective-permute-done.2.chunk.far_states), channel_id=1, source_target_pairs={{0,4},{4,0},{8,12},{12,8},{1,5},{5,1},{9,13},{13,9},{2,6},{6,2},{1... | collective-permute-start | bytes 417800 | tf_op jit(solution)/shard_map/ppermute | solution.py:501
  17.1 0.8 %shard_map.145 = (bf16[32,512]{1,0:T(8,128)(2,1)S(1)}, bf16[16,512]{1,0:T(8,128)(2,1)S(1)}, bf16[512,128]{1,0:T(8,128)(2,1)S(1)}) custom-call(f32[8,128]{1,0:T(8,128)S(1)} %pad_add_fusion.scalars), custom_call_target="tpu_custom_call" | custom-call | flops 10000000000 | tf_op jit(solution)/shard_map/pallas_call | solution.py:486
  19.1 1.1 %collective-permute-done.1.far = bf16[128,512]{1,0:T(8,128)(2,1)S(1)} collective-permute-done((bf16[128,512]{1,0:T(8,128)(2,1)}, bf16[128,512]{1,0:T(8,128)(2,1)S(1)}, u32[]{:S(2)}, u32[]{:S(2)}) %collective-permute-start.1) | collective-permute-done | bytes 131104 | tf_op jit(solution)/shard_map/ppermute | solution.py:501
  20.2 1.6 %collective-permute-start.5 = (bf16[128,512]{1,0:T(8,128)(2,1)S(1)}, bf16[128,512]{1,0:T(8,128)(2,1)S(1)}, u32[]{:S(2)}, u32[]{:S(2)}) collective-permute-start(bf16[128,512]{1,0:T(8,128)(2,1)S(1)} %collective-permute-done.1.far), channel_id=1, source_target_pairs={{0,4},{4,0},{8,12},{12,8},{1,5},{5,1},{9,13},{13,9},{2,6},{6,2},{1... | collective-permute-start | bytes 393224 | tf_op jit(solution)/shard_map/ppermute | solution.py:501
  21.7 4.0 %shard_map.149 = (bf16[512,512]{1,0:T(8,128)(2,1)S(1)}, bf16[512,768]{1,0:T(8,128)(2,1)S(1)}, bf16[2,1024,512]{2,1,0:T(8,128)(2,1)S(1)}, bf16[512,256]{1,0:T(8,128)(2,1)S(1)}, bf16[256,512]{1,0:T(8,128)(2,1)S(1)}) custom-call(s32[2]{0:T(128)S(1)} %pad_add_fusion.1.place, f32[8,128]{1,0:T(8,128)S(1)} %pad_add_fusion.scalars, ...), custom_call_target="tpu_custom_call" | custom-call | flops 5000000000 | tf_op jit(solution)/shard_map/pallas_call | solution.py:486
  25.7 0.9 %shard_map.150 = (bf16[512,512]{1,0:T(8,128)(2,1)S(1)}, bf16[512,256]{1,0:T(8,128)(2,1)S(1)}) custom-call(s32[2]{0:T(128)S(1)} %pad_add_fusion.1.place, bf16[128,512]{1,0:T(8,128)(2,1)S(1)} %bitcast.10, bf16[128,512]{1,0:T(8,128)(2,1)S(1)} %collective-permute-done.4.near, bf16[128,512]{1,0:T(8,128)(2,1)S(1)} %collective-permute-done.1.far, ...), custom_call_target="tpu_custom_call" | custom-call | tf_op jit(solution)/shard_map/pallas_call | solution.py:486
  26.6 2.4 %shard_map.151 = (bf16[128,384]{1,0:T(8,128)(2,1)S(1)}, f32[256,384]{1,0:T(8,128)S(1)}, bf16[256,384]{1,0:T(8,128)(2,1)S(1)}) custom-call(s32[2]{0:T(128)S(1)} %pad_add_fusion.1.place, bf16[512,512]{1,0:T(8,128)(2,1)S(1)} %get-tuple-element.72.normed_t, bf16[512,768]{1,0:T(8,128)(2,1)S(1)} %get-tuple-element.73.projected, ...), custom_call_target="tpu_custom_call" | custom-call | tf_op jit(solution)/shard_map/pallas_call | solution.py:486
  29.1 0.8 %shard_map.152 = (f32[128,512]{1,0:T(8,128)S(1)}, bf16[128,512]{1,0:T(8,128)(2,1)S(1)}) custom-call(s32[2]{0:T(128)S(1)} %pad_add_fusion.1.place, bf16[512,512]{1,0:T(8,128)(2,1)S(1)} %get-tuple-element.81.gathered, bf16[256,512]{1,0:T(8,128)(2,1)S(1)} %get-tuple-element.82.mixed_t), custom_call_target="tpu_custom_call" | custom-call | tf_op jit(solution)/shard_map/pallas_call | solution.py:486
  30.8 1.5 %collective-permute-start.8 = (bf16[256,384]{1,0:T(8,128)(2,1)S(1)}, bf16[256,384]{1,0:T(8,128)(2,1)S(1)}, u32[]{:S(2)}, u32[]{:S(2)}) collective-permute-start(bf16[256,384]{1,0:T(8,128)(2,1)S(1)} %add_convert_fusion.3), channel_id=1, source_target_pairs={{0,2},{1,3},{2,0},{3,1},{4,6},{5,7},{6,4},{7,5},{8,10},{9,11},{10,... | collective-permute-start | bytes 589832 | tf_op jit(solution)/shard_map/ppermute | solution.py:501
  32.3 2.4 %shard_map.153 = (bf16[128,384]{1,0:T(8,128)(2,1)S(1)}, f32[256,384]{1,0:T(8,128)S(1)}, bf16[256,384]{1,0:T(8,128)(2,1)S(1)}) custom-call(s32[2]{0:T(128)S(1)} %pad_add_fusion.1.place, bf16[512,512]{1,0:T(8,128)(2,1)S(1)} %get-tuple-element.72.normed_t, bf16[512,768]{1,0:T(8,128)(2,1)S(1)} %get-tuple-element.73.projected, ...), custom_call_target="tpu_custom_call" | custom-call | tf_op jit(solution)/shard_map/pallas_call | solution.py:486
  35.5 0.7 %collective-permute-done.7 = bf16[256,384]{1,0:T(8,128)(2,1)S(1)} collective-permute-done((bf16[256,384]{1,0:T(8,128)(2,1)S(1)}, bf16[256,384]{1,0:T(8,128)(2,1)S(1)}, u32[]{:S(2)}, u32[]{:S(2)}) %collective-permute-start.7) | collective-permute-done | bytes 196640 | tf_op jit(solution)/shard_map/ppermute | solution.py:501
  36.3 0.8 %collective-permute-start.11 = (bf16[256,384]{1,0:T(8,128)(2,1)S(1)}, bf16[256,384]{1,0:T(8,128)(2,1)S(1)}, u32[]{:S(2)}, u32[]{:S(2)}) collective-permute-start(bf16[256,384]{1,0:T(8,128)(2,1)S(1)} %add_convert_fusion.2), channel_id=1, source_target_pairs={{0,2},{1,3},{2,0},{3,1},{4,6},{5,7},{6,4},{7,5},{8,10},{9,11},{10,... | collective-permute-start | bytes 589832 | tf_op jit(solution)/shard_map/ppermute | solution.py:501
  37.1 1.7 %shard_map.154 = (bf16[128,512]{1,0:T(8,128)(2,1)}, bf16[128,512]{1,0:T(8,128)(2,1)}) custom-call(s32[2]{0:T(128)S(1)} %pad_add_fusion.1.place, bf16[136,512]{1,0:T(8,128)(2,1)S(1)} %fusion.1.chunk.own_states.own, bf16[128,512]{1,0:T(8,128)(2,1)S(1)} %bitcast.11, bf16[512,256]{1,0:T(8,128)(2,1)S(1)} %get-tuple-element.71.mixed, ...), custom_call_target="tpu_custom_call" | custom-call | tf_op jit(solution)/shard_map/pallas_call | solution.py:486
  39.0 6.1 %collective-permute-done.11 = bf16[256,384]{1,0:T(8,128)(2,1)S(1)} collective-permute-done((bf16[256,384]{1,0:T(8,128)(2,1)S(1)}, bf16[256,384]{1,0:T(8,128)(2,1)S(1)}, u32[]{:S(2)}, u32[]{:S(2)}) %collective-permute-start.11) | collective-permute-done | bytes 196640 | tf_op jit(solution)/shard_map/ppermute | solution.py:501
  45.8 1.0 %collective-permute-done.12.refs_3_ = bf16[128,512]{1,0:T(8,128)(2,1)S(1)} collective-permute-done((bf16[128,512]{1,0:T(8,128)(2,1)S(1)}, bf16[128,512]{1,0:T(8,128)(2,1)S(1)}, u32[]{:S(2)}, u32[]{:S(2)}) %collective-permute-start.12) | collective-permute-done | bytes 131104 | tf_op jit(solution)/shard_map/ppermute | solution.py:501
  46.8 1.9 %shard_map.155 = (f32[512,256]{1,0:T(8,128)}, f32[512,256]{1,0:T(8,128)}, f32[512,256]{1,0:T(8,128)}, f32[256,512]{1,0:T(8,128)}) custom-call(s32[2]{0:T(128)S(1)} %pad_add_fusion.1.place, bf16[128,512]{1,0:T(8,128)(2,1)S(1)} %add_convert_fusion.4.refs_0_, bf16[256,384]{1,0:T(8,128)(2,1)S(1)} %add_convert_fusion.1.refs_1_, ...), custom_call_target="tpu_custom_call" | custom-call | tf_op jit(solution)/shard_map/pallas_call | solution.py:486
  (41 shorter events, 4.1 us)
Async XLA Ops:
  2.4 9.9 %collective-permute-start = (bf16[136,512]{1,0:T(8,128)(2,1)S(1)}, bf16[136,512]{1,0:T(8,128)(2,1)S(1)}, u32[]{:S(2)}, u32[]{:S(2)}) collective-permute-start(bf16[136,512]{1,0:T(8,128)(2,1)S(1)} %fusion.1.chunk.own_states.own), channel_id=1, source_target_pairs={{0,4},{4,0},{8,12},{12,8},{1,5},{5,1},{9,13},{13,9},{2,6},{6,2},{1... | collective-permute-start | bytes 417800 | tf_op jit(solution)/shard_map/ppermute | solution.py:501
  5.5 8.7 %collective-permute-start.2 = (bf16[136,512]{1,0:T(8,128)(2,1)S(1)}, bf16[136,512]{1,0:T(8,128)(2,1)S(1)}, u32[]{:S(2)}, u32[]{:S(2)}) collective-permute-start(bf16[136,512]{1,0:T(8,128)(2,1)S(1)} %fusion.1.chunk.own_states.own), channel_id=1, source_target_pairs={{0,8},{4,12},{8,0},{12,4},{1,9},{5,13},{9,1},{13,5},{2,10},{6,14},... | collective-permute-start | bytes 417800 | tf_op jit(solution)/shard_map/ppermute | solution.py:501
  8.1 17.7 %collective-permute-start.4 = (bf16[128,512]{1,0:T(8,128)(2,1)}, bf16[128,512]{1,0:T(8,128)(2,1)S(1)}, u32[]{:S(2)}, u32[]{:S(2)}) collective-permute-start(bf16[128,512]{1,0:T(8,128)(2,1)} %bitcast.8), channel_id=1, source_target_pairs={{0,4},{4,0},{8,12},{12,8},{1,5},{5,1},{9,13},{13,9},{2,6},{6,2},{1... | collective-permute-start | bytes 393224 | tf_op jit(solution)/shard_map/ppermute | solution.py:501
  9.9 8.1 %copy-start = (bf16[512,256]{1,0:T(8,128)(2,1)S(1)}, bf16[512,256]{1,0:T(8,128)(2,1)}, u32[]{:S(2)}) copy-start(bf16[512,256]{1,0:T(8,128)(2,1)} %query_w.4) | copy-start | bytes 786436
  9.9 8.1 %copy-start.1 = (bf16[512,256]{1,0:T(8,128)(2,1)S(1)}, bf16[512,256]{1,0:T(8,128)(2,1)}, u32[]{:S(2)}) copy-start(bf16[512,256]{1,0:T(8,128)(2,1)} %key_w.4) | copy-start | bytes 786436
  9.9 8.1 %copy-start.2 = (bf16[512,256]{1,0:T(8,128)(2,1)S(1)}, bf16[512,256]{1,0:T(8,128)(2,1)}, u32[]{:S(2)}) copy-start(bf16[512,256]{1,0:T(8,128)(2,1)} %value_w.4) | copy-start | bytes 786436
  12.2 7.9 %collective-permute-start.1 = (bf16[128,512]{1,0:T(8,128)(2,1)}, bf16[128,512]{1,0:T(8,128)(2,1)S(1)}, u32[]{:S(2)}, u32[]{:S(2)}) collective-permute-start(bf16[128,512]{1,0:T(8,128)(2,1)} %bitcast.9), channel_id=1, source_target_pairs={{0,8},{4,12},{8,0},{12,4},{1,9},{5,13},{9,1},{13,5},{2,10},{6,14},... | collective-permute-start | bytes 393224 | tf_op jit(solution)/shard_map/ppermute | solution.py:501
  14.1 7.6 %collective-permute-start.3 = (bf16[136,512]{1,0:T(8,128)(2,1)S(1)}, bf16[136,512]{1,0:T(8,128)(2,1)S(1)}, u32[]{:S(2)}, u32[]{:S(2)}) collective-permute-start(bf16[136,512]{1,0:T(8,128)(2,1)S(1)} %collective-permute-done.2.chunk.far_states), channel_id=1, source_target_pairs={{0,4},{4,0},{8,12},{12,8},{1,5},{5,1},{9,13},{13,9},{2,6},{6,2},{1... | collective-permute-start | bytes 417800 | tf_op jit(solution)/shard_map/ppermute | solution.py:501
  20.2 5.6 %collective-permute-start.5 = (bf16[128,512]{1,0:T(8,128)(2,1)S(1)}, bf16[128,512]{1,0:T(8,128)(2,1)S(1)}, u32[]{:S(2)}, u32[]{:S(2)}) collective-permute-start(bf16[128,512]{1,0:T(8,128)(2,1)S(1)} %collective-permute-done.1.far), channel_id=1, source_target_pairs={{0,4},{4,0},{8,12},{12,8},{1,5},{5,1},{9,13},{13,9},{2,6},{6,2},{1... | collective-permute-start | bytes 393224 | tf_op jit(solution)/shard_map/ppermute | solution.py:501
  21.7 4.0 %copy-start.3 = (bf16[256,512]{1,0:T(8,128)(2,1)S(1)}, bf16[256,512]{1,0:T(8,128)(2,1)}, u32[]{:S(2)}) copy-start(bf16[256,512]{1,0:T(8,128)(2,1)} %out_w.3) | copy-start | bytes 786436
  21.7 4.0 %copy-start.4 = (bf16[1,128,512]{2,1,0:T(8,128)(2,1)S(1)}, bf16[1,128,512]{2,1,0:T(8,128)(2,1)}, u32[]{:S(2)}) copy-start(bf16[1,128,512]{2,1,0:T(8,128)(2,1)} %param.11) | copy-start | bytes 393220
  29.0 1.5 %collective-permute-start.6 = (bf16[256,384]{1,0:T(8,128)(2,1)S(1)}, bf16[256,384]{1,0:T(8,128)(2,1)S(1)}, u32[]{:S(2)}, u32[]{:S(2)}) collective-permute-start(bf16[256,384]{1,0:T(8,128)(2,1)S(1)} %get-tuple-element.79), channel_id=1, source_target_pairs={{0,1},{1,0},{2,3},{3,2},{4,5},{5,4},{6,7},{7,6},{8,9},{9,8},{10,11... | collective-permute-start | bytes 589832 | tf_op jit(solution)/shard_map/ppermute | solution.py:501
  30.6 4.3 %collective-permute-start.9 = (bf16[128,512]{1,0:T(8,128)(2,1)S(1)}, bf16[128,512]{1,0:T(8,128)(2,1)S(1)}, u32[]{:S(2)}, u32[]{:S(2)}) collective-permute-start(bf16[128,512]{1,0:T(8,128)(2,1)S(1)} %get-tuple-element.93), channel_id=1, source_target_pairs={{0,1},{1,0},{2,3},{3,2},{4,5},{5,4},{6,7},{7,6},{8,9},{9,8},{10,11... | collective-permute-start | bytes 393224 | tf_op jit(solution)/shard_map/ppermute | solution.py:501
  30.8 8.0 %collective-permute-start.8 = (bf16[256,384]{1,0:T(8,128)(2,1)S(1)}, bf16[256,384]{1,0:T(8,128)(2,1)S(1)}, u32[]{:S(2)}, u32[]{:S(2)}) collective-permute-start(bf16[256,384]{1,0:T(8,128)(2,1)S(1)} %add_convert_fusion.3), channel_id=1, source_target_pairs={{0,2},{1,3},{2,0},{3,1},{4,6},{5,7},{6,4},{7,5},{8,10},{9,11},{10,... | collective-permute-start | bytes 589832 | tf_op jit(solution)/shard_map/ppermute | solution.py:501
  34.7 1.5 %collective-permute-start.7 = (bf16[256,384]{1,0:T(8,128)(2,1)S(1)}, bf16[256,384]{1,0:T(8,128)(2,1)S(1)}, u32[]{:S(2)}, u32[]{:S(2)}) collective-permute-start(bf16[256,384]{1,0:T(8,128)(2,1)S(1)} %get-tuple-element.87), channel_id=1, source_target_pairs={{0,1},{1,0},{2,3},{3,2},{4,5},{5,4},{6,7},{7,6},{8,9},{9,8},{10,11... | collective-permute-start | bytes 589832 | tf_op jit(solution)/shard_map/ppermute | solution.py:501
  34.9 10.3 %collective-permute-start.10 = (bf16[128,512]{1,0:T(8,128)(2,1)S(1)}, bf16[128,512]{1,0:T(8,128)(2,1)S(1)}, u32[]{:S(2)}, u32[]{:S(2)}) collective-permute-start(bf16[128,512]{1,0:T(8,128)(2,1)S(1)} %add_convert_fusion.5), channel_id=1, source_target_pairs={{0,2},{1,3},{2,0},{3,1},{4,6},{5,7},{6,4},{7,5},{8,10},{9,11},{10,... | collective-permute-start | bytes 393224 | tf_op jit(solution)/shard_map/ppermute | solution.py:501
  36.3 8.7 %collective-permute-start.11 = (bf16[256,384]{1,0:T(8,128)(2,1)S(1)}, bf16[256,384]{1,0:T(8,128)(2,1)S(1)}, u32[]{:S(2)}, u32[]{:S(2)}) collective-permute-start(bf16[256,384]{1,0:T(8,128)(2,1)S(1)} %add_convert_fusion.2), channel_id=1, source_target_pairs={{0,2},{1,3},{2,0},{3,1},{4,6},{5,7},{6,4},{7,5},{8,10},{9,11},{10,... | collective-permute-start | bytes 589832 | tf_op jit(solution)/shard_map/ppermute | solution.py:501
  38.9 7.9 %collective-permute-start.13 = (bf16[256,384]{1,0:T(8,128)(2,1)S(1)}, bf16[256,384]{1,0:T(8,128)(2,1)S(1)}, u32[]{:S(2)}, u32[]{:S(2)}) collective-permute-start(bf16[256,384]{1,0:T(8,128)(2,1)S(1)} %add_convert_fusion.1.refs_1_), channel_id=1, source_target_pairs={{0,1},{1,0},{2,3},{3,2},{4,5},{5,4},{6,7},{7,6},{8,9},{9,8},{10,11... | collective-permute-start | bytes 589832 | tf_op jit(solution)/shard_map/ppermute | solution.py:501
  45.1 1.7 %collective-permute-start.14 = (bf16[256,384]{1,0:T(8,128)(2,1)S(1)}, bf16[256,384]{1,0:T(8,128)(2,1)S(1)}, u32[]{:S(2)}, u32[]{:S(2)}) collective-permute-start(bf16[256,384]{1,0:T(8,128)(2,1)S(1)} %add_convert_fusion.refs_2_), channel_id=1, source_target_pairs={{0,1},{1,0},{2,3},{3,2},{4,5},{5,4},{6,7},{7,6},{8,9},{9,8},{10,11... | collective-permute-start | bytes 589832 | tf_op jit(solution)/shard_map/ppermute | solution.py:501
  45.2 1.6 %collective-permute-start.12 = (bf16[128,512]{1,0:T(8,128)(2,1)S(1)}, bf16[128,512]{1,0:T(8,128)(2,1)S(1)}, u32[]{:S(2)}, u32[]{:S(2)}) collective-permute-start(bf16[128,512]{1,0:T(8,128)(2,1)S(1)} %add_convert_fusion.4.refs_0_), channel_id=1, source_target_pairs={{0,1},{1,0},{2,3},{3,2},{4,5},{5,4},{6,7},{7,6},{8,9},{9,8},{10,11... | collective-permute-start | bytes 393224 | tf_op jit(solution)/shard_map/ppermute | solution.py:501

commit v7 on v6

--- a/solution.py
+++ b/solution.py
@@ -393,15 +393,18 @@
     keep[...] = plain_product(left[mine, :], right)
 
 
-def mix_kernel(place, own, near, far, last, out_w, gathered, d_mixed):
+def mix_kernel(place, own, near, far, last, out_w, d_mixed):
+    rows = own.shape[0]
+    for index, chunk in enumerate((own, near, far, last)):
+        at = pl.ds(pl.multiple_of((place[0] ^ index) * rows, rows), rows)
+        d_mixed[at, :] = pair_product(chunk[...], out_w[...]).astype(jnp.bfloat16)
+
+
+def output_kernel(place, own, near, far, last, mixed_t, keep, send, gathered):
     rows = own.shape[0]
     for index, chunk in enumerate((own, near, far, last)):
         at = pl.ds(pl.multiple_of((place[0] ^ index) * rows, rows), rows)
         gathered[at, :] = chunk[...]
-    d_mixed[...] = pair_product(gathered[...], out_w[...]).astype(jnp.bfloat16)
-
-
-def output_kernel(place, gathered, mixed_t, keep, send):
     product_halves(place, mixed_t, gathered[...], keep, send)
 
 
@@ -591,23 +594,24 @@
         ],
         cost=5,
     )
-    gathered, d_mixed = run(
+    d_mixed = run(
         mix_kernel,
-        [((total, model), half), ((total, width), half)],
+        [((total, width), half)],
         [place],
         [grads_in, grads_near, grads_far, grads_last, out_weight],
-    )
+    )[0]
     halves = []
     d_own = []
     for pair in range(HEADS // 2):
         if pair == 1:
             local, across = halves[0]
-            gathered, keep = lax.optimization_barrier((gathered, keep))
+            grads_last, keep = lax.optimization_barrier((grads_last, keep))
             out_keep, out_send = run(
                 output_kernel,
                 [((width // 2, model), wide), ((width // 2, model), half)],
                 [place],
-                [gathered, mixed_t],
+                [grads_in, grads_near, grads_far, grads_last, mixed_t],
+                [pltpu.VMEM((total, model), half)],
             )
             d_mixed, local, out_send = lax.optimization_barrier((d_mixed, local, out_send))
             halves[0] = (local, across)

time: 49 us -> 49.1 us (level)
  no operation moved by 1% of the time
where the time goes in v7:
time: 49.1 us; the launch traced here: 48.9 us
  starting transfers between devices  16.6 us (34%)
  Pallas kernels  16.2 us (33%)
  waiting for transfers between devices  11.8 us (24%)
  other arithmetic  3.41 us (7%)
  between operations  0.86 us (2%)
    ppermute x15, starting transfers between devices, swap(): lax.ppermute(array, axis, [(i, i ^ flip) for i in range(lax.axis_size(axi...  16.6 us
    pallas_call x11, Pallas kernels, run(): pl.pallas_call(kernel, out_shape=out_shape, in_specs=[pl.BlockSpec(memory...  16.2 us
    ppermute x15, waiting for transfers between devices, swap(): lax.ppermute(array, axis, [(i, i ^ flip) for i in range(lax.axis_size(axi...  11.8 us
  transfers between devices with their start and end apart: 15, of which 6 were waited for; matrix products, arithmetic and copies ran while one was open for 3% of the time, Pallas kernels for 22%

profile of v7, /device:TPU:0, one launch (start us, length us, event | category | flops | bytes accessed | tf_op | source)
XLA Modules:
  0.0 48.9 jit_solution(10325498980118690875)
XLA Ops:
  0.7 0.8 %convert_reduce_fusion = f32[2,512]{1,0:T(2,128)S(1)} fusion(s32[2]{0:T(128)} %bitcast.15, s32[512]{0:T(512)S(1)} %and_add_fusion, s32[2,8]{1,0:T(2,128)} %bitcast.14, pred[512]{0:T(512)(128)(4,1)S(1)} %compare_or_fusion), kind=kLoop, calls=%fused_computation.9 | loop fusion | flops 48128 | bytes 6728 | tf_op jit(solution)/shard_map/reduce_max | solution.py:543
  1.5 0.9 %fusion.1.chunk.own_states.own = bf16[136,512]{1,0:T(8,128)(2,1)S(1)} fusion(bf16[2,512]{1,0:T(2,128)(2,1)S(1)} %multiply_convert_fusion, bf16[128,512]{1,0:T(8,128)(2,1)} %bitcast.13), kind=kLoop, calls=%fused_computation.8 | loop fusion | flops 417792 | bytes 272384 | tf_op jit(solution)/shard_map/concatenate | solution.py:544
  2.4 3.1 %collective-permute-start = (bf16[136,512]{1,0:T(8,128)(2,1)S(1)}, bf16[136,512]{1,0:T(8,128)(2,1)S(1)}, u32[]{:S(2)}, u32[]{:S(2)}) collective-permute-start(bf16[136,512]{1,0:T(8,128)(2,1)S(1)} %fusion.1.chunk.own_states.own), channel_id=1, source_target_pairs={{0,4},{4,0},{8,12},{12,8},{1,5},{5,1},{9,13},{13,9},{2,6},{6,2},{1... | collective-permute-start | bytes 417800 | tf_op jit(solution)/shard_map/ppermute | solution.py:504
  5.5 2.6 %collective-permute-start.2 = (bf16[136,512]{1,0:T(8,128)(2,1)S(1)}, bf16[136,512]{1,0:T(8,128)(2,1)S(1)}, u32[]{:S(2)}, u32[]{:S(2)}) collective-permute-start(bf16[136,512]{1,0:T(8,128)(2,1)S(1)} %fusion.1.chunk.own_states.own), channel_id=1, source_target_pairs={{0,8},{4,12},{8,0},{12,4},{1,9},{5,13},{9,1},{13,5},{2,10},{6,14},... | collective-permute-start | bytes 417800 | tf_op jit(solution)/shard_map/ppermute | solution.py:504
  8.5 0.7 %convert_element_type.63 = f32[1,17]{1,0:T(1,128)S(1)} convert(s32[1,17]{1,0:T(1,128)} %param.14) | non-fusion elementwise | flops 17 | bytes 136 | tf_op jit(solution)/shard_map/convert_element_type | solution.py:554
  9.2 0.7 %pad_add_fusion.scalars = f32[8,128]{1,0:T(8,128)S(1)} fusion(f32[1,17]{1,0:T(1,128)S(1)} %convert_element_type.63, f32[4,32]{1,0:T(4,128)} %param.19), kind=kLoop, calls=%fused_computation.13 | loop fusion | flops 1024 | bytes 4676 | tf_op jit(solution)/shard_map/add | solution.py:553
  9.9 2.4 %collective-permute-done.chunk.near_states = bf16[136,512]{1,0:T(8,128)(2,1)S(1)} collective-permute-done((bf16[136,512]{1,0:T(8,128)(2,1)S(1)}, bf16[136,512]{1,0:T(8,128)(2,1)S(1)}, u32[]{:S(2)}, u32[]{:S(2)}) %collective-permute-start) | collective-permute-done | bytes 139296 | tf_op jit(solution)/shard_map/ppermute | solution.py:504
  12.2 1.9 %collective-permute-start.1 = (bf16[128,512]{1,0:T(8,128)(2,1)}, bf16[128,512]{1,0:T(8,128)(2,1)S(1)}, u32[]{:S(2)}, u32[]{:S(2)}) collective-permute-start(bf16[128,512]{1,0:T(8,128)(2,1)} %bitcast.9), channel_id=1, source_target_pairs={{0,8},{4,12},{8,0},{12,4},{1,9},{5,13},{9,1},{13,5},{2,10},{6,14},... | collective-permute-start | bytes 393224 | tf_op jit(solution)/shard_map/ppermute | solution.py:504
  14.1 3.0 %collective-permute-start.3 = (bf16[136,512]{1,0:T(8,128)(2,1)S(1)}, bf16[136,512]{1,0:T(8,128)(2,1)S(1)}, u32[]{:S(2)}, u32[]{:S(2)}) collective-permute-start(bf16[136,512]{1,0:T(8,128)(2,1)S(1)} %collective-permute-done.2.chunk.far_states), channel_id=1, source_target_pairs={{0,4},{4,0},{8,12},{12,8},{1,5},{5,1},{9,13},{13,9},{2,6},{6,2},{1... | collective-permute-start | bytes 417800 | tf_op jit(solution)/shard_map/ppermute | solution.py:504
  17.1 0.8 %shard_map.145 = (bf16[32,512]{1,0:T(8,128)(2,1)S(1)}, bf16[16,512]{1,0:T(8,128)(2,1)S(1)}, bf16[512,128]{1,0:T(8,128)(2,1)S(1)}) custom-call(f32[8,128]{1,0:T(8,128)S(1)} %pad_add_fusion.scalars), custom_call_target="tpu_custom_call" | custom-call | flops 10000000000 | tf_op jit(solution)/shard_map/pallas_call | solution.py:489
  19.1 1.1 %collective-permute-done.1.far = bf16[128,512]{1,0:T(8,128)(2,1)S(1)} collective-permute-done((bf16[128,512]{1,0:T(8,128)(2,1)}, bf16[128,512]{1,0:T(8,128)(2,1)S(1)}, u32[]{:S(2)}, u32[]{:S(2)}) %collective-permute-start.1) | collective-permute-done | bytes 131104 | tf_op jit(solution)/shard_map/ppermute | solution.py:504
  20.2 1.6 %collective-permute-start.5 = (bf16[128,512]{1,0:T(8,128)(2,1)S(1)}, bf16[128,512]{1,0:T(8,128)(2,1)S(1)}, u32[]{:S(2)}, u32[]{:S(2)}) collective-permute-start(bf16[128,512]{1,0:T(8,128)(2,1)S(1)} %collective-permute-done.1.far), channel_id=1, source_target_pairs={{0,4},{4,0},{8,12},{12,8},{1,5},{5,1},{9,13},{13,9},{2,6},{6,2},{1... | collective-permute-start | bytes 393224 | tf_op jit(solution)/shard_map/ppermute | solution.py:504
  21.7 4.0 %shard_map.149 = (bf16[512,512]{1,0:T(8,128)(2,1)S(1)}, bf16[512,768]{1,0:T(8,128)(2,1)S(1)}, bf16[2,1024,512]{2,1,0:T(8,128)(2,1)S(1)}, bf16[512,256]{1,0:T(8,128)(2,1)S(1)}, bf16[256,512]{1,0:T(8,128)(2,1)S(1)}) custom-call(s32[2]{0:T(128)S(1)} %pad_add_fusion.1.place, f32[8,128]{1,0:T(8,128)S(1)} %pad_add_fusion.scalars, ...), custom_call_target="tpu_custom_call" | custom-call | flops 5000000000 | tf_op jit(solution)/shard_map/pallas_call | solution.py:489
  25.7 1.0 %shard_map.150.d_mixed = bf16[512,256]{1,0:T(8,128)(2,1)S(1)} custom-call(s32[2]{0:T(128)S(1)} %pad_add_fusion.1.place, bf16[128,512]{1,0:T(8,128)(2,1)S(1)} %bitcast.10, bf16[128,512]{1,0:T(8,128)(2,1)S(1)} %collective-permute-done.4.near, bf16[128,512]{1,0:T(8,128)(2,1)S(1)} %collective-permute-done.1.far, ...), custom_call_target="tpu_custom_call" | custom-call | tf_op jit(solution)/shard_map/pallas_call | solution.py:489
  26.8 2.4 %shard_map.151 = (bf16[128,384]{1,0:T(8,128)(2,1)S(1)}, f32[256,384]{1,0:T(8,128)S(1)}, bf16[256,384]{1,0:T(8,128)(2,1)S(1)}) custom-call(s32[2]{0:T(128)S(1)} %pad_add_fusion.1.place, bf16[512,512]{1,0:T(8,128)(2,1)S(1)} %get-tuple-element.70.normed_t, bf16[512,768]{1,0:T(8,128)(2,1)S(1)} %get-tuple-element.71.projected, ...), custom_call_target="tpu_custom_call" | custom-call | tf_op jit(solution)/shard_map/pallas_call | solution.py:489
  29.3 0.9 %shard_map.152 = (f32[128,512]{1,0:T(8,128)S(1)}, bf16[128,512]{1,0:T(8,128)(2,1)S(1)}) custom-call(s32[2]{0:T(128)S(1)} %pad_add_fusion.1.place, bf16[128,512]{1,0:T(8,128)(2,1)S(1)} %bitcast.11, bf16[128,512]{1,0:T(8,128)(2,1)S(1)} %collective-permute-done.4.near, bf16[128,512]{1,0:T(8,128)(2,1)S(1)} %collective-permute-done.1.far, ...), custom_call_target="tpu_custom_call" | custom-call | tf_op jit(solution)/shard_map/pallas_call | solution.py:489
  31.0 1.5 %collective-permute-start.8 = (bf16[256,384]{1,0:T(8,128)(2,1)S(1)}, bf16[256,384]{1,0:T(8,128)(2,1)S(1)}, u32[]{:S(2)}, u32[]{:S(2)}) collective-permute-start(bf16[256,384]{1,0:T(8,128)(2,1)S(1)} %add_convert_fusion.3), channel_id=1, source_target_pairs={{0,2},{1,3},{2,0},{3,1},{4,6},{5,7},{6,4},{7,5},{8,10},{9,11},{10,... | collective-permute-start | bytes 589832 | tf_op jit(solution)/shard_map/ppermute | solution.py:504
  32.5 2.4 %shard_map.153 = (bf16[128,384]{1,0:T(8,128)(2,1)S(1)}, f32[256,384]{1,0:T(8,128)S(1)}, bf16[256,384]{1,0:T(8,128)(2,1)S(1)}) custom-call(s32[2]{0:T(128)S(1)} %pad_add_fusion.1.place, bf16[512,512]{1,0:T(8,128)(2,1)S(1)} %get-tuple-element.70.normed_t, bf16[512,768]{1,0:T(8,128)(2,1)S(1)} %get-tuple-element.71.projected, ...), custom_call_target="tpu_custom_call" | custom-call | tf_op jit(solution)/shard_map/pallas_call | solution.py:489
  35.7 0.7 %collective-permute-done.7 = bf16[256,384]{1,0:T(8,128)(2,1)S(1)} collective-permute-done((bf16[256,384]{1,0:T(8,128)(2,1)S(1)}, bf16[256,384]{1,0:T(8,128)(2,1)S(1)}, u32[]{:S(2)}, u32[]{:S(2)}) %collective-permute-start.7) | collective-permute-done | bytes 196640 | tf_op jit(solution)/shard_map/ppermute | solution.py:504
  36.4 0.8 %collective-permute-start.11 = (bf16[256,384]{1,0:T(8,128)(2,1)S(1)}, bf16[256,384]{1,0:T(8,128)(2,1)S(1)}, u32[]{:S(2)}, u32[]{:S(2)}) collective-permute-start(bf16[256,384]{1,0:T(8,128)(2,1)S(1)} %add_convert_fusion.2), channel_id=1, source_target_pairs={{0,2},{1,3},{2,0},{3,1},{4,6},{5,7},{6,4},{7,5},{8,10},{9,11},{10,... | collective-permute-start | bytes 589832 | tf_op jit(solution)/shard_map/ppermute | solution.py:504
  37.3 1.7 %shard_map.154 = (bf16[128,512]{1,0:T(8,128)(2,1)}, bf16[128,512]{1,0:T(8,128)(2,1)}) custom-call(s32[2]{0:T(128)S(1)} %pad_add_fusion.1.place, bf16[136,512]{1,0:T(8,128)(2,1)S(1)} %fusion.1.chunk.own_states.own, bf16[128,512]{1,0:T(8,128)(2,1)S(1)} %bitcast.12, bf16[512,256]{1,0:T(8,128)(2,1)S(1)} %get-tuple-element.69.mixed, ...), custom_call_target="tpu_custom_call" | custom-call | tf_op jit(solution)/shard_map/pallas_call | solution.py:489
  39.1 6.1 %collective-permute-done.11 = bf16[256,384]{1,0:T(8,128)(2,1)S(1)} collective-permute-done((bf16[256,384]{1,0:T(8,128)(2,1)S(1)}, bf16[256,384]{1,0:T(8,128)(2,1)S(1)}, u32[]{:S(2)}, u32[]{:S(2)}) %collective-permute-start.11) | collective-permute-done | bytes 196640 | tf_op jit(solution)/shard_map/ppermute | solution.py:504
  45.9 1.0 %collective-permute-done.12.refs_3_ = bf16[128,512]{1,0:T(8,128)(2,1)S(1)} collective-permute-done((bf16[128,512]{1,0:T(8,128)(2,1)S(1)}, bf16[128,512]{1,0:T(8,128)(2,1)S(1)}, u32[]{:S(2)}, u32[]{:S(2)}) %collective-permute-start.12) | collective-permute-done | bytes 131104 | tf_op jit(solution)/shard_map/ppermute | solution.py:504
  47.0 1.9 %shard_map.155 = (f32[512,256]{1,0:T(8,128)}, f32[512,256]{1,0:T(8,128)}, f32[512,256]{1,0:T(8,128)}, f32[256,512]{1,0:T(8,128)}) custom-call(s32[2]{0:T(128)S(1)} %pad_add_fusion.1.place, bf16[128,512]{1,0:T(8,128)(2,1)S(1)} %add_convert_fusion.4.refs_0_, bf16[256,384]{1,0:T(8,128)(2,1)S(1)} %add_convert_fusion.1.refs_1_, ...), custom_call_target="tpu_custom_call" | custom-call | tf_op jit(solution)/shard_map/pallas_call | solution.py:489
  (41 shorter events, 4.1 us)
Async XLA Ops:
  2.4 9.9 %collective-permute-start = (bf16[136,512]{1,0:T(8,128)(2,1)S(1)}, bf16[136,512]{1,0:T(8,128)(2,1)S(1)}, u32[]{:S(2)}, u32[]{:S(2)}) collective-permute-start(bf16[136,512]{1,0:T(8,128)(2,1)S(1)} %fusion.1.chunk.own_states.own), channel_id=1, source_target_pairs={{0,4},{4,0},{8,12},{12,8},{1,5},{5,1},{9,13},{13,9},{2,6},{6,2},{1... | collective-permute-start | bytes 417800 | tf_op jit(solution)/shard_map/ppermute | solution.py:504
  5.5 8.7 %collective-permute-start.2 = (bf16[136,512]{1,0:T(8,128)(2,1)S(1)}, bf16[136,512]{1,0:T(8,128)(2,1)S(1)}, u32[]{:S(2)}, u32[]{:S(2)}) collective-permute-start(bf16[136,512]{1,0:T(8,128)(2,1)S(1)} %fusion.1.chunk.own_states.own), channel_id=1, source_target_pairs={{0,8},{4,12},{8,0},{12,4},{1,9},{5,13},{9,1},{13,5},{2,10},{6,14},... | collective-permute-start | bytes 417800 | tf_op jit(solution)/shard_map/ppermute | solution.py:504
  8.1 17.7 %collective-permute-start.4 = (bf16[128,512]{1,0:T(8,128)(2,1)}, bf16[128,512]{1,0:T(8,128)(2,1)S(1)}, u32[]{:S(2)}, u32[]{:S(2)}) collective-permute-start(bf16[128,512]{1,0:T(8,128)(2,1)} %bitcast.8), channel_id=1, source_target_pairs={{0,4},{4,0},{8,12},{12,8},{1,5},{5,1},{9,13},{13,9},{2,6},{6,2},{1... | collective-permute-start | bytes 393224 | tf_op jit(solution)/shard_map/ppermute | solution.py:504
  9.9 8.1 %copy-start = (bf16[512,256]{1,0:T(8,128)(2,1)S(1)}, bf16[512,256]{1,0:T(8,128)(2,1)}, u32[]{:S(2)}) copy-start(bf16[512,256]{1,0:T(8,128)(2,1)} %query_w.4) | copy-start | bytes 786436
  9.9 8.1 %copy-start.1 = (bf16[512,256]{1,0:T(8,128)(2,1)S(1)}, bf16[512,256]{1,0:T(8,128)(2,1)}, u32[]{:S(2)}) copy-start(bf16[512,256]{1,0:T(8,128)(2,1)} %key_w.4) | copy-start | bytes 786436
  9.9 8.1 %copy-start.2 = (bf16[512,256]{1,0:T(8,128)(2,1)S(1)}, bf16[512,256]{1,0:T(8,128)(2,1)}, u32[]{:S(2)}) copy-start(bf16[512,256]{1,0:T(8,128)(2,1)} %value_w.4) | copy-start | bytes 786436
  12.2 7.9 %collective-permute-start.1 = (bf16[128,512]{1,0:T(8,128)(2,1)}, bf16[128,512]{1,0:T(8,128)(2,1)S(1)}, u32[]{:S(2)}, u32[]{:S(2)}) collective-permute-start(bf16[128,512]{1,0:T(8,128)(2,1)} %bitcast.9), channel_id=1, source_target_pairs={{0,8},{4,12},{8,0},{12,4},{1,9},{5,13},{9,1},{13,5},{2,10},{6,14},... | collective-permute-start | bytes 393224 | tf_op jit(solution)/shard_map/ppermute | solution.py:504
  14.1 7.6 %collective-permute-start.3 = (bf16[136,512]{1,0:T(8,128)(2,1)S(1)}, bf16[136,512]{1,0:T(8,128)(2,1)S(1)}, u32[]{:S(2)}, u32[]{:S(2)}) collective-permute-start(bf16[136,512]{1,0:T(8,128)(2,1)S(1)} %collective-permute-done.2.chunk.far_states), channel_id=1, source_target_pairs={{0,4},{4,0},{8,12},{12,8},{1,5},{5,1},{9,13},{13,9},{2,6},{6,2},{1... | collective-permute-start | bytes 417800 | tf_op jit(solution)/shard_map/ppermute | solution.py:504
  20.2 5.6 %collective-permute-start.5 = (bf16[128,512]{1,0:T(8,128)(2,1)S(1)}, bf16[128,512]{1,0:T(8,128)(2,1)S(1)}, u32[]{:S(2)}, u32[]{:S(2)}) collective-permute-start(bf16[128,512]{1,0:T(8,128)(2,1)S(1)} %collective-permute-done.1.far), channel_id=1, source_target_pairs={{0,4},{4,0},{8,12},{12,8},{1,5},{5,1},{9,13},{13,9},{2,6},{6,2},{1... | collective-permute-start | bytes 393224 | tf_op jit(solution)/shard_map/ppermute | solution.py:504
  21.7 4.0 %copy-start.3 = (bf16[1,128,512]{2,1,0:T(8,128)(2,1)S(1)}, bf16[1,128,512]{2,1,0:T(8,128)(2,1)}, u32[]{:S(2)}) copy-start(bf16[1,128,512]{2,1,0:T(8,128)(2,1)} %param.11) | copy-start | bytes 393220
  21.7 4.0 %copy-start.4 = (bf16[256,512]{1,0:T(8,128)(2,1)S(1)}, bf16[256,512]{1,0:T(8,128)(2,1)}, u32[]{:S(2)}) copy-start(bf16[256,512]{1,0:T(8,128)(2,1)} %out_w.3) | copy-start | bytes 786436
  29.2 1.5 %collective-permute-start.6 = (bf16[256,384]{1,0:T(8,128)(2,1)S(1)}, bf16[256,384]{1,0:T(8,128)(2,1)S(1)}, u32[]{:S(2)}, u32[]{:S(2)}) collective-permute-start(bf16[256,384]{1,0:T(8,128)(2,1)S(1)} %get-tuple-element.76), channel_id=1, source_target_pairs={{0,1},{1,0},{2,3},{3,2},{4,5},{5,4},{6,7},{7,6},{8,9},{9,8},{10,11... | collective-permute-start | bytes 589832 | tf_op jit(solution)/shard_map/ppermute | solution.py:504
  30.8 4.3 %collective-permute-start.9 = (bf16[128,512]{1,0:T(8,128)(2,1)S(1)}, bf16[128,512]{1,0:T(8,128)(2,1)S(1)}, u32[]{:S(2)}, u32[]{:S(2)}) collective-permute-start(bf16[128,512]{1,0:T(8,128)(2,1)S(1)} %get-tuple-element.89), channel_id=1, source_target_pairs={{0,1},{1,0},{2,3},{3,2},{4,5},{5,4},{6,7},{7,6},{8,9},{9,8},{10,11... | collective-permute-start | bytes 393224 | tf_op jit(solution)/shard_map/ppermute | solution.py:504
  31.0 8.0 %collective-permute-start.8 = (bf16[256,384]{1,0:T(8,128)(2,1)S(1)}, bf16[256,384]{1,0:T(8,128)(2,1)S(1)}, u32[]{:S(2)}, u32[]{:S(2)}) collective-permute-start(bf16[256,384]{1,0:T(8,128)(2,1)S(1)} %add_convert_fusion.3), channel_id=1, source_target_pairs={{0,2},{1,3},{2,0},{3,1},{4,6},{5,7},{6,4},{7,5},{8,10},{9,11},{10,... | collective-permute-start | bytes 589832 | tf_op jit(solution)/shard_map/ppermute | solution.py:504
  34.9 1.5 %collective-permute-start.7 = (bf16[256,384]{1,0:T(8,128)(2,1)S(1)}, bf16[256,384]{1,0:T(8,128)(2,1)S(1)}, u32[]{:S(2)}, u32[]{:S(2)}) collective-permute-start(bf16[256,384]{1,0:T(8,128)(2,1)S(1)} %get-tuple-element.83), channel_id=1, source_target_pairs={{0,1},{1,0},{2,3},{3,2},{4,5},{5,4},{6,7},{7,6},{8,9},{9,8},{10,11... | collective-permute-start | bytes 589832 | tf_op jit(solution)/shard_map/ppermute | solution.py:504
  35.1 10.3 %collective-permute-start.10 = (bf16[128,512]{1,0:T(8,128)(2,1)S(1)}, bf16[128,512]{1,0:T(8,128)(2,1)S(1)}, u32[]{:S(2)}, u32[]{:S(2)}) collective-permute-start(bf16[128,512]{1,0:T(8,128)(2,1)S(1)} %add_convert_fusion.5), channel_id=1, source_target_pairs={{0,2},{1,3},{2,0},{3,1},{4,6},{5,7},{6,4},{7,5},{8,10},{9,11},{10,... | collective-permute-start | bytes 393224 | tf_op jit(solution)/shard_map/ppermute | solution.py:504
  36.4 8.8 %collective-permute-start.11 = (bf16[256,384]{1,0:T(8,128)(2,1)S(1)}, bf16[256,384]{1,0:T(8,128)(2,1)S(1)}, u32[]{:S(2)}, u32[]{:S(2)}) collective-permute-start(bf16[256,384]{1,0:T(8,128)(2,1)S(1)} %add_convert_fusion.2), channel_id=1, source_target_pairs={{0,2},{1,3},{2,0},{3,1},{4,6},{5,7},{6,4},{7,5},{8,10},{9,11},{10,... | collective-permute-start | bytes 589832 | tf_op jit(solution)/shard_map/ppermute | solution.py:504
  39.0 7.9 %collective-permute-start.13 = (bf16[256,384]{1,0:T(8,128)(2,1)S(1)}, bf16[256,384]{1,0:T(8,128)(2,1)S(1)}, u32[]{:S(2)}, u32[]{:S(2)}) collective-permute-start(bf16[256,384]{1,0:T(8,128)(2,1)S(1)} %add_convert_fusion.1.refs_1_), channel_id=1, source_target_pairs={{0,1},{1,0},{2,3},{3,2},{4,5},{5,4},{6,7},{7,6},{8,9},{9,8},{10,11... | collective-permute-start | bytes 589832 | tf_op jit(solution)/shard_map/ppermute | solution.py:504
  45.2 1.7 %collective-permute-start.14 = (bf16[256,384]{1,0:T(8,128)(2,1)S(1)}, bf16[256,384]{1,0:T(8,128)(2,1)S(1)}, u32[]{:S(2)}, u32[]{:S(2)}) collective-permute-start(bf16[256,384]{1,0:T(8,128)(2,1)S(1)} %add_convert_fusion.refs_2_), channel_id=1, source_target_pairs={{0,1},{1,0},{2,3},{3,2},{4,5},{5,4},{6,7},{7,6},{8,9},{9,8},{10,11... | collective-permute-start | bytes 589832 | tf_op jit(solution)/shard_map/ppermute | solution.py:504
  45.4 1.6 %collective-permute-start.12 = (bf16[128,512]{1,0:T(8,128)(2,1)S(1)}, bf16[128,512]{1,0:T(8,128)(2,1)S(1)}, u32[]{:S(2)}, u32[]{:S(2)}) collective-permute-start(bf16[128,512]{1,0:T(8,128)(2,1)S(1)} %add_convert_fusion.4.refs_0_), channel_id=1, source_target_pairs={{0,1},{1,0},{2,3},{3,2},{4,5},{5,4},{6,7},{7,6},{8,9},{9,8},{10,11... | collective-permute-start | bytes 393224 | tf_op jit(solution)/shard_map/ppermute | solution.py:504
